TPU v7x, 32 devices: a whole 2x2x4 slice. The times are simulated.
32 devices in a mesh: dp: 16 (over z, y, core), tensor: 2 (over x).
Axes of the slice: x: 2, y: 2, z: 4, core: 2. Of those that a mesh axis runs over, the one named last changes fastest.
Arguments:
- tokens: bfloat16 [4096, 1024], P(('dp', 'tensor')), may hold values from -6 to 6
- out_cotangent: bfloat16 [4096, 1024], P(('dp', 'tensor')), may hold values from -6 to 6
- seq_lengths: int32 [16], P('dp'), may hold values from 1 to 256, 2048 in all
- norm_gain1: float32 [1024], replicated, may hold values from 0.1 to 1.9
- query_weight: bfloat16 [1024, 1024], P('dp', 'tensor'), may hold values from -0.1875 to 0.1875
- key_weight: bfloat16 [1024, 1024], P('dp', 'tensor'), may hold values from -0.1875 to 0.1875
- value_weight: bfloat16 [1024, 2048], P('dp', 'tensor'), may hold values from -0.1875 to 0.1875
- out_gate_weight: bfloat16 [1024, 2048], P('dp', 'tensor'), may hold values from -0.1875 to 0.1875
- beta_weight: bfloat16 [1024, 8], P('dp', 'tensor'), may hold values from -0.1875 to 0.1875
- decay_weight: bfloat16 [1024, 8], P('dp', 'tensor'), may hold values from -0.1875 to 0.1875
- conv_query: float32 [4, 1024], P(None, 'tensor'), may hold values from -3 to 3
- conv_key: float32 [4, 1024], P(None, 'tensor'), may hold values from -3 to 3
- conv_value: float32 [4, 2048], P(None, 'tensor'), may hold values from -3 to 3
- decay_log_rate: float32 [8], P('tensor'), may hold values from -4 to 1
- decay_bias: float32 [8], P('tensor'), may hold values from -4 to 0
- out_gain: float32 [256], replicated, may hold values from 0.1 to 1.9
- out_weight: bfloat16 [1024, 2048], P('dp', 'tensor'), may hold values from -0.25 to 0.25
- norm_gain2: float32 [1024], replicated, may hold values from 0.1 to 1.9
- ffn_gate_weight: bfloat16 [1024, 2816], P('dp', 'tensor'), may hold values from -0.1875 to 0.1875
- ffn_up_weight: bfloat16 [1024, 2816], P('dp', 'tensor'), may hold values from -0.1875 to 0.1875
- ffn_down_weight: bfloat16 [1024, 2816], P('dp', 'tensor'), may hold values from -0.109375 to 0.109375
Outputs:
- output: bfloat16 [4096, 1024], P(('dp', 'tensor'))
- grad_tokens: bfloat16 [4096, 1024], P(('dp', 'tensor'))
- grad_norm_gain1: float32 [1024], replicated
- grad_query_weight: float32 [1024, 1024], P('dp', 'tensor')
- grad_key_weight: float32 [1024, 1024], P('dp', 'tensor')
- grad_value_weight: float32 [1024, 2048], P('dp', 'tensor')
- grad_out_gate_weight: float32 [1024, 2048], P('dp', 'tensor')
- grad_beta_weight: float32 [1024, 8], P('dp', 'tensor')
- grad_decay_weight: float32 [1024, 8], P('dp', 'tensor')
- grad_conv_query: float32 [4, 1024], replicated
- grad_conv_key: float32 [4, 1024], replicated
- grad_conv_value: float32 [4, 2048], replicated
- grad_decay_log_rate: float32 [8], replicated
- grad_decay_bias: float32 [8], replicated
- grad_out_gain: float32 [256], replicated
- grad_out_weight: float32 [1024, 2048], P('dp', 'tensor')
- grad_norm_gain2: float32 [1024], replicated
- grad_ffn_gate_weight: float32 [1024, 2816], P('dp', 'tensor')
- grad_ffn_up_weight: float32 [1024, 2816], P('dp', 'tensor')
- grad_ffn_down_weight: float32 [1024, 2816], P('dp', 'tensor')
Inputs may be any that keep to these rules, and one draw needn't show every extreme that they name: `seq_lengths`: the number of valid tokens of each sequence; the largest is exactly 256.
All inputs are finite; a program needn't handle non-finite values. No bound on the sum of `seq_lengths` on one device may be relied on, other than what follows from the above.
Results may differ from a plain program's by a relative error of at most 0.012.
Values may be sent and summed in bfloat16 or wider, within the bound.
No kernel may reach another device: no remote copies, remote signals or barrier semaphores. Data moves between devices by JAX's collectives and lax.ppermute only.
A program may use at most 192 MiB of HBM per device.

v0:
```python
import jax
import jax.numpy as jnp
from jax import lax
from jax.sharding import PartitionSpec as P

GROUP = 64


highest = lax.Precision.HIGHEST


def plain_dot(left, right):
    return jnp.dot(left, right, preferred_element_type=jnp.float32)


def left_dot(left, right):
    return lax.dot_general(
        left, right, (((0,), (0,)), ((), ())), preferred_element_type=jnp.float32
    )


def right_dot(left, right):
    return lax.dot_general(
        left, right, (((1,), (1,)), ((), ())), preferred_element_type=jnp.float32
    )


def exact_dot(left, right):
    return jnp.dot(left, right, precision=highest)


def rms_rows(inputs, gain):
    wide_rows = inputs.astype(jnp.float32)
    inverse = lax.rsqrt(jnp.mean(wide_rows * wide_rows, -1, keepdims=True) + 1e-05)
    normed = wide_rows * inverse
    return (normed, inverse, (normed * gain).astype(jnp.bfloat16))


def rms_back(grad_rows, normed, inverse, gain):
    scaled = grad_rows * gain
    grad_in = inverse * (scaled - normed * jnp.mean(scaled * normed, -1, keepdims=True))
    return (grad_in, jnp.sum(grad_rows * normed, 0))


def causal_conv(projected, kernel):
    kernel_len = kernel.shape[0]
    summed = kernel[kernel_len - 1] * projected
    for offset in range(1, kernel_len):
        shifted = jnp.pad(projected[:-offset], ((offset, 0), (0, 0)))
        summed = summed + kernel[kernel_len - 1 - offset] * shifted
    return summed


def delta_block(state, element):
    block_query, block_key, block_value, block_beta, block_gate = element
    block_len = block_key.shape[0]
    value_dim = block_value.shape[1]
    lower_all = jnp.tril(jnp.ones((block_len, block_len), dtype=bool))
    strict_lower = jnp.tril(jnp.ones((block_len, block_len), dtype=bool), -1)
    cumulative = jnp.cumsum(block_gate)
    spread = cumulative[:, None] - cumulative[None, :]
    decays = jnp.where(lower_all, jnp.exp(jnp.where(lower_all, spread, 0.0)), 0.0)
    key_key = exact_dot(block_key, block_key.T)
    coupling = jnp.where(strict_lower, block_beta[:, None] * key_key * decays, 0.0)
    stacked = jnp.concatenate(
        [
            block_beta[:, None] * block_value,
            (block_beta * jnp.exp(cumulative))[:, None] * block_key,
        ],
        axis=1,
    )
    solved = lax.linalg.triangular_solve(
        coupling + jnp.eye(block_len, dtype=jnp.float32),
        stacked,
        left_side=True,
        lower=True,
        unit_diagonal=True,
    )
    updates = solved[:, :value_dim] - exact_dot(solved[:, value_dim:], state.T)
    query_key = jnp.where(lower_all, exact_dot(block_query, block_key.T) * decays, 0.0)
    outputs = jnp.exp(cumulative)[:, None] * exact_dot(block_query, state.T) + exact_dot(
        query_key, updates
    )
    final_log = cumulative[-1]
    new_state = jnp.exp(final_log) * state + exact_dot(
        updates.T, block_key * jnp.exp(final_log - cumulative)[:, None]
    )
    return (new_state, outputs)


def delta_rule(query_rows, key_rows, value_rows, beta_rows, log_gates, block_len):
    length, head_count, key_dim = key_rows.shape
    value_dim = value_rows.shape[2]
    blocks = length // block_len

    def split_heads(array):
        shaped = array.reshape((blocks, block_len) + array.shape[1:])
        return jnp.moveaxis(shaped, 2, 0)

    def one_head(head_query, head_key, head_value, head_beta, head_gate):
        start_state = jnp.zeros((value_dim, key_dim), jnp.float32)
        unused, outputs = lax.scan(
            delta_block, start_state, (head_query, head_key, head_value, head_beta, head_gate)
        )
        return outputs

    per_head = jax.vmap(one_head)(
        split_heads(query_rows),
        split_heads(key_rows),
        split_heads(value_rows),
        split_heads(beta_rows),
        split_heads(log_gates),
    )
    return jnp.transpose(per_head, (1, 2, 0, 3)).reshape(length, head_count, value_dim)


def mixer(
    proj_query,
    proj_key,
    proj_value,
    proj_gate,
    proj_beta,
    proj_decay,
    conv_query,
    conv_key,
    conv_value,
    decay_log_rate,
    decay_bias,
    out_gain,
):
    length = proj_query.shape[0]
    head_count = proj_beta.shape[1]
    query_rows = jax.nn.silu(causal_conv(proj_query, conv_query)).reshape(length, head_count, -1)
    key_rows = jax.nn.silu(causal_conv(proj_key, conv_key)).reshape(length, head_count, -1)
    value_rows = jax.nn.silu(causal_conv(proj_value, conv_value)).reshape(length, head_count, -1)
    key_dim = query_rows.shape[2]
    query_rows = (
        query_rows
        * lax.rsqrt(jnp.sum(query_rows * query_rows, -1, keepdims=True) + 1e-06)
        * key_dim ** (-0.5)
    )
    key_rows = key_rows * lax.rsqrt(jnp.sum(key_rows * key_rows, -1, keepdims=True) + 1e-06)
    beta_rows = jax.nn.sigmoid(proj_beta)
    log_gates = -jnp.exp(decay_log_rate) * jax.nn.softplus(proj_decay + decay_bias)
    mixed = delta_rule(query_rows, key_rows, value_rows, beta_rows, log_gates, GROUP)
    inverse = lax.rsqrt(jnp.mean(mixed * mixed, -1, keepdims=True) + 1e-05)
    gated = mixed * inverse * out_gain * jax.nn.silu(proj_gate.reshape(length, head_count, -1))
    return gated.reshape(length, -1)


def split_columns(array, widths):
    pieces = []
    offset = 0
    for width in widths:
        pieces.append(array[:, offset : offset + width])
        offset = offset + width
    return pieces


def on_device(
    tokens,
    out_cotangent,
    seq_lengths,
    norm_gain1,
    query_weight,
    key_weight,
    value_weight,
    out_gate_weight,
    beta_weight,
    decay_weight,
    conv_query,
    conv_key,
    conv_value,
    decay_log_rate,
    decay_bias,
    out_gain,
    out_weight,
    norm_gain2,
    ffn_gate_weight,
    ffn_up_weight,
    ffn_down_weight,
):
    local_rows = tokens.shape[0]
    tensor_index = lax.axis_index("tensor")
    tensor_count = lax.axis_size("tensor")
    seq_length = seq_lengths[0]
    local_pos = tensor_index * local_rows + jnp.arange(local_rows, dtype=jnp.int32)
    local_mask = (local_pos < seq_length).astype(jnp.float32)[:, None]
    whole_mask = (jnp.arange(local_rows * tensor_count, dtype=jnp.int32) < seq_length).astype(
        jnp.bfloat16
    )[:, None]
    key_cols = query_weight.shape[1]
    value_cols = value_weight.shape[1]
    head_cols = beta_weight.shape[1]
    hidden_cols = ffn_gate_weight.shape[1]
    mixer_widths = [key_cols, key_cols, value_cols, value_cols, head_cols, head_cols]
    mixer_joined = jnp.concatenate(
        [query_weight, key_weight, value_weight, out_gate_weight, beta_weight, decay_weight], axis=1
    )
    ffn_joined = jnp.concatenate([ffn_gate_weight, ffn_up_weight], axis=1)
    normed1, inverse1, hidden1 = rms_rows(tokens, norm_gain1)
    whole1 = lax.all_gather(hidden1, "tensor", axis=0, tiled=True)
    mixer_full = (
        lax.all_gather(mixer_joined, "dp", axis=0, tiled=True),
        lax.all_gather(out_weight, "dp", axis=0, tiled=True),
    )
    projections = split_columns(plain_dot(whole1, mixer_full[0]), mixer_widths)
    mixed_out, pullback = jax.vjp(
        mixer,
        projections[0],
        projections[1],
        projections[2],
        projections[3],
        projections[4],
        projections[5],
        conv_query,
        conv_key,
        conv_value,
        decay_log_rate,
        decay_bias,
        out_gain,
    )
    mixed_half = mixed_out.astype(jnp.bfloat16)
    out_full = mixer_full[1]
    branch = lax.psum_scatter(
        right_dot(mixed_half, out_full), "tensor", scatter_dimension=0, tiled=True
    )
    residual = tokens.astype(jnp.float32) + branch
    normed2, inverse2, hidden2 = rms_rows(residual, norm_gain2)
    whole2 = lax.all_gather(hidden2, "tensor", axis=0, tiled=True)
    ffn_full = (
        lax.all_gather(ffn_joined, "dp", axis=0, tiled=True),
        lax.all_gather(ffn_down_weight, "dp", axis=0, tiled=True),
    )
    pre_both = plain_dot(whole2, ffn_full[0])
    gate_pre = pre_both[:, :hidden_cols]
    up_pre = pre_both[:, hidden_cols:]
    gate_act = jax.nn.silu(gate_pre)
    inner_act = (gate_act * up_pre).astype(jnp.bfloat16)
    down_full = ffn_full[1]
    ffn_branch = lax.psum_scatter(
        right_dot(inner_act, down_full).astype(jnp.bfloat16),
        "tensor",
        scatter_dimension=0,
        tiled=True,
    ).astype(jnp.float32)
    output = (local_mask * (residual + ffn_branch)).astype(jnp.bfloat16)
    grad_whole = lax.all_gather(out_cotangent, "tensor", axis=0, tiled=True) * whole_mask
    grad_inner = plain_dot(grad_whole, ffn_full[1])
    sigma_gate = jax.nn.sigmoid(gate_pre)
    grad_gate_pre = (
        grad_inner * up_pre * sigma_gate * (1.0 + gate_pre * (1.0 - sigma_gate))
    ).astype(jnp.bfloat16)
    grad_up_pre = (grad_inner * gate_act).astype(jnp.bfloat16)
    grad_pre_both = jnp.concatenate([grad_gate_pre, grad_up_pre], axis=1)
    grad_hidden2 = lax.psum_scatter(
        right_dot(grad_pre_both, ffn_full[0]), "tensor", scatter_dimension=0, tiled=True
    )
    grad_normed2, second_gain_gradient = rms_back(grad_hidden2, normed2, inverse2, norm_gain2)
    grad_residual = local_mask * out_cotangent.astype(jnp.float32) + grad_normed2
    gate_up_part = left_dot(whole2, grad_pre_both)
    down_part = left_dot(grad_whole, inner_act)
    ffn_shard = lax.psum_scatter(
        jnp.concatenate([gate_up_part, down_part], axis=1), "dp", scatter_dimension=0, tiled=True
    )
    grad_whole1 = lax.all_gather(grad_residual.astype(jnp.bfloat16), "tensor", axis=0, tiled=True)
    grad_mixed = plain_dot(grad_whole1, mixer_full[1])
    mixer_gradient_list = pullback(grad_mixed)
    grad_projs = jnp.concatenate(
        [member.astype(jnp.bfloat16) for member in mixer_gradient_list[:6]], axis=1
    )
    grad_hidden1 = lax.psum_scatter(
        right_dot(grad_projs, mixer_full[0]).astype(jnp.bfloat16),
        "tensor",
        scatter_dimension=0,
        tiled=True,
    ).astype(jnp.float32)
    grad_normed1, first_gain_gradient = rms_back(grad_hidden1, normed1, inverse1, norm_gain1)
    grad_tokens = (grad_residual + grad_normed1).astype(jnp.bfloat16)
    proj_part = left_dot(whole1, grad_projs)
    out_part = left_dot(grad_whole1, mixed_half)
    mixer_shard = lax.psum_scatter(
        jnp.concatenate([proj_part, out_part], axis=1), "dp", scatter_dimension=0, tiled=True
    )
    mixer_grads = split_columns(mixer_shard, mixer_widths + [value_cols])
    ffn_grads = split_columns(ffn_shard, [hidden_cols, hidden_cols, hidden_cols])

    def widen(element, axis_pos):
        size_one = element.shape[axis_pos]
        shape_all = list(element.shape)
        shape_all[axis_pos] = size_one * tensor_count
        return lax.dynamic_update_slice_in_dim(
            jnp.zeros(shape_all, jnp.float32), element, tensor_index * size_one, axis_pos
        )

    small_sums = lax.psum(
        (
            first_gain_gradient,
            second_gain_gradient,
            mixer_gradient_list[11],
            widen(mixer_gradient_list[6], 1),
            widen(mixer_gradient_list[7], 1),
            widen(mixer_gradient_list[8], 1),
            widen(mixer_gradient_list[9], 0),
            widen(mixer_gradient_list[10], 0),
        ),
        ("dp", "tensor"),
    )
    return (
        output,
        grad_tokens,
        small_sums[0],
        mixer_grads[0],
        mixer_grads[1],
        mixer_grads[2],
        mixer_grads[3],
        mixer_grads[4],
        mixer_grads[5],
        small_sums[3],
        small_sums[4],
        small_sums[5],
        small_sums[6],
        small_sums[7],
        small_sums[2],
        mixer_grads[6],
        small_sums[1],
        ffn_grads[0],
        ffn_grads[1],
        ffn_grads[2],
    )


def solution(mesh):
    in_specs = (
        P(("dp", "tensor"), None),
        P(("dp", "tensor"), None),
        P("dp"),
        P(),
        P("dp", "tensor"),
        P("dp", "tensor"),
        P("dp", "tensor"),
        P("dp", "tensor"),
        P("dp", "tensor"),
        P("dp", "tensor"),
        P(None, "tensor"),
        P(None, "tensor"),
        P(None, "tensor"),
        P("tensor"),
        P("tensor"),
        P(),
        P("dp", "tensor"),
        P(),
        P("dp", "tensor"),
        P("dp", "tensor"),
        P("dp", "tensor"),
    )
    out_specs = (
        P(("dp", "tensor"), None),
        P(("dp", "tensor"), None),
        P(),
        P("dp", "tensor"),
        P("dp", "tensor"),
        P("dp", "tensor"),
        P("dp", "tensor"),
        P("dp", "tensor"),
        P("dp", "tensor"),
        P(),
        P(),
        P(),
        P(),
        P(),
        P(),
        P("dp", "tensor"),
        P(),
        P("dp", "tensor"),
        P("dp", "tensor"),
        P("dp", "tensor"),
    )
    return jax.shard_map(
        on_device, mesh=mesh, in_specs=in_specs, out_specs=out_specs, check_vma=False
    )
```

profile of v0, /device:TPU:8, one launch (start us, length us, event | category | flops | bytes accessed | tf_op | source)
XLA Modules:
  0.0 1243.7 jit_solution(5438580144339664088)
XLA Ops:
  14.0 8.7 all_gather.24
  23.0 52.0 %all-gather.5.cloned.1.call-done = bf16[1024,3080]{1,0:T(8,128)(2,1)} async-done(((bf16[64,3080]{1,0:T(8,128)(2,1)}), bf16[1024,3080]{1,0:T(8,128)(2,1)}) %all-gather.5.cloned.1.call-update) | async-done | bytes 6307856 | tf_op jit(solution)/shard_map/all_gather | solution.py:204
  75.0 5.6 fusion.229
  85.8 3.5 multiply_reduce_fusion.15
  91.7 2.0 reshape.705
  95.3 3.9 fusion.168
  102.3 2.4 copy.201
  109.7 144.0 %while.98 = (s32[]{:T(128)}, f32[4,256,128]{2,1,0:T(8,128)S(1)}, f32[4,4,64,256]{3,1,2,0:T(4,128)}, f32[4,4,64,64]{3,2,1,0:T(8,128)}, f32[4,4,128,64]{2,3,1,0:T(...) while((s32[]{:T(128)}, f32[4,256,128]{2,1,0:T(8,128)S(1)}, ...), condition=%wide.region_5.6_spmd.clone.clone, body=%wide.region_3.5_spmd.clone.clone.sunk | while | flops 479990848 | bytes 12846126 | solution.py:102
  115.0 19.7 %custom-call.48 = f32[4,1,64,64]{2,3,1,0:T(8,128)S(1)} custom-call(f32[4,1,64,64]{3,2,1,0:T(8,128)S(1)} %add_bitcast_fusion.4), custom_call_target="InvertDiagBlocksLowerTriangular" | custom-call | tf_op jit(solution)/shard_map/jvp(vmap())/while/body/eval_jaxpr/triangular_solve | solution.py:72
  151.0 19.7 %custom-call.48 = f32[4,1,64,64]{2,3,1,0:T(8,128)S(1)} custom-call(f32[4,1,64,64]{3,2,1,0:T(8,128)S(1)} %add_bitcast_fusion.4), custom_call_target="InvertDiagBlocksLowerTriangular" | custom-call | tf_op jit(solution)/shard_map/jvp(vmap())/while/body/eval_jaxpr/triangular_solve | solution.py:72
  186.9 19.7 %custom-call.48 = f32[4,1,64,64]{2,3,1,0:T(8,128)S(1)} custom-call(f32[4,1,64,64]{3,2,1,0:T(8,128)S(1)} %add_bitcast_fusion.4), custom_call_target="InvertDiagBlocksLowerTriangular" | custom-call | tf_op jit(solution)/shard_map/jvp(vmap())/while/body/eval_jaxpr/triangular_solve | solution.py:72
  222.9 19.7 %custom-call.48 = f32[4,1,64,64]{2,3,1,0:T(8,128)S(1)} custom-call(f32[4,1,64,64]{3,2,1,0:T(8,128)S(1)} %add_bitcast_fusion.4), custom_call_target="InvertDiagBlocksLowerTriangular" | custom-call | tf_op jit(solution)/shard_map/jvp(vmap())/while/body/eval_jaxpr/triangular_solve | solution.py:72
  253.7 2.5 copy.321
  256.3 2.5 copy.205
  259.4 2.8 fusion.218
  262.3 3.6 fusion.230
  268.1 14.2 %all_gather.30 = bf16[256,1024]{1,0:T(8,128)(2,1)S(1)} all-gather(bf16[128,1024]{1,0:T(8,128)(2,1)S(1)} %copy-done.41), channel_id=1, replica_groups=mesh['dp'=16,'tensor'=2] {'tensor'}, dimensions={0}, use_global_device_ids=true | all-gather | bytes 786432 | tf_op jit(solution)/shard_map/all_gather | solution.py:248
  282.3 7.4 reduce-scatter.9.cloned.1.call-done
  291.0 8.8 all_gather.27
  299.9 50.1 %all-gather.9.cloned.1.call-done = bf16[1024,2816]{1,0:T(8,128)(2,1)} async-done(((bf16[64,2816]{1,0:T(8,128)(2,1)}), bf16[1024,2816]{1,0:T(8,128)(2,1)}) %all-gather.9.cloned.1.call-update) | async-done | bytes 5767184 | tf_op jit(solution)/shard_map/all_gather | solution.py:232
  350.0 5.9 fusion.231
  355.9 38.8 %all-gather.11.cloned.1.call-done = bf16[1024,1408]{1,0:T(8,128)(2,1)} async-done(((bf16[64,1408]{1,0:T(8,128)(2,1)}), bf16[1024,1408]{1,0:T(8,128)(2,1)}) %all-gather.11.cloned.1.call-update) | async-done | bytes 2883600 | tf_op jit(solution)/shard_map/all_gather | solution.py:233
  394.7 5.0 multiply_convert_fusion.1
  400.9 2.7 fusion.170
  406.1 2.6 copy.206
  408.7 2.7 reshape.712
  412.4 3.9 convolution_convert_fusion.1
  416.4 4.8 fusion.191
  421.3 5.9 fusion.169
  429.1 10.6 reduce-scatter.11.cloned.1.call-done
  439.7 2.4 fusion.216
  442.1 8.7 all_gather.31
  452.6 2.7 reshape.711
  455.3 4.0 fusion.165
  459.6 2.7 fusion.157
  465.2 191.7 %while.99 = (s32[]{:T(128)}, f32[4,256,128]{2,1,0:T(8,128)S(1)}, f32[4,4,64,128]{3,2,1,0:T(8,128)}, f32[4,4,64,128]{3,2,1,0:T(8,128)}, f32[4,4,64,256]{3,2,1,0:T...) while((s32[]{:T(128)}, f32[4,256,128]{2,1,0:T(8,128)S(1)}, ...), condition=%wide.region_24.25_spmd.clone.clone, body=%wide.region_13.24_spmd.clone.clone.sunk | while | flops 971683904 | bytes 18991880 | solution.py:102
  472.8 19.7 %custom-call.49 = f32[4,1,64,64]{2,3,1,0:T(8,128)S(1)} custom-call(f32[4,1,64,64]{3,2,1,0:T(8,128)S(1)} %add_bitcast_fusion.5), custom_call_target="InvertDiagBlocksLowerTriangular" | custom-call | tf_op jit(solution)/shard_map/transpose(jvp(vmap()))/while/body/eval_jaxpr/triangular_solve | solution.py:72
  497.1 1.9 convolution_add_fusion.17
  500.7 2.2 fusion.340
  520.6 19.7 %custom-call.49 = f32[4,1,64,64]{2,3,1,0:T(8,128)S(1)} custom-call(f32[4,1,64,64]{3,2,1,0:T(8,128)S(1)} %add_bitcast_fusion.5), custom_call_target="InvertDiagBlocksLowerTriangular" | custom-call | tf_op jit(solution)/shard_map/transpose(jvp(vmap()))/while/body/eval_jaxpr/triangular_solve | solution.py:72
  544.9 2.0 convolution_add_fusion.17
  548.5 2.2 fusion.340
  568.5 19.7 %custom-call.49 = f32[4,1,64,64]{2,3,1,0:T(8,128)S(1)} custom-call(f32[4,1,64,64]{3,2,1,0:T(8,128)S(1)} %add_bitcast_fusion.5), custom_call_target="InvertDiagBlocksLowerTriangular" | custom-call | tf_op jit(solution)/shard_map/transpose(jvp(vmap()))/while/body/eval_jaxpr/triangular_solve | solution.py:72
  592.7 1.9 convolution_add_fusion.17
  596.3 2.2 fusion.340
  616.3 19.7 %custom-call.49 = f32[4,1,64,64]{2,3,1,0:T(8,128)S(1)} custom-call(f32[4,1,64,64]{3,2,1,0:T(8,128)S(1)} %add_bitcast_fusion.5), custom_call_target="InvertDiagBlocksLowerTriangular" | custom-call | tf_op jit(solution)/shard_map/transpose(jvp(vmap()))/while/body/eval_jaxpr/triangular_solve | solution.py:72
  640.5 1.9 convolution_add_fusion.17
  644.1 2.2 fusion.340
  663.9 2.6 reshape.735
  666.6 3.7 multiply_reduce_fusion.5
  680.0 3.3 reshape.739
  683.3 4.9 multiply_reduce_fusion.3
  693.1 2.3 add_convert_fusion.2
  697.5 4.1 concatenate.28
  701.6 5.6 convolution_convert_fusion
  707.3 11.9 pad_maximum_fusion
  722.9 7.2 pad_maximum_fusion.1
  730.1 18.9 %copy.246 = f32[1024,4104]{1,0:T(8,128)} copy(f32[1024,4104]{0,1:T(8,128)} %pad_maximum_fusion.1) | data formatting | bytes 33619968
  751.8 2.0 fusion.178
  753.8 153.3 %reduce-scatter.17.cloned.1.call-done = f32[64,4224]{1,0:T(8,128)} async-done(((f32[1024,4224]{1,0:T(8,128)}), f32[64,4224]{1,0:T(8,128)}) %reduce-scatter.17.cloned.1.call-update) | async-done | bytes 1081360 | tf_op jit(solution)/shard_map/reduce_scatter | solution.py:263
  907.1 2.2 fusion.222
  909.3 182.9 %reduce-scatter.19.cloned.1.call-done = f32[64,4104]{1,0:T(8,128)} async-done(((f32[1024,4104]{1,0:T(8,128)}), f32[64,4104]{1,0:T(8,128)}) %reduce-scatter.19.cloned.1.call-update) | async-done | bytes 1050640
  1093.9 2.1 fusion.223
  1098.1 128.7 %all-reduce.36.cloned.1.call-done = (f32[1024]{0:T(1024)}, f32[4,1024]{1,0:T(4,128)}, f32[4,1024]{1,0:T(4,128)}, f32[4,2048]{1,0:T(4,128)}, f32[8]{0:T(128)}, /*index=5*/f32[8]{0:T(128)}, f32[256]{0:T(256)}, f32[1024]{0:T(1024)}) async-done(((f32[1024]{0:T(1024)}, f32[4,1024]{1,0:T(4,128)}, f32[4,1024]{1,0:T(4,128)}, f32[4,2048]{1,0:T(4,128)}, f32[8]{0:T(128)}, /*index=5*/f32[8]{0:T(128)}, f32[256]{0:T(256)}, ...) | async-done | bytes 74832 | tf_op jit(solution)/shard_map/psum | solution.py:296
  (671 shorter events, 242.4 us)
Async XLA Ops:
  7.2 15.5 %copy-start.101 = (f32[256]{0:T(256)S(1)}, f32[256]{0:T(256)}, u32[]{:S(2)}) copy-start(f32[256]{0:T(256)} %param.40) | copy-start | bytes 3076
  7.2 15.5 %copy-start.116 = (f32[4]{0:T(128)S(1)}, f32[4]{0:T(128)}, u32[]{:S(2)}) copy-start(f32[4]{0:T(128)} %param.38) | copy-start | bytes 52
  7.2 15.5 %copy-start.103 = (f32[4,512]{1,0:T(4,128)S(1)}, f32[4,512]{1,0:T(4,128)}, u32[]{:S(2)}) copy-start(f32[4,512]{1,0:T(4,128)} %param.35) | copy-start | bytes 24580
  7.2 15.5 %copy-start.104 = (f32[4,512]{1,0:T(4,128)S(1)}, f32[4,512]{1,0:T(4,128)}, u32[]{:S(2)}) copy-start(f32[4,512]{1,0:T(4,128)} %param.36) | copy-start | bytes 24580
  7.2 15.6 %copy-start.99 = (f32[4,1024]{1,0:T(4,128)S(1)}, f32[4,1024]{1,0:T(4,128)}, u32[]{:S(2)}) copy-start(f32[4,1024]{1,0:T(4,128)} %param.37) | copy-start | bytes 49156
  7.2 67.7 %all-gather.5.cloned.1.call-start = ((), (), s32[]{:S(2)}) async-start(), calls=%async_computation.6 | async-start | bytes 6963200 | tf_op jit(solution)/shard_map/all_gather | solution.py:204
  10.8 251.5 %all-gather.7.cloned.1.call-start = ((), (), s32[]{:S(2)}) async-start(), calls=%async_computation.7 | async-start | bytes 2228224 | tf_op jit(solution)/shard_map/all_gather | solution.py:205
  11.5 278.2 %reduce-scatter.9.cloned.1.call-start = ((), (), s32[]{:S(2)}) async-start(), calls=%async_computation.8 | async-start | bytes 1572864 | tf_op jit(solution)/shard_map/reduce_scatter | solution.py:225
  12.9 67.7 %copy-start.105 = (f32[128]{0:T(128)}, f32[128]{0:T(128)S(1)}, u32[]{:S(2)}) copy-start(f32[128]{0:T(128)S(1)} %add_rsqrt_fusion.3) | copy-start | bytes 1540
  22.7 52.3 %copy-start.31 = (bf16[256,1024]{1,0:T(8,128)(2,1)}, bf16[256,1024]{1,0:T(8,128)(2,1)S(1)}, u32[]{:S(2)}) copy-start(bf16[256,1024]{1,0:T(8,128)(2,1)S(1)} %all_gather.24) | copy-start | bytes 1572868
  22.7 236.7 %copy-start.67 = (f32[1,2,4,128]{3,1,2,0:T(2,128)}, f32[1,2,4,128]{3,1,2,0:T(2,128)S(1)}, u32[]{:S(2)}) copy-start(f32[1,2,4,128]{3,1,2,0:T(2,128)S(1)} %copy.322) | copy-start | bytes 12292
  22.7 62.8 %copy-start.111 = (f32[4]{0:T(128)}, f32[4]{0:T(128)S(1)}, u32[]{:S(2)}) copy-start(f32[4]{0:T(128)S(1)} %exponential_negate_fusion) | copy-start | bytes 52
  22.8 63.0 %copy-start.85 = (f32[1,512]{1,0:T(1,128)}, f32[1,512]{1,0:T(1,128)S(1)}, u32[]{:S(2)}) copy-start(f32[1,512]{1,0:T(1,128)S(1)} %get-tuple-element.2632) | copy-start | bytes 6148
  22.8 63.0 %copy-start.89 = (f32[1,512]{1,0:T(1,128)}, f32[1,512]{1,0:T(1,128)S(1)}, u32[]{:S(2)}) copy-start(f32[1,512]{1,0:T(1,128)S(1)} %get-tuple-element.2633) | copy-start | bytes 6148
  22.8 63.0 %copy-start.93 = (f32[1,512]{1,0:T(1,128)}, f32[1,512]{1,0:T(1,128)S(1)}, u32[]{:S(2)}) copy-start(f32[1,512]{1,0:T(1,128)S(1)} %get-tuple-element.2631) | copy-start | bytes 6148
  22.8 63.0 %copy-start.97 = (f32[1,512]{1,0:T(1,128)}, f32[1,512]{1,0:T(1,128)S(1)}, u32[]{:S(2)}) copy-start(f32[1,512]{1,0:T(1,128)S(1)} %get-tuple-element.2630) | copy-start | bytes 6148
  22.8 63.0 %copy-start.83 = (f32[1,512]{1,0:T(1,128)}, f32[1,512]{1,0:T(1,128)S(1)}, u32[]{:S(2)}) copy-start(f32[1,512]{1,0:T(1,128)S(1)} %get-tuple-element.2636) | copy-start | bytes 6148
  22.8 63.0 %copy-start.87 = (f32[1,512]{1,0:T(1,128)}, f32[1,512]{1,0:T(1,128)S(1)}, u32[]{:S(2)}) copy-start(f32[1,512]{1,0:T(1,128)S(1)} %get-tuple-element.2637) | copy-start | bytes 6148
  22.8 63.0 %copy-start.91 = (f32[1,512]{1,0:T(1,128)}, f32[1,512]{1,0:T(1,128)S(1)}, u32[]{:S(2)}) copy-start(f32[1,512]{1,0:T(1,128)S(1)} %get-tuple-element.2635) | copy-start | bytes 6148
  22.9 63.0 %copy-start.95 = (f32[1,512]{1,0:T(1,128)}, f32[1,512]{1,0:T(1,128)S(1)}, u32[]{:S(2)}) copy-start(f32[1,512]{1,0:T(1,128)S(1)} %get-tuple-element.2634) | copy-start | bytes 6148
  22.9 72.4 %copy-start.69 = (f32[1,1024]{1,0:T(1,128)}, f32[1,1024]{1,0:T(1,128)S(1)}, u32[]{:S(2)}) copy-start(f32[1,1024]{1,0:T(1,128)S(1)} %get-tuple-element.2628) | copy-start | bytes 12292
  22.9 72.4 %copy-start.71 = (f32[1,1024]{1,0:T(1,128)}, f32[1,1024]{1,0:T(1,128)S(1)}, u32[]{:S(2)}) copy-start(f32[1,1024]{1,0:T(1,128)S(1)} %get-tuple-element.2629) | copy-start | bytes 12292
  22.9 72.4 %copy-start.73 = (f32[1,1024]{1,0:T(1,128)}, f32[1,1024]{1,0:T(1,128)S(1)}, u32[]{:S(2)}) copy-start(f32[1,1024]{1,0:T(1,128)S(1)} %get-tuple-element.2627) | copy-start | bytes 12292
  22.9 72.4 %copy-start.81 = (f32[1,1024]{1,0:T(1,128)}, f32[1,1024]{1,0:T(1,128)S(1)}, u32[]{:S(2)}) copy-start(f32[1,1024]{1,0:T(1,128)S(1)} %get-tuple-element.2626) | copy-start | bytes 12292
  80.7 5.1 copy-start.9
  80.7 5.1 copy-start.11
  83.3 12.0 copy-start.4
  90.5 14.2 %copy-start.21 = (f32[256,512]{0,1:T(8,128)}, f32[256,512]{0,1:T(8,128)S(1)}, u32[]{:S(2)}) copy-start(f32[256,512]{0,1:T(8,128)S(1)} %get-tuple-element.2640) | copy-start | bytes 1572868
  93.7 5.6 copy-start.60
  253.7 5.1 copy-start.47
  253.7 5.1 copy-start.51
  253.7 5.1 copy-start.53
  253.7 5.1 copy-start.100
  253.7 5.1 copy-start.1
  262.3 5.8 copy-start.41
  265.9 23.8 %copy-start.8 = (bf16[128,1024]{1,0:T(8,128)(2,1)S(1)}, bf16[128,1024]{1,0:T(8,128)(2,1)}, u32[]{:S(2)}) copy-start(bf16[128,1024]{1,0:T(8,128)(2,1)} %param.25) | copy-start | bytes 786436
  265.9 25.0 %copy-start.62 = (f32[1024]{0:T(1024)S(1)}, f32[1024]{0:T(1024)}, u32[]{:S(2)}) copy-start(f32[1024]{0:T(1024)} %param.42) | copy-start | bytes 12292
  265.9 84.1 %all-gather.9.cloned.1.call-start = ((), (), s32[]{:S(2)}) async-start(), calls=%async_computation.9 | async-start | bytes 6127616 | tf_op jit(solution)/shard_map/all_gather | solution.py:232
  266.8 128.0 %all-gather.11.cloned.1.call-start = ((), (), s32[]{:S(2)}) async-start(), calls=%async_computation.10 | async-start | bytes 3063808 | tf_op jit(solution)/shard_map/all_gather | solution.py:233
  267.4 159.9 %reduce-scatter.13.cloned.1.call-start = ((), (), s32[]{:S(2)}) async-start(), calls=%async_computation.12 | async-start | bytes 1572864 | tf_op jit(solution)/shard_map/reduce_scatter | solution.py:256
  268.1 126.7 %copy-start.113 = (bf16[256]{0:T(256)(128)(2,1)}, bf16[256]{0:T(256)(128)(2,1)S(1)}, u32[]{:S(2)}) copy-start(bf16[256]{0:T(256)(128)(2,1)S(1)} %compare_convert_fusion) | copy-start | bytes 1540
  282.3 112.4 %copy-start.29 = (bf16[256,1024]{1,0:T(8,128)(2,1)}, bf16[256,1024]{1,0:T(8,128)(2,1)S(1)}, u32[]{:S(2)}) copy-start(bf16[256,1024]{1,0:T(8,128)(2,1)S(1)} %all_gather.30) | copy-start | bytes 1572868
  290.9 65.0 %copy-start.107 = (f32[128]{0:T(128)}, f32[128]{0:T(128)S(1)}, u32[]{:S(2)}) copy-start(f32[128]{0:T(128)S(1)} %add_rsqrt_fusion.2) | copy-start | bytes 1540
  299.9 56.0 %copy-start.33 = (bf16[256,1024]{1,0:T(8,128)(2,1)}, bf16[256,1024]{1,0:T(8,128)(2,1)S(1)}, u32[]{:S(2)}) copy-start(bf16[256,1024]{1,0:T(8,128)(2,1)S(1)} %all_gather.27) | copy-start | bytes 1572868
  394.7 6.1 copy-start.119
  403.6 36.1 %reduce-scatter.11.cloned.1.call-start = ((), (), s32[]{:S(2)}) async-start(), calls=%async_computation.11 | async-start | bytes 786432 | tf_op jit(solution)/shard_map/reduce_scatter | solution.py:241
  406.1 5.3 copy-start.22
  416.3 333.5 %reduce-scatter.15.cloned.1.call-start = ((), (), s32[]{:S(2)}) async-start(), calls=%async_computation.13 | async-start | bytes 786432 | tf_op jit(solution)/shard_map/reduce_scatter | solution.py:272
  421.2 6.0 copy-start.63
  421.2 6.0 copy-start.108
  421.2 18.5 %copy-start.42 = (bf16[128,1024]{1,0:T(8,128)(2,1)S(1)}, bf16[128,1024]{1,0:T(8,128)(2,1)}, u32[]{:S(2)}) copy-start(bf16[128,1024]{1,0:T(8,128)(2,1)} %param.26) | copy-start | bytes 786436
  421.3 18.5 %copy-start.118 = (f32[128]{0:T(128)S(1)}, f32[128]{0:T(128)}, u32[]{:S(2)}) copy-start(f32[128]{0:T(128)} %compare_convert_fusion.1) | copy-start | bytes 1540
  439.7 11.2 copy-start.5
  459.6 5.6 copy-start.52
  459.6 5.6 copy-start.54
  493.0 7.4 copy-start.28
  540.8 7.4 copy-start.28
  588.6 7.4 copy-start.28
  636.4 7.4 copy-start.28
  683.3 4.9 copy-start.74
  690.3 5.1 copy-start.96
  707.2 199.9 %reduce-scatter.17.cloned.1.call-start = ((), (), s32[]{:S(2)}) async-start(), calls=%async_computation.14 | async-start | bytes 18382848 | tf_op jit(solution)/shard_map/reduce_scatter | solution.py:263
  719.2 372.9 %reduce-scatter.19.cloned.1.call-start = ((), (), s32[]{:S(2)}) async-start(), calls=%async_computation.15 | async-start | bytes 18382848
  749.1 477.8 %all-reduce.36.cloned.1.call-start = ((), (), s32[]{:S(2)}) async-start(), calls=%async_computation.16 | async-start | bytes 151552 | tf_op jit(solution)/shard_map/psum | solution.py:296
  (70 other events, 213.1 us)
Sparse Core Ops, SparseCore 0:
  10.9 64.0 all-gather.4
  77.1 39.0 all-gather.6
  266.0 23.6 reduce-scatter.8
  292.4 57.5 all-gather.8
  352.1 42.5 all-gather.10
  403.8 18.9 reduce-scatter.12
  425.0 14.6 reduce-scatter.10
  707.4 14.6 reduce-scatter.14
  726.2 180.9 reduce-scatter.16
  911.1 181.0 reduce-scatter.18
  1100.3 126.4 all-reduce.35
where the time goes:
time: 1250 us; the launch traced here: 1240 us
  waiting for transfers between devices  625 us (50%)
  other arithmetic  277 us (22%)
  matrix products  149 us (12%)
  local copies, waits for them, and re-layouts  134 us (11%)
  blocking collectives  40.5 us (3%)
  between operations  16.3 us (1%)
    unnamed x12, waiting for transfers between devices  184 us
    another operation x40, other arithmetic, delta_block(): lax.linalg.triangular_solve(coupling + jnp.eye(block_len, dtype=jnp.float...  162 us
    reduce_scatter x1, waiting for transfers between devices, on_device(): lax.psum_scatter(jnp.concatenate([gate_up_part, down_part], axis=1), 'dp'...  153 us
    psum x1, waiting for transfers between devices, on_device(): lax.psum((first_gain_gradient, second_gain_gradient, mixer_gradient_list[...  129 us
    dot_general x72, matrix products, exact_dot(): return jnp.dot(left, right, precision=highest)  82 us
    all_gather x1, waiting for transfers between devices, on_device(): lax.all_gather(mixer_joined, 'dp', axis=0, tiled=True)  52 us
    all_gather x1, waiting for transfers between devices, on_device(): lax.all_gather(ffn_joined, 'dp', axis=0, tiled=True)  50.1 us
    unnamed x256, local copies, waits for them, and re-layouts  41.7 us
  transfers between devices with their start and end apart: 11, of which 8 were waited for; matrix products, arithmetic and copies ran while one was open for 22% of the time, Pallas kernels for 0%

commit v1 on v0

v1 whole, which is shorter than its diff:
```python
import functools

import jax
import jax.numpy as jnp
from jax import lax
from jax.experimental import pallas as pl
from jax.experimental.pallas import tpu as pltpu
from jax.sharding import PartitionSpec as P

SUB = 128
UNROLLED_CHIPS = 16
bf16 = jnp.bfloat16
f32 = jnp.float32


def dims_of(kind):
    return {
        "nn": (((1,), (0,)), ((), ())),
        "nt": (((1,), (1,)), ((), ())),
        "tn": (((0,), (0,)), ((), ())),
    }[kind]


def dot1(left, right, kind="nn"):
    return lax.dot_general(left, right, dims_of(kind), preferred_element_type=f32)


def cut(array):
    high = array.astype(bf16)
    return (high, (array - high.astype(f32)).astype(bf16))


def dot3(left, right, kind="nn"):
    return (
        dot1(left[0], right[0], kind)
        + dot1(left[0], right[1], kind)
        + dot1(left[1], right[0], kind)
    )


def shift_down(array, amount):
    if amount == 0:
        return array
    rows = lax.broadcasted_iota(jnp.int32, array.shape, 0)
    return jnp.where(rows >= amount, pltpu.roll(array, amount, 0), 0.0)


def shift_up(array, amount):
    if amount == 0:
        return array
    length = array.shape[0]
    rows = lax.broadcasted_iota(jnp.int32, array.shape, 0)
    return jnp.where(rows < length - amount, pltpu.roll(array, length - amount, 0), 0.0)


def conv_rows(projected, kernel):
    taps = kernel.shape[0]
    summed = kernel[taps - 1 : taps] * projected
    for offset in range(1, taps):
        tap = taps - 1 - offset
        summed = summed + kernel[tap : tap + 1] * shift_down(projected, offset)
    return summed


def conv_back(grad_conv, projected, kernel):
    taps = kernel.shape[0]
    grad_proj = kernel[taps - 1 : taps] * grad_conv
    for offset in range(1, taps):
        tap = taps - 1 - offset
        grad_proj = grad_proj + kernel[tap : tap + 1] * shift_up(grad_conv, offset)
    terms = []
    for tap in range(taps):
        moved = shift_down(projected, taps - 1 - tap)
        terms.append(jnp.sum(grad_conv * moved, 0, keepdims=True))
    return grad_proj, jnp.concatenate(terms, 0)


def silu_slope(values, sigma):
    return sigma * (1.0 + values * (1.0 - sigma))


def gate_rows(small, lanes_ref, heads):
    lane = lax.broadcasted_iota(jnp.int32, small.shape, 1)
    rate = jnp.exp(lanes_ref[0:1, :])
    shifted = small + lanes_ref[1:2, :]
    soft = jnp.maximum(shifted, 0.0) + jnp.log1p(jnp.exp(-jnp.abs(shifted)))
    gates = jnp.where(lane >= heads, -rate * soft, 0.0)
    slope = jnp.where(lane >= heads, -rate * jax.nn.sigmoid(shifted), 0.0)
    return jax.nn.sigmoid(small), gates, slope


def sum_gates(gates):
    length = gates.shape[0]
    row = lax.broadcasted_iota(jnp.int32, (length, length), 0)
    col = lax.broadcasted_iota(jnp.int32, (length, length), 1)
    lower = (row >= col).astype(f32)
    upper = (row <= col).astype(f32)
    kwargs = dict(precision=lax.Precision.HIGHEST, preferred_element_type=f32)
    by_row = lax.dot_general(lower, gates, dims_of("nn"), **kwargs)
    by_col = lax.dot_general(gates, upper, dims_of("tn"), **kwargs)
    return by_row, by_col


def lane_pick(array, index):
    lane = lax.broadcasted_iota(jnp.int32, array.shape, 1)
    return jnp.sum(jnp.where(lane == index, array, 0.0), 1, keepdims=True)


def row_pick(array, index):
    row = lax.broadcasted_iota(jnp.int32, array.shape, 0)
    return jnp.sum(jnp.where(row == index, array, 0.0), 0, keepdims=True)


def decay_square(cum_col, cum_row):
    length = cum_col.shape[0]
    row = lax.broadcasted_iota(jnp.int32, (length, length), 0)
    col = lax.broadcasted_iota(jnp.int32, (length, length), 1)
    keep = row >= col
    square = jnp.where(keep, jnp.exp(jnp.where(keep, cum_col - cum_row, 0.0)), 0.0)
    return square, keep, row > col


def unit_rows(raw, kernel):
    conv = conv_rows(raw, kernel)
    sigma = jax.nn.sigmoid(conv)
    act = conv * sigma
    inverse = lax.rsqrt(jnp.sum(act * act, -1, keepdims=True) + 1e-06)
    return conv, sigma, act, inverse


def forward_kernel(
    heads, per_step, key_dim, value_dim,
    query_ref, key_ref, value_ref, gate_ref, small_ref, lanes_ref,
    conv_query_ref, conv_key_ref, conv_value_ref, gain_ref,
    half_ref, mixed_ref, update_ref, inverse_ref,
):
    step = pl.program_id(0)
    length = query_ref.shape[0]
    blocks = length // SUB
    beta_all, gates_all, _ = gate_rows(small_ref[...], lanes_ref, heads)
    cum_all, cum_rows = sum_gates(gates_all)
    sub_row = lax.broadcasted_iota(jnp.int32, (SUB, SUB), 0)
    sub_col = lax.broadcasted_iota(jnp.int32, (SUB, SUB), 1)
    state = []
    for local in range(per_step):
        head = step * per_step + local
        kcut = slice(local * key_dim, (local + 1) * key_dim)
        vcut = slice(local * value_dim, (local + 1) * value_dim)
        _, _, query_act, query_inv = unit_rows(query_ref[:, kcut], conv_query_ref[:, kcut])
        query = query_act * query_inv * key_dim ** (-0.5)
        _, _, key_act, key_inv = unit_rows(key_ref[:, kcut], conv_key_ref[:, kcut])
        key = key_act * key_inv
        value_conv = conv_rows(value_ref[:, vcut], conv_value_ref[:, vcut])
        value = value_conv * jax.nn.sigmoid(value_conv)
        beta = lane_pick(beta_all, head)
        decay, keep, strict = decay_square(
            lane_pick(cum_all, heads + head), row_pick(cum_rows, heads + head)
        )
        key_parts = cut(key)
        coupling = jnp.where(strict, beta * dot3(key_parts, key_parts, "nt") * decay, 0.0)
        mix = dot3(cut(query), key_parts, "nt") * decay
        state.append((coupling, mix, beta * value))
    inverses = []
    for coupling, _, _ in state:
        parts = []
        for block in range(blocks):
            span = slice(block * SUB, (block + 1) * SUB)
            parts.append(coupling[span, span])
        inverses.append(parts)
    squares = [[part for part in parts] for parts in inverses]
    eye = (sub_row == sub_col).astype(f32)
    size = 1
    current = [[None] * blocks for _ in state]
    while size < SUB:
        member = ((sub_row // (2 * size)) == (sub_col // (2 * size))) & (
            (sub_row // size) != (sub_col // size)
        )
        for h in range(per_step):
            for block in range(blocks):
                cross = jnp.where(member, squares[h][block], 0.0)
                if size == 1:
                    current[h][block] = eye - cross
                else:
                    now = cut(current[h][block])
                    inner = dot3(cut(cross), now)
                    current[h][block] = current[h][block] - dot3(now, cut(inner))
        size = 2 * size
    for local in range(per_step):
        vcut = slice(local * value_dim, (local + 1) * value_dim)
        coupling, mix, target = state[local]
        solved = []
        for block in range(blocks):
            span = slice(block * SUB, (block + 1) * SUB)
            rest = target[span]
            for before in range(block):
                past = slice(before * SUB, (before + 1) * SUB)
                rest = rest - dot3(cut(coupling[span, past]), cut(solved[before]))
            solved.append(dot3(cut(current[local][block]), cut(rest)))
            inverse_ref[local, block] = current[local][block]
        updates = jnp.concatenate(solved, 0)
        mixed = dot3(cut(mix), cut(updates))
        update_ref[:, vcut] = updates
        mixed_ref[:, vcut] = mixed
        inverse = lax.rsqrt(jnp.mean(mixed * mixed, -1, keepdims=True) + 1e-05)
        gate = gate_ref[:, vcut]
        half_ref[:, vcut] = (
            mixed * inverse * gain_ref[...] * (gate * jax.nn.sigmoid(gate))
        ).astype(bf16)


def unit_back(grad, conv, sigma, act, inverse, scale):
    inner = jnp.sum(grad * act, -1, keepdims=True)
    grad_act = scale * inverse * (grad - act * (inverse * inverse) * inner)
    return grad_act * silu_slope(conv, sigma)


def backward_kernel(
    heads, per_step, key_dim, value_dim, offsets,
    query_ref, key_ref, value_ref, gate_ref, small_ref, lanes_ref,
    conv_query_ref, conv_key_ref, conv_value_ref, gain_ref,
    mixed_ref, update_ref, inverse_ref, grad_ref,
    grads_ref, conv_query_out, conv_key_out, conv_value_out, gain_out, lanes_out,
    beta_acc, gate_acc,
):
    step = pl.program_id(0)
    length = query_ref.shape[0]
    blocks = length // SUB
    small = small_ref[...]
    beta_all, gates_all, slope_all = gate_rows(small, lanes_ref, heads)
    cum_all, cum_rows = sum_gates(gates_all)
    lane = lax.broadcasted_iota(jnp.int32, small.shape, 1)
    upper = (
        lax.broadcasted_iota(jnp.int32, (length, length), 0)
        <= lax.broadcasted_iota(jnp.int32, (length, length), 1)
    ).astype(bf16)

    @pl.when(step == 0)
    def _():
        beta_acc[...] = jnp.zeros_like(beta_acc)
        gate_acc[...] = jnp.zeros_like(gate_acc)
        gain_out[...] = jnp.zeros_like(gain_out)

    for local in range(per_step):
        head = step * per_step + local
        kcut = slice(local * key_dim, (local + 1) * key_dim)
        vcut = slice(local * value_dim, (local + 1) * value_dim)
        scale = key_dim ** (-0.5)
        query_raw = query_ref[:, kcut]
        key_raw = key_ref[:, kcut]
        value_raw = value_ref[:, vcut]
        query_conv, query_sigma, query_act, query_inv = unit_rows(
            query_raw, conv_query_ref[:, kcut]
        )
        query = query_act * query_inv * scale
        key_conv, key_sigma, key_act, key_inv = unit_rows(key_raw, conv_key_ref[:, kcut])
        key = key_act * key_inv
        value_conv = conv_rows(value_raw, conv_value_ref[:, vcut])
        value_sigma = jax.nn.sigmoid(value_conv)
        value = value_conv * value_sigma
        mixed = mixed_ref[:, vcut]
        inverse = lax.rsqrt(jnp.mean(mixed * mixed, -1, keepdims=True) + 1e-05)
        gate = gate_ref[:, vcut]
        gate_sigma = jax.nn.sigmoid(gate)
        gain = gain_ref[...]
        normed = mixed * inverse
        grad_out = grad_ref[:, vcut]
        through = grad_out * normed
        grad_gate = through * gain * silu_slope(gate, gate_sigma)
        swish = gate * gate_sigma
        gain_out[0:1, :] += jnp.sum(through * swish, 0, keepdims=True)
        grad_normed = grad_out * gain * swish
        grad_mixed = inverse * (
            grad_normed - normed * jnp.mean(grad_normed * normed, -1, keepdims=True)
        )
        beta = lane_pick(beta_all, head)
        decay, keep, strict = decay_square(
            lane_pick(cum_all, heads + head), row_pick(cum_rows, heads + head)
        )
        key_parts = cut(key)
        query_parts = cut(query)
        pair = dot3(key_parts, key_parts, "nt") * decay
        coupling = jnp.where(strict, beta * pair, 0.0)
        mix = dot3(query_parts, key_parts, "nt") * decay
        updates = cut(update_ref[:, vcut])
        grad_parts = cut(grad_mixed)
        grad_mix = jnp.where(keep, dot3(grad_parts, updates, "nt"), 0.0)
        grad_updates = dot3(cut(mix), grad_parts, "tn")
        solved = [None] * blocks
        for block in reversed(range(blocks)):
            span = slice(block * SUB, (block + 1) * SUB)
            rest = grad_updates[span]
            for after in range(block + 1, blocks):
                later = slice(after * SUB, (after + 1) * SUB)
                rest = rest - dot3(cut(coupling[later, span]), cut(solved[after]), "tn")
            solved[block] = dot3(cut(inverse_ref[local, block]), cut(rest), "tn")
        grad_target = jnp.concatenate(solved, 0)
        grad_coupling = jnp.where(strict, -dot3(cut(grad_target), updates, "nt"), 0.0)
        grad_value = beta * grad_target
        grad_beta = jnp.sum(grad_target * value, -1, keepdims=True) + jnp.sum(
            grad_coupling * pair, -1, keepdims=True
        )
        flow = cut(grad_coupling * coupling + grad_mix * mix)
        run = dot1(upper, flow[0]) + dot1(upper, flow[1])
        grad_log = jnp.sum(jnp.where(strict, run, 0.0), -1, keepdims=True)
        grad_pair = cut(grad_coupling * beta * decay)
        grad_cross = cut(grad_mix * decay)
        grad_query = dot3(grad_cross, key_parts)
        grad_key = (
            dot3(grad_cross, query_parts, "tn")
            + dot3(grad_pair, key_parts)
            + dot3(grad_pair, key_parts, "tn")
        )
        grad_query_raw, grad_conv = conv_back(
            unit_back(grad_query, query_conv, query_sigma, query_act, query_inv, scale),
            query_raw, conv_query_ref[:, kcut],
        )
        conv_query_out[:, kcut] = grad_conv
        grad_key_raw, grad_conv = conv_back(
            unit_back(grad_key, key_conv, key_sigma, key_act, key_inv, 1.0),
            key_raw, conv_key_ref[:, kcut],
        )
        conv_key_out[:, kcut] = grad_conv
        grad_value_raw, grad_conv = conv_back(
            grad_value * silu_slope(value_conv, value_sigma), value_raw, conv_value_ref[:, vcut]
        )
        conv_value_out[:, vcut] = grad_conv
        key_start = pl.multiple_of(head * key_dim, key_dim)
        value_start = pl.multiple_of(head * value_dim, value_dim)
        grads_ref[:, pl.ds(offsets[0] + key_start, key_dim)] = grad_query_raw.astype(bf16)
        grads_ref[:, pl.ds(offsets[1] + key_start, key_dim)] = grad_key_raw.astype(bf16)
        grads_ref[:, pl.ds(offsets[2] + value_start, value_dim)] = grad_value_raw.astype(bf16)
        grads_ref[:, pl.ds(offsets[3] + value_start, value_dim)] = grad_gate.astype(bf16)
        beta_acc[...] += jnp.where(lane == head, grad_beta, 0.0)
        gate_acc[...] += jnp.where(lane == heads + head, grad_log, 0.0)

    @pl.when(step == pl.num_programs(0) - 1)
    def _():
        grad_log = gate_acc[...]
        grad_decay = grad_log * slope_all
        grad_small = beta_acc[...] * beta_all * (1.0 - beta_all) + grad_decay
        grads_ref[:, offsets[4] : offsets[4] + 2 * heads] = grad_small.astype(bf16)
        lanes_out[0:1, :] = jnp.sum(grad_log * gates_all, 0, keepdims=True)
        lanes_out[1:2, :] = jnp.sum(grad_decay, 0, keepdims=True)


def mixer_layout(projections, heads, key_cols, value_cols, per_step):
    length = projections.shape[0]
    key_dim = key_cols // heads
    value_dim = value_cols // heads
    wide_key = per_step * key_dim
    wide_value = per_step * value_dim
    taps_of = lambda taps: [
        pl.BlockSpec((taps, wide_key), lambda g: (0, g)),
        pl.BlockSpec((taps, wide_key), lambda g: (0, g)),
        pl.BlockSpec((taps, wide_value), lambda g: (0, g)),
    ]
    key_at = key_cols // wide_key
    value_at = 2 * key_cols // wide_value
    gate_at = (2 * key_cols + value_cols) // wide_value
    columns = [
        pl.BlockSpec((length, wide_key), lambda g: (0, g)),
        pl.BlockSpec((length, wide_key), lambda g: (0, key_at + g)),
        pl.BlockSpec((length, wide_value), lambda g: (0, value_at + g)),
        pl.BlockSpec((length, wide_value), lambda g: (0, gate_at + g)),
        pl.BlockSpec((length, 2 * heads), lambda g: (0, 0)),
        pl.BlockSpec((2, 2 * heads), lambda g: (0, 0)),
    ]
    rows = pl.BlockSpec((length, wide_value), lambda g: (0, g))
    blocks = length // SUB
    inverse = pl.BlockSpec((per_step, blocks, SUB, SUB), lambda g: (g, 0, 0, 0))
    gain = pl.BlockSpec((1, value_dim), lambda g: (0, 0))
    return columns, taps_of, rows, inverse, gain, key_dim, value_dim


def mixer_forward(projections, small, lanes, convs, gain, heads, key_cols, value_cols, per_step=2):
    length = projections.shape[0]
    taps = convs[0].shape[0]
    columns, taps_of, rows, inverse, gain_spec, key_dim, value_dim = mixer_layout(
        projections, heads, key_cols, value_cols, per_step
    )
    return pl.pallas_call(
        functools.partial(forward_kernel, heads, per_step, key_dim, value_dim),
        grid=(heads // per_step,),
        in_specs=columns + taps_of(taps) + [gain_spec],
        out_specs=[rows, rows, rows, inverse],
        out_shape=[
            jax.ShapeDtypeStruct((length, value_cols), bf16),
            jax.ShapeDtypeStruct((length, value_cols), f32),
            jax.ShapeDtypeStruct((length, value_cols), f32),
            jax.ShapeDtypeStruct((heads, length // SUB, SUB, SUB), f32),
        ],
        name="mixer_forward",
    )(projections, projections, projections, projections, small, lanes, *convs, gain)


def mixer_backward(
    projections, small, lanes, convs, gain, mixed, updates, inverses, grad_mixed,
    heads, key_cols, value_cols, per_step=2,
):
    length, width = projections.shape
    taps = convs[0].shape[0]
    columns, taps_of, rows, inverse, gain_spec, key_dim, value_dim = mixer_layout(
        projections, heads, key_cols, value_cols, per_step
    )
    offsets = (
        0, key_cols, 2 * key_cols, 2 * key_cols + value_cols, 2 * key_cols + 2 * value_cols
    )
    return pl.pallas_call(
        functools.partial(backward_kernel, heads, per_step, key_dim, value_dim, offsets),
        grid=(heads // per_step,),
        in_specs=columns + taps_of(taps) + [gain_spec, rows, rows, inverse, rows],
        out_specs=[pl.BlockSpec((length, width), lambda g: (0, 0))]
        + taps_of(taps)
        + [
            pl.BlockSpec((1, value_dim), lambda g: (0, 0)),
            pl.BlockSpec((2, 2 * heads), lambda g: (0, 0)),
        ],
        out_shape=[
            jax.ShapeDtypeStruct((length, width), bf16),
            jax.ShapeDtypeStruct((taps, key_cols), f32),
            jax.ShapeDtypeStruct((taps, key_cols), f32),
            jax.ShapeDtypeStruct((taps, value_cols), f32),
            jax.ShapeDtypeStruct((1, value_dim), f32),
            jax.ShapeDtypeStruct((2, 2 * heads), f32),
        ],
        scratch_shapes=[
            pltpu.VMEM((length, 2 * heads), f32),
            pltpu.VMEM((length, 2 * heads), f32),
        ],
        name="mixer_backward",
    )(
        projections, projections, projections, projections, small, lanes, *convs, gain,
        mixed, updates, inverses, grad_mixed,
    )


def plain_dot(left, right):
    return jnp.dot(left, right, preferred_element_type=f32)


def left_dot(left, right):
    return lax.dot_general(left, right, dims_of("tn"), preferred_element_type=f32)


def right_dot(left, right):
    return lax.dot_general(left, right, dims_of("nt"), preferred_element_type=f32)


def rms_rows(inputs, gain):
    wide_rows = inputs.astype(f32)
    inverse = lax.rsqrt(jnp.mean(wide_rows * wide_rows, -1, keepdims=True) + 1e-05)
    normed = wide_rows * inverse
    return (normed, inverse, (normed * gain).astype(bf16))


def rms_back(grad_rows, normed, inverse, gain):
    scaled = grad_rows * gain
    grad_in = inverse * (scaled - normed * jnp.mean(scaled * normed, -1, keepdims=True))
    return (grad_in, jnp.sum(grad_rows * normed, 0))


class Ring:
    def __init__(self, axis):
        self.axis = axis
        self.chips = lax.axis_size(axis) // 2
        evens = [chip for chip in range(self.chips) if chip % 2 == 0]
        odds = [chip for chip in range(self.chips) if chip % 2 == 1]
        order = evens + odds[::-1]
        following = [(order[i], order[(i + 1) % self.chips]) for i in range(self.chips)]
        self.ahead = [(2 * a + c, 2 * b + c) for a, b in following for c in (0, 1)]
        self.behind = [(2 * b + c, 2 * a + c) for a, b in following for c in (0, 1)]
        self.pairs = [(i, i ^ 1) for i in range(2 * self.chips)]
        index = lax.axis_index(axis)
        self.core = index % 2
        chip = index // 2
        self.position = jnp.where(
            chip % 2 == 0, chip // 2, self.chips - 1 - (chip - 1) // 2
        )

    def chip_at(self, shift):
        spot = (self.position + shift) % self.chips
        evens = (self.chips + 1) // 2
        return jnp.where(spot < evens, 2 * spot, 2 * (self.chips - 1 - spot) + 1)

    def forward(self, array):
        return lax.ppermute(array, self.axis, self.ahead)

    def backward(self, array):
        return lax.ppermute(array, self.axis, self.behind)

    def partner(self, array):
        return lax.ppermute(array, self.axis, self.pairs)

    def gather(self, shard):
        if self.chips > UNROLLED_CHIPS:
            return lax.all_gather(shard, self.axis, axis=0, tiled=True), shard
        rows = shard.shape[0]
        full = jnp.zeros((2 * self.chips * rows, shard.shape[1]), shard.dtype)

        def place(full, piece, shift, skip=0):
            base = 2 * self.chip_at(shift) * rows + skip
            full = lax.dynamic_update_slice(full, piece, (base + self.core * rows, 0))
            return lax.dynamic_update_slice(
                full, self.partner(piece), (base + (1 - self.core) * rows, 0)
            )

        full = place(full, shard, 0)
        ahead = behind = shard
        half = self.chips // 2
        for step in range(1, half):
            ahead = self.forward(ahead)
            behind = self.backward(behind)
            full = place(full, ahead, -step)
            full = place(full, behind, step)
        late = (ahead, behind)
        cut_row = rows // 2
        full = place(full, self.forward(ahead[:cut_row]), -half)
        full = place(full, self.backward(behind[cut_row:]), half, cut_row)
        return full, late

    def scatter(self, partial):
        if self.chips > UNROLLED_CHIPS:
            return lax.psum_scatter(
                partial.astype(f32), self.axis, scatter_dimension=0, tiled=True
            )
        rows = partial.shape[0] // (2 * self.chips)
        cut_row = rows // 2
        half = self.chips // 2

        def chunk(shift, core):
            start = (2 * self.chip_at(shift) + core) * rows
            return lax.dynamic_slice_in_dim(partial, start, rows, 0)

        def both(shift):
            mine = chunk(shift, self.core).astype(f32)
            return mine + self.partner(chunk(shift, 1 - self.core)).astype(f32)

        far = both(half).astype(bf16)
        ahead = self.forward(far[:cut_row])
        behind = self.backward(far[cut_row:])
        ahead_rows = slice(0, cut_row)
        behind_rows = slice(cut_row, rows)
        for step in range(half - 1, 0, -1):
            own = both(step)
            if step == half - 1:
                own = jnp.concatenate([own[:cut_row] + ahead.astype(f32), own[cut_row:]], 0)
            else:
                own = own + ahead.astype(f32)
            mirrored = both(-step)
            if step == half - 1:
                mirrored = jnp.concatenate(
                    [mirrored[:cut_row], mirrored[cut_row:] + behind.astype(f32)], 0
                )
            else:
                mirrored = mirrored + behind.astype(f32)
            ahead = self.forward(own.astype(bf16))
            behind = self.backward(mirrored.astype(bf16))
        own = both(0)
        if half == 1:
            return own + jnp.concatenate([ahead, behind], 0).astype(f32)
        return own + ahead.astype(f32) + behind.astype(f32)

    def total(self, array):
        size = 1
        while size < 2 * self.chips:
            flips = [(i, i ^ size) for i in range(2 * self.chips)]
            array = array + lax.ppermute(array, self.axis, flips)
            size = 2 * size
        return array


def others_of(array, axis):
    count = lax.axis_size(axis)
    received = []
    for shift in range(1, count):
        moves = [(i, (i + shift) % count) for i in range(count)]
        received.append(lax.ppermute(array, axis, moves))
    return received


def by_index(axis, pieces, dim):
    count = lax.axis_size(axis)
    index = lax.axis_index(axis)
    joined = None
    for value in range(count):
        here = jnp.concatenate([pieces[(value - i) % count] for i in range(count)], dim)
        joined = here if joined is None else jnp.where(index == value, here, joined)
    return joined


def gather_rows(array, axis):
    return by_index(axis, [array] + others_of(array, axis), 0)


def scatter_rows(partial, axis):
    count = lax.axis_size(axis)
    index = lax.axis_index(axis)
    rows = partial.shape[0] // count
    total = lax.dynamic_slice_in_dim(partial, index * rows, rows, 0)
    for shift in range(1, count):
        target = (index + shift) % count
        part = lax.dynamic_slice_in_dim(partial, target * rows, rows, 0).astype(bf16)
        moves = [(i, (i + shift) % count) for i in range(count)]
        total = total + lax.ppermute(part, axis, moves).astype(f32)
    return total


def after(array, done):
    return lax.optimization_barrier((array, done))[0]


def split_columns(array, widths):
    pieces = []
    offset = 0
    for width in widths:
        pieces.append(array[:, offset : offset + width])
        offset = offset + width
    return pieces


def on_device(
    tokens, out_cotangent, seq_lengths, norm_gain1, query_weight, key_weight, value_weight,
    out_gate_weight, beta_weight, decay_weight, conv_query, conv_key, conv_value,
    decay_log_rate, decay_bias, out_gain, out_weight, norm_gain2, ffn_gate_weight,
    ffn_up_weight, ffn_down_weight,
):
    ring = Ring("dp")
    local_rows = tokens.shape[0]
    tensor_index = lax.axis_index("tensor")
    tensor_count = lax.axis_size("tensor")
    seq_length = seq_lengths[0]
    local_pos = tensor_index * local_rows + jnp.arange(local_rows, dtype=jnp.int32)
    local_mask = (local_pos < seq_length).astype(f32)[:, None]
    key_cols = query_weight.shape[1]
    value_cols = value_weight.shape[1]
    heads = beta_weight.shape[1]
    hidden_cols = ffn_gate_weight.shape[1]
    mixer_widths = [key_cols, key_cols, value_cols, value_cols, heads, heads]
    small_at = 2 * key_cols + 2 * value_cols
    mixer_joined = jnp.concatenate(
        [query_weight, key_weight, value_weight, out_gate_weight, beta_weight, decay_weight], axis=1
    )
    ffn_joined = jnp.concatenate([ffn_gate_weight, ffn_up_weight], axis=1)
    mixer_full, late = ring.gather(mixer_joined)
    out_full, late = ring.gather(after(out_weight, late))
    ffn_full, late = ring.gather(after(ffn_joined, late))
    down_full, late = ring.gather(after(ffn_down_weight, late))

    normed1, inverse1, hidden1 = rms_rows(tokens, norm_gain1)
    whole1 = gather_rows(hidden1, "tensor")
    grad_local = (local_mask * out_cotangent.astype(f32)).astype(bf16)
    grad_whole = gather_rows(grad_local, "tensor")
    projections = plain_dot(whole1, mixer_full)
    small = projections[:, small_at:]
    blank = jnp.zeros((heads,), f32)
    lanes = jnp.stack(
        [jnp.concatenate([blank, decay_log_rate]), jnp.concatenate([blank, decay_bias])]
    )
    convs = (conv_query, conv_key, conv_value)
    gain_row = out_gain[None]
    mixed_half, mixed, updates, inverses = mixer_forward(
        projections, small, lanes, convs, gain_row, heads, key_cols, value_cols
    )
    branch = scatter_rows(right_dot(mixed_half, out_full), "tensor")
    residual = tokens.astype(f32) + branch
    normed2, inverse2, hidden2 = rms_rows(residual, norm_gain2)
    whole2 = gather_rows(hidden2, "tensor")
    pre_both = plain_dot(whole2, ffn_full)
    gate_pre = pre_both[:, :hidden_cols]
    up_pre = pre_both[:, hidden_cols:]
    sigma_gate = jax.nn.sigmoid(gate_pre)
    gate_act = gate_pre * sigma_gate
    inner_act = (gate_act * up_pre).astype(bf16)
    grad_inner = plain_dot(grad_whole, down_full)
    grad_gate_pre = (
        grad_inner * up_pre * sigma_gate * (1.0 + gate_pre * (1.0 - sigma_gate))
    ).astype(bf16)
    grad_up_pre = (grad_inner * gate_act).astype(bf16)
    grad_pre_both = jnp.concatenate([grad_gate_pre, grad_up_pre], axis=1)
    grad_hidden2 = scatter_rows(right_dot(grad_pre_both, ffn_full), "tensor")
    down_shard = ring.scatter(left_dot(grad_whole, inner_act).astype(bf16))
    ffn_shard = ring.scatter(left_dot(whole2, grad_pre_both).astype(bf16))
    ffn_branch = scatter_rows(right_dot(inner_act, down_full), "tensor")
    output = (local_mask * (residual + ffn_branch)).astype(bf16)
    grad_normed2, second_gain_gradient = rms_back(grad_hidden2, normed2, inverse2, norm_gain2)
    grad_residual = local_mask * out_cotangent.astype(f32) + grad_normed2
    grad_whole1 = gather_rows(grad_residual.astype(bf16), "tensor")
    grad_mixed = plain_dot(grad_whole1, out_full)
    out_shard = ring.scatter(left_dot(grad_whole1, mixed_half).astype(bf16))
    grad_projs, grad_conv_query, grad_conv_key, grad_conv_value, gain_sum, lane_sums = mixer_backward(
        projections, small, lanes, convs, gain_row, mixed, updates, inverses, grad_mixed,
        heads, key_cols, value_cols,
    )
    proj_shard = ring.scatter(left_dot(whole1, grad_projs).astype(bf16))
    grad_hidden1 = scatter_rows(right_dot(grad_projs, mixer_full), "tensor")
    grad_normed1, first_gain_gradient = rms_back(grad_hidden1, normed1, inverse1, norm_gain1)
    grad_tokens = (grad_residual + grad_normed1).astype(bf16)
    mixer_grads = split_columns(proj_shard, mixer_widths)
    ffn_grads = split_columns(ffn_shard, [hidden_cols, hidden_cols])

    taps = conv_query.shape[0]
    key_end = taps * key_cols
    value_end = taps * value_cols
    flat = [
        grad_conv_query.reshape(-1),
        grad_conv_key.reshape(-1),
        grad_conv_value.reshape(-1),
        lane_sums.reshape(-1),
    ]
    own_size = sum(member.shape[0] for member in flat)
    shared = [first_gain_gradient, second_gain_gradient, gain_sum.reshape(-1)]
    flat = jnp.concatenate(flat + shared)
    size = flat.shape[0]
    lanes_wide = 1024
    padded = -(-size // lanes_wide) * lanes_wide
    packed = jnp.pad(flat, (0, padded - size)).reshape(-1, lanes_wide)
    packed = ring.total(packed)
    pieces = [member.reshape(-1) for member in [packed] + others_of(packed, "tensor")]
    summed = pieces[0]
    for member in pieces[1:]:
        summed = summed + member

    def joined(start, rows, cols):
        parts = [member[start : start + rows * cols].reshape(rows, cols) for member in pieces]
        return by_index("tensor", parts, 1)

    lanes_at = 2 * key_end + value_end
    rates = joined(lanes_at + heads, 1, heads)[0]
    biases = joined(lanes_at + 3 * heads, 1, heads)[0]
    width1 = norm_gain1.shape[0]
    width2 = norm_gain2.shape[0]
    gain1_at = own_size
    gain2_at = own_size + width1
    gain_at = gain2_at + width2
    return (
        output,
        grad_tokens,
        summed[gain1_at : gain1_at + width1],
        mixer_grads[0],
        mixer_grads[1],
        mixer_grads[2],
        mixer_grads[3],
        mixer_grads[4],
        mixer_grads[5],
        joined(0, taps, key_cols),
        joined(key_end, taps, key_cols),
        joined(2 * key_end, taps, value_cols),
        rates,
        biases,
        summed[gain_at : gain_at + out_gain.shape[0]],
        out_shard,
        summed[gain2_at : gain2_at + width2],
        ffn_grads[0],
        ffn_grads[1],
        down_shard,
    )


def solution(mesh):
    in_specs = (
        P(("dp", "tensor"), None),
        P(("dp", "tensor"), None),
        P("dp"),
        P(),
        P("dp", "tensor"),
        P("dp", "tensor"),
        P("dp", "tensor"),
        P("dp", "tensor"),
        P("dp", "tensor"),
        P("dp", "tensor"),
        P(None, "tensor"),
        P(None, "tensor"),
        P(None, "tensor"),
        P("tensor"),
        P("tensor"),
        P(),
        P("dp", "tensor"),
        P(),
        P("dp", "tensor"),
        P("dp", "tensor"),
        P("dp", "tensor"),
    )
    out_specs = (
        P(("dp", "tensor"), None),
        P(("dp", "tensor"), None),
        P(),
        P("dp", "tensor"),
        P("dp", "tensor"),
        P("dp", "tensor"),
        P("dp", "tensor"),
        P("dp", "tensor"),
        P("dp", "tensor"),
        P(),
        P(),
        P(),
        P(),
        P(),
        P(),
        P("dp", "tensor"),
        P(),
        P("dp", "tensor"),
        P("dp", "tensor"),
        P("dp", "tensor"),
    )
    return jax.shard_map(
        on_device, mesh=mesh, in_specs=in_specs, out_specs=out_specs, check_vma=False
    )
```

time: 1250 us -> 463 us (0.37)
  waiting for transfers between devices: 625 us -> 166 us
  other arithmetic: 277 us -> 50.2 us
  matrix products: 149 us -> 32.4 us
  starting transfers between devices: 0.45 us -> 98.1 us
  local copies, waits for them, and re-layouts: 134 us -> 76.4 us
  blocking collectives: 40.5 us -> 0 us
  Pallas kernels: 0 us -> 28.4 us
  between operations: 16.3 us -> 3.16 us
    unnamed x12 -> x0, waiting for transfers between devices: 184 us -> none
    reduce_scatter x5 -> x0, waiting for transfers between devices: 171 us -> none  [the longest x1 153 us: on_device(): lax.psum_scatter(jnp.concatenate([gate_up_part, down_part], axis=1), 'dp'...]
    ppermute x0 -> x145, waiting for transfers between devices: none -> 166 us  [the longest x32 97.2 us: backward(): return lax.ppermute(array, self.axis, self.behind)]
    another operation x68 -> x9, other arithmetic: 168 us -> 2.85 us  [the longest x40 162 us: delta_block(): lax.linalg.triangular_solve(coupling + jnp.eye(block_len, dtype=jnp.float...]
    all_gather x4 -> x0, waiting for transfers between devices: 141 us -> none  [the longest x1 52 us: on_device(): lax.all_gather(mixer_joined, 'dp', axis=0, tiled=True)]
    psum x1 -> x0, waiting for transfers between devices: 129 us -> none  [on_device(): lax.psum((first_gain_gradient, second_gain_gradient, mixer_gradient_list[...]
    dot_general x88 -> x12, matrix products: 136 us -> 32.4 us  [the longest x4 13.8 us: plain_dot(): return jnp.dot(left, right, preferred_element_type=f32)]
    ppermute x0 -> x145, starting transfers between devices: none -> 98.1 us  [the longest x32 53.7 us: forward(): return lax.ppermute(array, self.axis, self.ahead)]
  transfers between devices with their start and end apart: 11 -> 145, of which waited for: 8 -> 53; matrix products, arithmetic and copies ran while one was open for 22% -> 31% of each run, Pallas kernels for 0% -> 6%
where the time goes in v1:
time: 463 us; the launch traced here: 454 us
  waiting for transfers between devices  166 us (36%)
  starting transfers between devices  98.1 us (21%)
  local copies, waits for them, and re-layouts  76.4 us (17%)
  other arithmetic  50.2 us (11%)
  matrix products  32.4 us (7%)
  Pallas kernels  28.4 us (6%)
    ppermute x32, waiting for transfers between devices, backward(): return lax.ppermute(array, self.axis, self.behind)  97.2 us
    ppermute x32, starting transfers between devices, forward(): return lax.ppermute(array, self.axis, self.ahead)  53.7 us
    ppermute x32, waiting for transfers between devices, forward(): return lax.ppermute(array, self.axis, self.ahead)  45.3 us
    dynamic_update_slice x36, local copies, waits for them, and re-layouts, place(): full = lax.dynamic_update_slice(full, piece, (base + self.core * rows, 0))  20.8 us
    ppermute x32, starting transfers between devices, backward(): return lax.ppermute(array, self.axis, self.behind)  18 us
    dynamic_update_slice x36, local copies, waits for them, and re-layouts, place(): lax.dynamic_update_slice(full, self.partner(piece), (base + (1 - self.cor...  17.5 us
    pallas_call x1, Pallas kernels, mixer_backward(): pl.pallas_call(functools.partial(backward_kernel, heads, per_step, key_di...  15.9 us
    dot_general x4, matrix products, plain_dot(): return jnp.dot(left, right, preferred_element_type=f32)  13.8 us
  transfers between devices with their start and end apart: 145, of which 53 were waited for; matrix products, arithmetic and copies ran while one was open for 31% of the time, Pallas kernels for 6%

profile of v1, /device:TPU:8, one launch (start us, length us, event | category | flops | bytes accessed | tf_op | source)
XLA Modules:
  0.0 454.3 jit_solution(11974489702147281724)
XLA Ops:
  3.4 2.0 collective-permute-start.2
  13.6 3.2 broadcast_in_dim.10
  22.6 7.7 %collective-permute-done.6 = bf16[64,3080]{1,0:T(8,128)(2,1)S(1)} collective-permute-done((bf16[64,3080]{1,0:T(8,128)(2,1)S(1)}, bf16[64,3080]{1,0:T(8,128)(2,1)S(1)}, u32[]{:S(2)}, u32[]{:S(2)}) %collective-permute-start.6) | collective-permute-done | bytes 394272 | tf_op jit(solution)/shard_map/ppermute | solution.py:486
  35.7 9.6 %collective-permute-done.12 = bf16[64,3080]{1,0:T(8,128)(2,1)S(1)} collective-permute-done((bf16[64,3080]{1,0:T(8,128)(2,1)S(1)}, bf16[64,3080]{1,0:T(8,128)(2,1)S(1)}, u32[]{:S(2)}, u32[]{:S(2)}) %collective-permute-start.12) | collective-permute-done | bytes 394272 | tf_op jit(solution)/shard_map/ppermute | solution.py:489
  54.8 2.1 collective-permute-done.25
  60.5 5.6 %collective-permute-done.29 = bf16[64,1024]{1,0:T(8,128)(2,1)S(1)} collective-permute-done((bf16[64,1024]{1,0:T(8,128)(2,1)S(1)}, bf16[64,1024]{1,0:T(8,128)(2,1)S(1)}, u32[]{:S(2)}, u32[]{:S(2)}) %collective-permute-start.29) | collective-permute-done | bytes 131104 | tf_op jit(solution)/shard_map/ppermute | solution.py:489
  73.8 4.6 %collective-permute-done.14 = bf16[32,3080]{1,0:T(8,128)(2,1)S(1)} collective-permute-done((bf16[32,3080]{1,0:T(8,128)(2,1)S(1)}, bf16[32,3080]{1,0:T(8,128)(2,1)S(1)}, u32[]{:S(2)}, u32[]{:S(2)}) %collective-permute-start.14) | collective-permute-done | bytes 197152 | tf_op jit(solution)/shard_map/ppermute | solution.py:486
  85.5 2.0 collective-permute-start.31
  88.9 5.0 %fusion.26.query_ref.key_ref.value_ref.gate_ref = f32[256,3080]{1,0:T(8,128)S(1)} fusion(bf16[1024,3080]{1,0:T(8,128)(2,1)} %constant_dynamic-update-slice_fusion.54, bf16[128,1024]{1,0:T(8,128)(2,1)S(1)} %fusion.6, bf16[128,1024]{1,0:T(8,128)(2,1)} %copy-done.31, pred[]{:T(512)S(6)} %eq.121), kind=kOutput, calls=%fused_computation.112 | convolution fusion | flops 1617166336 | bytes 9986049 | tf_op jit(solution)/shard_map/dot_general | solution.py:438
  95.6 12.5 %mixer_forward.1 = (bf16[256,1024]{1,0:T(8,128)(2,1)}, f32[256,1024]{1,0:T(8,128)}, f32[256,1024]{1,0:T(8,128)}, f32[4,2,128,128]{3,2,1,0:T(8,128)}) custom-call(f32[256,3080]{1,0:T(8,128)} %copy-done, f32[256,3080]{1,0:T(8,128)} %copy-done, f32[256,3080]{1,0:T(8,128)} %copy-done, f32[256,3080]{1,0:T(8,128)} %copy-done, f32[256,8]{1,0:T(8,128)} %slice.240.small_ref, ...), custom_call_target="tpu_custom_call" | custom-call | tf_op jit(solution)/shard_map/mixer_forward/pallas_call | solution.py:381
  114.4 1.9 collective-permute-done.33
  118.9 2.5 fusion.50
  125.9 1.8 constant_dynamic-update-slice_fusion.33
  127.7 2.2 collective-permute-done.35
  130.2 4.3 collective-permute-done.42
  137.4 1.8 constant_dynamic-update-slice_fusion.31
  141.2 8.9 %collective-permute-done.48 = bf16[64,2816]{1,0:T(8,128)(2,1)S(1)} collective-permute-done((bf16[64,2816]{1,0:T(8,128)(2,1)S(1)}, bf16[64,2816]{1,0:T(8,128)(2,1)S(1)}, u32[]{:S(2)}, u32[]{:S(2)}) %collective-permute-start.48) | collective-permute-done | bytes 360480 | tf_op jit(solution)/shard_map/ppermute | solution.py:489
  160.4 2.5 collective-permute-done.50
  164.8 3.6 collective-permute-done.52
  172.4 3.0 collective-permute-done.61
  179.6 4.3 fusion.25
  186.8 2.2 collective-permute-done.69
  190.7 2.8 multiply_convert_fusion.1
  198.4 2.2 convolution_convert_fusion.2
  207.0 3.4 collective-permute-done.73
  213.6 2.2 collective-permute-done.134
  220.9 3.2 collective-permute-done.135
  226.3 5.2 %collective-permute-done.74 = bf16[128,1024]{1,0:T(8,128)(2,1)S(1)} collective-permute-done((bf16[128,1024]{1,0:T(8,128)(2,1)S(1)}, bf16[128,1024]{1,0:T(8,128)(2,1)S(1)}, u32[]{:S(2)}, u32[]{:S(2)}) %collective-permute-start.74) | collective-permute-done | bytes 262176 | tf_op jit(solution)/shard_map/ppermute | solution.py:577
  231.6 1.9 collective-permute-start.118
  235.2 15.9 %mixer_backward.1 = (bf16[256,3080]{1,0:T(8,128)(2,1)}, f32[4,512]{1,0:T(4,128)}, f32[4,512]{1,0:T(4,128)}, f32[4,1024]{1,0:T(4,128)}, f32[1,256]{1,0:T(1,128)}, /*index=5*/f32[2,8]{1,0:T(2,128)}) custom-call(f32[256,3080]{1,0:T(8,128)} %copy-done, f32[256,3080]{1,0:T(8,128)} %copy-done, f32[256,3080]{1,0:T(8,128)} %copy-done, f32[256,3080]{1,0:T(8,128)} %copy-done, ...), custom_call_target="tpu_custom_call" | custom-call | tf_op jit(solution)/shard_map/mixer_backward/pallas_call | solution.py:408
  251.1 5.4 %fusion.52 = f32[256,1024]{1,0:T(8,128)S(1)} fusion(bf16[256,3080]{1,0:T(8,128)(2,1)} %get-tuple-element.40, bf16[1024,3080]{1,0:T(8,128)(2,1)} %constant_dynamic-update-slice_fusion.54), kind=kOutput, calls=%fused_computation.256 | convolution fusion | flops 1614807040 | bytes 8933376 | tf_op jit(solution)/shard_map/dot_general | solution.py:446
  256.6 2.0 convolution_convert_fusion
  260.3 2.0 copy-done.1
  262.4 2.0 convolution_convert_fusion.3
  265.3 2.2 constant_dynamic-slice_fusion.23
  273.2 1.8 add_convert_fusion.12
  280.7 2.3 collective-permute-done.102
  286.6 2.2 fusion.11
  293.3 2.0 collective-permute-done.103
  296.9 2.7 collective-permute-done.77
  300.3 2.1 add_convert_fusion.8
  304.7 2.4 collective-permute-done.78
  307.1 2.6 collective-permute-start.79
  310.5 1.8 collective-permute-done.79
  312.3 1.9 collective-permute-start.104
  317.9 1.8 add_convert_fusion.17
  319.8 2.1 collective-permute-done.109
  323.1 4.4 collective-permute-done.143
  344.4 1.9 collective-permute-start.86
  347.3 3.4 collective-permute-done.86
  354.1 2.4 collective-permute-done.144
  365.3 1.9 collective-permute-start.87
  370.0 3.8 collective-permute-done.112
  376.0 1.9 collective-permute-done.87
  380.2 7.2 %collective-permute-done.126 = bf16[64,2816]{1,0:T(8,128)(2,1)S(1)} collective-permute-done((bf16[64,2816]{1,0:T(8,128)(2,1)S(1)}, bf16[64,2816]{1,0:T(8,128)(2,1)S(1)}, u32[]{:S(2)}, u32[]{:S(2)}) %collective-permute-start.126) | collective-permute-done | bytes 360480 | tf_op jit(solution)/shard_map/ppermute | solution.py:489
  387.4 1.8 collective-permute-start.88
  391.0 6.1 %collective-permute-done.88 = bf16[64,3080]{1,0:T(8,128)(2,1)S(1)} collective-permute-done((bf16[64,3080]{1,0:T(8,128)(2,1)S(1)}, bf16[64,3080]{1,0:T(8,128)(2,1)S(1)}, u32[]{:S(2)}, u32[]{:S(2)}) %collective-permute-start.88) | collective-permute-done | bytes 394272 | tf_op jit(solution)/shard_map/ppermute | solution.py:486
  399.8 3.8 collective-permute-done.93
  404.9 8.1 %collective-permute-done.127 = bf16[64,2816]{1,0:T(8,128)(2,1)S(1)} collective-permute-done((bf16[64,2816]{1,0:T(8,128)(2,1)S(1)}, bf16[64,2816]{1,0:T(8,128)(2,1)S(1)}, u32[]{:S(2)}, u32[]{:S(2)}) %collective-permute-start.127) | collective-permute-done | bytes 360480 | tf_op jit(solution)/shard_map/ppermute | solution.py:489
  416.5 7.7 %collective-permute-done.94 = bf16[64,3080]{1,0:T(8,128)(2,1)S(1)} collective-permute-done((bf16[64,3080]{1,0:T(8,128)(2,1)S(1)}, bf16[64,3080]{1,0:T(8,128)(2,1)S(1)}, u32[]{:S(2)}, u32[]{:S(2)}) %collective-permute-start.94) | collective-permute-done | bytes 394272 | tf_op jit(solution)/shard_map/ppermute | solution.py:489
  425.6 2.0 collective-permute-start.89
  428.4 5.0 %collective-permute-done.128 = bf16[64,2816]{1,0:T(8,128)(2,1)S(1)} collective-permute-done((bf16[64,2816]{1,0:T(8,128)(2,1)S(1)}, bf16[64,2816]{1,0:T(8,128)(2,1)S(1)}, u32[]{:S(2)}, u32[]{:S(2)}) %collective-permute-start.128) | collective-permute-done | bytes 360480 | tf_op jit(solution)/shard_map/ppermute | solution.py:489
  434.5 5.8 %collective-permute-done.95 = bf16[64,3080]{1,0:T(8,128)(2,1)S(1)} collective-permute-done((bf16[64,3080]{1,0:T(8,128)(2,1)S(1)}, bf16[64,3080]{1,0:T(8,128)(2,1)S(1)}, u32[]{:S(2)}, u32[]{:S(2)}) %collective-permute-start.95) | collective-permute-done | bytes 394272 | tf_op jit(solution)/shard_map/ppermute | solution.py:489
  442.8 6.9 %collective-permute-done.96 = bf16[64,3080]{1,0:T(8,128)(2,1)S(1)} collective-permute-done((bf16[64,3080]{1,0:T(8,128)(2,1)S(1)}, bf16[64,3080]{1,0:T(8,128)(2,1)S(1)}, u32[]{:S(2)}, u32[]{:S(2)}) %collective-permute-start.96) | collective-permute-done | bytes 394272 | tf_op jit(solution)/shard_map/ppermute | solution.py:489
  (550 shorter events, 207.6 us)
Async XLA Ops:
  3.4 17.1 %collective-permute-start.4 = (bf16[64,3080]{1,0:T(8,128)(2,1)S(1)}, bf16[64,3080]{1,0:T(8,128)(2,1)S(1)}, u32[]{:S(2)}, u32[]{:S(2)}) collective-permute-start(bf16[64,3080]{1,0:T(8,128)(2,1)S(1)} %concatenate.118), channel_id=1, source_target_pairs={{8,0},{10,2},{16,8},{18,10},{24,16},{26,18},{28,24},{30,26},{20,28... | collective-permute-start | bytes 1182728 | tf_op jit(solution)/shard_map/ppermute | solution.py:489
  3.4 15.5 %collective-permute-start.2 = (bf16[64,3080]{1,0:T(8,128)(2,1)S(1)}, bf16[64,3080]{1,0:T(8,128)(2,1)S(1)}, u32[]{:S(2)}, u32[]{:S(2)}) collective-permute-start(bf16[64,3080]{1,0:T(8,128)(2,1)S(1)} %concatenate.118), channel_id=1, source_target_pairs={{0,8},{2,10},{8,16},{10,18},{16,24},{18,26},{24,28},{26,30},{28,20... | collective-permute-start | bytes 1182728 | tf_op jit(solution)/shard_map/ppermute | solution.py:486
  5.4 15.1 %collective-permute-start.1 = (bf16[64,3080]{1,0:T(8,128)(2,1)S(1)}, bf16[64,3080]{1,0:T(8,128)(2,1)S(1)}, u32[]{:S(2)}, u32[]{:S(2)}) collective-permute-start(bf16[64,3080]{1,0:T(8,128)(2,1)S(1)} %concatenate.118), channel_id=1, source_target_pairs={{0,2},{2,0},{4,6},{6,4},{8,10},{10,8},{12,14},{14,12},{16,18},{18,... | collective-permute-start | bytes 1182728 | tf_op jit(solution)/shard_map/ppermute | solution.py:492
  7.9 182.8 %collective-permute-start.72 = (bf16[128,1024]{1,0:T(8,128)(2,1)}, bf16[128,1024]{1,0:T(8,128)(2,1)}, u32[]{:S(2)}, u32[]{:S(2)}) collective-permute-start(bf16[128,1024]{1,0:T(8,128)(2,1)} %fusion.14), channel_id=1, source_target_pairs={{0,1},{1,0},{2,3},{3,2},{4,5},{5,4},{6,7},{7,6},{8,9},{9,8},{10,11... | collective-permute-start | bytes 786440 | tf_op jit(solution)/shard_map/ppermute | solution.py:577
  11.6 76.6 %collective-permute-start = (bf16[128,1024]{1,0:T(8,128)(2,1)S(1)}, bf16[128,1024]{1,0:T(8,128)(2,1)S(1)}, u32[]{:S(2)}, u32[]{:S(2)}) collective-permute-start(bf16[128,1024]{1,0:T(8,128)(2,1)S(1)} %fusion.6), channel_id=1, source_target_pairs={{0,1},{1,0},{2,3},{3,2},{4,5},{5,4},{6,7},{7,6},{8,9},{9,8},{10,11... | collective-permute-start | bytes 786440 | tf_op jit(solution)/shard_map/ppermute | solution.py:577
  18.9 11.3 %collective-permute-start.6 = (bf16[64,3080]{1,0:T(8,128)(2,1)S(1)}, bf16[64,3080]{1,0:T(8,128)(2,1)S(1)}, u32[]{:S(2)}, u32[]{:S(2)}) collective-permute-start(bf16[64,3080]{1,0:T(8,128)(2,1)S(1)} %collective-permute-done.2), channel_id=1, source_target_pairs={{0,8},{2,10},{8,16},{10,18},{16,24},{18,26},{24,28},{26,30},{28,20... | collective-permute-start | bytes 1182728 | tf_op jit(solution)/shard_map/ppermute | solution.py:486
  20.5 9.8 %collective-permute-start.3 = (bf16[64,3080]{1,0:T(8,128)(2,1)S(1)}, bf16[64,3080]{1,0:T(8,128)(2,1)S(1)}, u32[]{:S(2)}, u32[]{:S(2)}) collective-permute-start(bf16[64,3080]{1,0:T(8,128)(2,1)S(1)} %collective-permute-done.2), channel_id=1, source_target_pairs={{0,2},{2,0},{4,6},{6,4},{8,10},{10,8},{12,14},{14,12},{16,18},{18,... | collective-permute-start | bytes 1182728 | tf_op jit(solution)/shard_map/ppermute | solution.py:492
  20.5 12.9 %collective-permute-start.8 = (bf16[64,3080]{1,0:T(8,128)(2,1)S(1)}, bf16[64,3080]{1,0:T(8,128)(2,1)S(1)}, u32[]{:S(2)}, u32[]{:S(2)}) collective-permute-start(bf16[64,3080]{1,0:T(8,128)(2,1)S(1)} %collective-permute-done.4), channel_id=1, source_target_pairs={{8,0},{10,2},{16,8},{18,10},{24,16},{26,18},{28,24},{30,26},{20,28... | collective-permute-start | bytes 1182728 | tf_op jit(solution)/shard_map/ppermute | solution.py:489
  30.2 15.0 %collective-permute-start.10 = (bf16[64,3080]{1,0:T(8,128)(2,1)S(1)}, bf16[64,3080]{1,0:T(8,128)(2,1)S(1)}, u32[]{:S(2)}, u32[]{:S(2)}) collective-permute-start(bf16[64,3080]{1,0:T(8,128)(2,1)S(1)} %collective-permute-done.6), channel_id=1, source_target_pairs={{0,8},{2,10},{8,16},{10,18},{16,24},{18,26},{24,28},{26,30},{28,20... | collective-permute-start | bytes 1182728 | tf_op jit(solution)/shard_map/ppermute | solution.py:486
  33.4 12.4 %collective-permute-start.7 = (bf16[64,3080]{1,0:T(8,128)(2,1)S(1)}, bf16[64,3080]{1,0:T(8,128)(2,1)S(1)}, u32[]{:S(2)}, u32[]{:S(2)}) collective-permute-start(bf16[64,3080]{1,0:T(8,128)(2,1)S(1)} %collective-permute-done.6), channel_id=1, source_target_pairs={{0,2},{2,0},{4,6},{6,4},{8,10},{10,8},{12,14},{14,12},{16,18},{18,... | collective-permute-start | bytes 1182728 | tf_op jit(solution)/shard_map/ppermute | solution.py:492
  33.6 11.7 %collective-permute-start.12 = (bf16[64,3080]{1,0:T(8,128)(2,1)S(1)}, bf16[64,3080]{1,0:T(8,128)(2,1)S(1)}, u32[]{:S(2)}, u32[]{:S(2)}) collective-permute-start(bf16[64,3080]{1,0:T(8,128)(2,1)S(1)} %collective-permute-done.8), channel_id=1, source_target_pairs={{8,0},{10,2},{16,8},{18,10},{24,16},{26,18},{28,24},{30,26},{20,28... | collective-permute-start | bytes 1182728 | tf_op jit(solution)/shard_map/ppermute | solution.py:489
  56.9 16.4 %collective-permute-start.16 = (bf16[32,3080]{1,0:T(8,128)(2,1)S(1)}, bf16[32,3080]{1,0:T(8,128)(2,1)S(1)}, u32[]{:S(2)}, u32[]{:S(2)}) collective-permute-start(bf16[32,3080]{1,0:T(8,128)(2,1)S(1)} %slice.239), channel_id=1, source_target_pairs={{8,0},{10,2},{16,8},{18,10},{24,16},{26,18},{28,24},{30,26},{20,28... | collective-permute-start | bytes 591368 | tf_op jit(solution)/shard_map/ppermute | solution.py:489
  66.2 12.2 %collective-permute-start.11 = (bf16[64,3080]{1,0:T(8,128)(2,1)S(1)}, bf16[64,3080]{1,0:T(8,128)(2,1)S(1)}, u32[]{:S(2)}, u32[]{:S(2)}) collective-permute-start(bf16[64,3080]{1,0:T(8,128)(2,1)S(1)} %collective-permute-done.10), channel_id=1, source_target_pairs={{0,2},{2,0},{4,6},{6,4},{8,10},{10,8},{12,14},{14,12},{16,18},{18,... | collective-permute-start | bytes 1182728 | tf_op jit(solution)/shard_map/ppermute | solution.py:492
  80.5 42.5 %collective-permute-start.40 = (bf16[64,2816]{1,0:T(8,128)(2,1)}, bf16[64,2816]{1,0:T(8,128)(2,1)}, u32[]{:S(2)}, u32[]{:S(2)}) collective-permute-start(bf16[64,2816]{1,0:T(8,128)(2,1)} %pad_maximum_fusion.5), channel_id=1, source_target_pairs={{8,0},{10,2},{16,8},{18,10},{24,16},{26,18},{28,24},{30,26},{20,28... | collective-permute-start | bytes 1081352 | tf_op jit(solution)/shard_map/ppermute | solution.py:489
  82.5 41.0 %collective-permute-start.38 = (bf16[64,2816]{1,0:T(8,128)(2,1)}, bf16[64,2816]{1,0:T(8,128)(2,1)}, u32[]{:S(2)}, u32[]{:S(2)}) collective-permute-start(bf16[64,2816]{1,0:T(8,128)(2,1)} %pad_maximum_fusion.5), channel_id=1, source_target_pairs={{0,8},{2,10},{8,16},{10,18},{16,24},{18,26},{24,28},{26,30},{28,20... | collective-permute-start | bytes 1081352 | tf_op jit(solution)/shard_map/ppermute | solution.py:486
  85.5 26.3 %collective-permute-start.31 = (bf16[32,1024]{1,0:T(8,128)(2,1)}, bf16[32,1024]{1,0:T(8,128)(2,1)}, u32[]{:S(2)}, u32[]{:S(2)}) collective-permute-start(bf16[32,1024]{1,0:T(8,128)(2,1)} %slice.241), channel_id=1, source_target_pairs={{0,8},{2,10},{8,16},{10,18},{16,24},{18,26},{24,28},{26,30},{28,20... | collective-permute-start | bytes 196616 | tf_op jit(solution)/shard_map/ppermute | solution.py:486
  88.9 19.2 %collective-permute-start.28 = (bf16[64,1024]{1,0:T(8,128)(2,1)}, bf16[64,1024]{1,0:T(8,128)(2,1)}, u32[]{:S(2)}, u32[]{:S(2)}) collective-permute-start(bf16[64,1024]{1,0:T(8,128)(2,1)} %collective-permute-done.27), channel_id=1, source_target_pairs={{0,2},{2,0},{4,6},{6,4},{8,10},{10,8},{12,14},{14,12},{16,18},{18,... | collective-permute-start | bytes 393224 | tf_op jit(solution)/shard_map/ppermute | solution.py:492
  123.0 16.2 %collective-permute-start.44 = (bf16[64,2816]{1,0:T(8,128)(2,1)}, bf16[64,2816]{1,0:T(8,128)(2,1)S(1)}, u32[]{:S(2)}, u32[]{:S(2)}) collective-permute-start(bf16[64,2816]{1,0:T(8,128)(2,1)} %collective-permute-done.40), channel_id=1, source_target_pairs={{8,0},{10,2},{16,8},{18,10},{24,16},{26,18},{28,24},{30,26},{20,28... | collective-permute-start | bytes 1081352 | tf_op jit(solution)/shard_map/ppermute | solution.py:489
  123.5 15.7 %collective-permute-start.41 = (bf16[64,2816]{1,0:T(8,128)(2,1)}, bf16[64,2816]{1,0:T(8,128)(2,1)S(1)}, u32[]{:S(2)}, u32[]{:S(2)}) collective-permute-start(bf16[64,2816]{1,0:T(8,128)(2,1)} %collective-permute-done.40), channel_id=1, source_target_pairs={{0,2},{2,0},{4,6},{6,4},{8,10},{10,8},{12,14},{14,12},{16,18},{18,... | collective-permute-start | bytes 1081352 | tf_op jit(solution)/shard_map/ppermute | solution.py:492
  123.5 11.0 %collective-permute-start.42 = (bf16[64,2816]{1,0:T(8,128)(2,1)}, bf16[64,2816]{1,0:T(8,128)(2,1)S(1)}, u32[]{:S(2)}, u32[]{:S(2)}) collective-permute-start(bf16[64,2816]{1,0:T(8,128)(2,1)} %collective-permute-done.38), channel_id=1, source_target_pairs={{0,8},{2,10},{8,16},{10,18},{16,24},{18,26},{24,28},{26,30},{28,20... | collective-permute-start | bytes 1081352 | tf_op jit(solution)/shard_map/ppermute | solution.py:486
  134.5 45.0 %collective-permute-start.36 = (bf16[128,1024]{1,0:T(8,128)(2,1)S(1)}, bf16[128,1024]{1,0:T(8,128)(2,1)S(1)}, u32[]{:S(2)}, u32[]{:S(2)}) collective-permute-start(bf16[128,1024]{1,0:T(8,128)(2,1)S(1)} %multiply_convert_fusion.4), channel_id=1, source_target_pairs={{0,1},{1,0},{2,3},{3,2},{4,5},{5,4},{6,7},{7,6},{8,9},{9,8},{10,11... | collective-permute-start | bytes 786440 | tf_op jit(solution)/shard_map/ppermute | solution.py:577
  135.1 15.0 %collective-permute-start.46 = (bf16[64,2816]{1,0:T(8,128)(2,1)S(1)}, bf16[64,2816]{1,0:T(8,128)(2,1)S(1)}, u32[]{:S(2)}, u32[]{:S(2)}) collective-permute-start(bf16[64,2816]{1,0:T(8,128)(2,1)S(1)} %collective-permute-done.42), channel_id=1, source_target_pairs={{0,8},{2,10},{8,16},{10,18},{16,24},{18,26},{24,28},{26,30},{28,20... | collective-permute-start | bytes 1081352 | tf_op jit(solution)/shard_map/ppermute | solution.py:486
  139.2 11.3 %collective-permute-start.43 = (bf16[64,2816]{1,0:T(8,128)(2,1)S(1)}, bf16[64,2816]{1,0:T(8,128)(2,1)S(1)}, u32[]{:S(2)}, u32[]{:S(2)}) collective-permute-start(bf16[64,2816]{1,0:T(8,128)(2,1)S(1)} %collective-permute-done.42), channel_id=1, source_target_pairs={{0,2},{2,0},{4,6},{6,4},{8,10},{10,8},{12,14},{14,12},{16,18},{18,... | collective-permute-start | bytes 1081352 | tf_op jit(solution)/shard_map/ppermute | solution.py:492
  139.2 10.8 %collective-permute-start.48 = (bf16[64,2816]{1,0:T(8,128)(2,1)S(1)}, bf16[64,2816]{1,0:T(8,128)(2,1)S(1)}, u32[]{:S(2)}, u32[]{:S(2)}) collective-permute-start(bf16[64,2816]{1,0:T(8,128)(2,1)S(1)} %collective-permute-done.44), channel_id=1, source_target_pairs={{8,0},{10,2},{16,8},{18,10},{24,16},{26,18},{28,24},{30,26},{20,28... | collective-permute-start | bytes 1081352 | tf_op jit(solution)/shard_map/ppermute | solution.py:489
  150.1 18.3 %collective-permute-start.57 = (bf16[64,1408]{1,0:T(8,128)(2,1)S(1)}, bf16[64,1408]{1,0:T(8,128)(2,1)S(1)}, u32[]{:S(2)}, u32[]{:S(2)}) collective-permute-start(bf16[64,1408]{1,0:T(8,128)(2,1)S(1)} %copy-done.34), channel_id=1, source_target_pairs={{8,0},{10,2},{16,8},{18,10},{24,16},{26,18},{28,24},{30,26},{20,28... | collective-permute-start | bytes 540680 | tf_op jit(solution)/shard_map/ppermute | solution.py:489
  176.6 9.6 %collective-permute-start.62 = (bf16[64,1408]{1,0:T(8,128)(2,1)S(1)}, bf16[64,1408]{1,0:T(8,128)(2,1)S(1)}, u32[]{:S(2)}, u32[]{:S(2)}) collective-permute-start(bf16[64,1408]{1,0:T(8,128)(2,1)S(1)} %collective-permute-done.61), channel_id=1, source_target_pairs={{0,2},{2,0},{4,6},{6,4},{8,10},{10,8},{12,14},{14,12},{16,18},{18,... | collective-permute-start | bytes 540680 | tf_op jit(solution)/shard_map/ppermute | solution.py:492
  196.3 14.5 %collective-permute-start.71 = (bf16[128,1024]{1,0:T(8,128)(2,1)S(1)}, bf16[128,1024]{1,0:T(8,128)(2,1)S(1)}, u32[]{:S(2)}, u32[]{:S(2)}) collective-permute-start(bf16[128,1024]{1,0:T(8,128)(2,1)S(1)} %dynamic-slice_convert_fusion.2), channel_id=1, source_target_pairs={{0,1},{1,0},{2,3},{3,2},{4,5},{5,4},{6,7},{7,6},{8,9},{9,8},{10,11... | collective-permute-start | bytes 786440 | tf_op jit(solution)/shard_map/ppermute | solution.py:604
  197.8 12.6 %collective-permute-start.73 = (bf16[128,1024]{1,0:T(8,128)(2,1)S(1)}, bf16[128,1024]{1,0:T(8,128)(2,1)S(1)}, u32[]{:S(2)}, u32[]{:S(2)}) collective-permute-start(bf16[128,1024]{1,0:T(8,128)(2,1)S(1)} %dynamic-slice_convert_fusion.1), channel_id=1, source_target_pairs={{0,1},{1,0},{2,3},{3,2},{4,5},{5,4},{6,7},{7,6},{8,9},{9,8},{10,11... | collective-permute-start | bytes 786440 | tf_op jit(solution)/shard_map/ppermute | solution.py:604
  201.6 69.3 %collective-permute-start.140 = (bf16[64,1408]{1,0:T(8,128)(2,1)}, bf16[64,1408]{1,0:T(8,128)(2,1)}, u32[]{:S(2)}, u32[]{:S(2)}) collective-permute-start(bf16[64,1408]{1,0:T(8,128)(2,1)} %get-tuple-element.141), channel_id=1, source_target_pairs={{0,2},{2,0},{4,6},{6,4},{8,10},{10,8},{12,14},{14,12},{16,18},{18,... | collective-permute-start | bytes 540680 | tf_op jit(solution)/shard_map/ppermute | solution.py:492
  205.4 83.5 %collective-permute-start.139 = (bf16[64,1408]{1,0:T(8,128)(2,1)}, bf16[64,1408]{1,0:T(8,128)(2,1)}, u32[]{:S(2)}, u32[]{:S(2)}) collective-permute-start(bf16[64,1408]{1,0:T(8,128)(2,1)} %get-tuple-element.142), channel_id=1, source_target_pairs={{0,2},{2,0},{4,6},{6,4},{8,10},{10,8},{12,14},{14,12},{16,18},{18,... | collective-permute-start | bytes 540680 | tf_op jit(solution)/shard_map/ppermute | solution.py:492
  205.9 15.0 %collective-permute-start.131 = (bf16[64,1408]{1,0:T(8,128)(2,1)S(1)}, bf16[64,1408]{1,0:T(8,128)(2,1)S(1)}, u32[]{:S(2)}, u32[]{:S(2)}) collective-permute-start(bf16[64,1408]{1,0:T(8,128)(2,1)S(1)} %get-tuple-element.146), channel_id=1, source_target_pairs={{0,2},{2,0},{4,6},{6,4},{8,10},{10,8},{12,14},{14,12},{16,18},{18,... | collective-permute-start | bytes 540680 | tf_op jit(solution)/shard_map/ppermute | solution.py:492
  215.9 55.5 %collective-permute-start.130 = (bf16[64,1408]{1,0:T(8,128)(2,1)}, bf16[64,1408]{1,0:T(8,128)(2,1)}, u32[]{:S(2)}, u32[]{:S(2)}) collective-permute-start(bf16[64,1408]{1,0:T(8,128)(2,1)} %get-tuple-element.147), channel_id=1, source_target_pairs={{0,2},{2,0},{4,6},{6,4},{8,10},{10,8},{12,14},{14,12},{16,18},{18,... | collective-permute-start | bytes 540680 | tf_op jit(solution)/shard_map/ppermute | solution.py:492
  220.9 78.7 %collective-permute-start.115 = (bf16[64,2816]{1,0:T(8,128)(2,1)}, bf16[64,2816]{1,0:T(8,128)(2,1)}, u32[]{:S(2)}, u32[]{:S(2)}) collective-permute-start(bf16[64,2816]{1,0:T(8,128)(2,1)} %get-tuple-element.132), channel_id=1, source_target_pairs={{0,2},{2,0},{4,6},{6,4},{8,10},{10,8},{12,14},{14,12},{16,18},{18,... | collective-permute-start | bytes 1081352 | tf_op jit(solution)/shard_map/ppermute | solution.py:492
  231.6 35.9 %collective-permute-start.118 = (bf16[32,2816]{1,0:T(8,128)(2,1)}, bf16[32,2816]{1,0:T(8,128)(2,1)}, u32[]{:S(2)}, u32[]{:S(2)}) collective-permute-start(bf16[32,2816]{1,0:T(8,128)(2,1)} %get-tuple-element.176), channel_id=1, source_target_pairs={{0,8},{2,10},{8,16},{10,18},{16,24},{18,26},{24,28},{26,30},{28,20... | collective-permute-start | bytes 540680 | tf_op jit(solution)/shard_map/ppermute | solution.py:486
  271.4 13.5 %collective-permute-start.75 = (bf16[128,1024]{1,0:T(8,128)(2,1)S(1)}, bf16[128,1024]{1,0:T(8,128)(2,1)S(1)}, u32[]{:S(2)}, u32[]{:S(2)}) collective-permute-start(bf16[128,1024]{1,0:T(8,128)(2,1)S(1)} %copy-done.30), channel_id=1, source_target_pairs={{0,1},{1,0},{2,3},{3,2},{4,5},{5,4},{6,7},{7,6},{8,9},{9,8},{10,11... | collective-permute-start | bytes 786440 | tf_op jit(solution)/shard_map/ppermute | solution.py:604
  275.6 17.6 %collective-permute-start.99 = (bf16[64,1024]{1,0:T(8,128)(2,1)}, bf16[64,1024]{1,0:T(8,128)(2,1)}, u32[]{:S(2)}, u32[]{:S(2)}) collective-permute-start(bf16[64,1024]{1,0:T(8,128)(2,1)} %get-tuple-element.159), channel_id=1, source_target_pairs={{0,2},{2,0},{4,6},{6,4},{8,10},{10,8},{12,14},{14,12},{16,18},{18,... | collective-permute-start | bytes 393224 | tf_op jit(solution)/shard_map/ppermute | solution.py:492
  282.9 17.2 %collective-permute-start.119 = (bf16[64,2816]{1,0:T(8,128)(2,1)}, bf16[64,2816]{1,0:T(8,128)(2,1)}, u32[]{:S(2)}, u32[]{:S(2)}) collective-permute-start(bf16[64,2816]{1,0:T(8,128)(2,1)} %pad_maximum_fusion.6), channel_id=1, source_target_pairs={{0,8},{2,10},{8,16},{10,18},{16,24},{18,26},{24,28},{26,30},{28,20... | collective-permute-start | bytes 1081352 | tf_op jit(solution)/shard_map/ppermute | solution.py:486
  292.7 59.6 %collective-permute-start.129 = (bf16[64,1408]{1,0:T(8,128)(2,1)}, bf16[64,1408]{1,0:T(8,128)(2,1)}, u32[]{:S(2)}, u32[]{:S(2)}) collective-permute-start(bf16[64,1408]{1,0:T(8,128)(2,1)} %get-tuple-element.140), channel_id=1, source_target_pairs={{0,2},{2,0},{4,6},{6,4},{8,10},{10,8},{12,14},{14,12},{16,18},{18,... | collective-permute-start | bytes 540680 | tf_op jit(solution)/shard_map/ppermute | solution.py:492
  293.2 29.9 %collective-permute-start.138 = (bf16[64,1408]{1,0:T(8,128)(2,1)}, bf16[64,1408]{1,0:T(8,128)(2,1)}, u32[]{:S(2)}, u32[]{:S(2)}) collective-permute-start(bf16[64,1408]{1,0:T(8,128)(2,1)} %get-tuple-element.143), channel_id=1, source_target_pairs={{0,2},{2,0},{4,6},{6,4},{8,10},{10,8},{12,14},{14,12},{16,18},{18,... | collective-permute-start | bytes 540680 | tf_op jit(solution)/shard_map/ppermute | solution.py:492
  299.6 17.1 %collective-permute-start.108 = (bf16[64,1024]{1,0:T(8,128)(2,1)}, bf16[64,1024]{1,0:T(8,128)(2,1)S(1)}, u32[]{:S(2)}, u32[]{:S(2)}) collective-permute-start(bf16[64,1024]{1,0:T(8,128)(2,1)} %get-tuple-element.154), channel_id=1, source_target_pairs={{0,2},{2,0},{4,6},{6,4},{8,10},{10,8},{12,14},{14,12},{16,18},{18,... | collective-permute-start | bytes 393224 | tf_op jit(solution)/shard_map/ppermute | solution.py:492
  302.4 14.3 %collective-permute-start.98 = (bf16[64,1024]{1,0:T(8,128)(2,1)}, bf16[64,1024]{1,0:T(8,128)(2,1)}, u32[]{:S(2)}, u32[]{:S(2)}) collective-permute-start(bf16[64,1024]{1,0:T(8,128)(2,1)} %get-tuple-element.160), channel_id=1, source_target_pairs={{0,2},{2,0},{4,6},{6,4},{8,10},{10,8},{12,14},{14,12},{16,18},{18,... | collective-permute-start | bytes 393224 | tf_op jit(solution)/shard_map/ppermute | solution.py:492
  316.7 46.4 %collective-permute-start.124 = (bf16[64,2816]{1,0:T(8,128)(2,1)}, bf16[64,2816]{1,0:T(8,128)(2,1)}, u32[]{:S(2)}, u32[]{:S(2)}) collective-permute-start(bf16[64,2816]{1,0:T(8,128)(2,1)} %get-tuple-element.127), channel_id=1, source_target_pairs={{0,2},{2,0},{4,6},{6,4},{8,10},{10,8},{12,14},{14,12},{16,18},{18,... | collective-permute-start | bytes 1081352 | tf_op jit(solution)/shard_map/ppermute | solution.py:492
  316.7 46.9 %collective-permute-start.114 = (bf16[64,2816]{1,0:T(8,128)(2,1)}, bf16[64,2816]{1,0:T(8,128)(2,1)}, u32[]{:S(2)}, u32[]{:S(2)}) collective-permute-start(bf16[64,2816]{1,0:T(8,128)(2,1)} %get-tuple-element.133), channel_id=1, source_target_pairs={{0,2},{2,0},{4,6},{6,4},{8,10},{10,8},{12,14},{14,12},{16,18},{18,... | collective-permute-start | bytes 1081352 | tf_op jit(solution)/shard_map/ppermute | solution.py:492
  323.1 19.8 %collective-permute-start.107 = (bf16[64,1024]{1,0:T(8,128)(2,1)}, bf16[64,1024]{1,0:T(8,128)(2,1)}, u32[]{:S(2)}, u32[]{:S(2)}) collective-permute-start(bf16[64,1024]{1,0:T(8,128)(2,1)} %get-tuple-element.155), channel_id=1, source_target_pairs={{0,2},{2,0},{4,6},{6,4},{8,10},{10,8},{12,14},{14,12},{16,18},{18,... | collective-permute-start | bytes 393224 | tf_op jit(solution)/shard_map/ppermute | solution.py:492
  332.1 12.2 %collective-permute-start.110 = (bf16[64,1024]{1,0:T(8,128)(2,1)}, bf16[64,1024]{1,0:T(8,128)(2,1)}, u32[]{:S(2)}, u32[]{:S(2)}) collective-permute-start(bf16[64,1024]{1,0:T(8,128)(2,1)} %pad_maximum_fusion.11), channel_id=1, source_target_pairs={{8,0},{10,2},{16,8},{18,10},{24,16},{26,18},{28,24},{30,26},{20,28... | collective-permute-start | bytes 393224 | tf_op jit(solution)/shard_map/ppermute | solution.py:489
  342.9 9.5 %collective-permute-start.137 = (bf16[64,1408]{1,0:T(8,128)(2,1)}, bf16[64,1408]{1,0:T(8,128)(2,1)S(1)}, u32[]{:S(2)}, u32[]{:S(2)}) collective-permute-start(bf16[64,1408]{1,0:T(8,128)(2,1)} %get-tuple-element.148), channel_id=1, source_target_pairs={{0,8},{2,10},{8,16},{10,18},{16,24},{18,26},{24,28},{26,30},{28,20... | collective-permute-start | bytes 540680 | tf_op jit(solution)/shard_map/ppermute | solution.py:486
  352.3 13.0 %collective-permute-start.120 = (bf16[64,2816]{1,0:T(8,128)(2,1)}, bf16[64,2816]{1,0:T(8,128)(2,1)S(1)}, u32[]{:S(2)}, u32[]{:S(2)}) collective-permute-start(bf16[64,2816]{1,0:T(8,128)(2,1)} %add_convert_fusion.8), channel_id=1, source_target_pairs={{0,8},{2,10},{8,16},{10,18},{16,24},{18,26},{24,28},{26,30},{28,20... | collective-permute-start | bytes 1081352 | tf_op jit(solution)/shard_map/ppermute | solution.py:486
  358.6 10.2 %collective-permute-start.125 = (bf16[32,2816]{1,0:T(8,128)(2,1)S(1)}, bf16[32,2816]{1,0:T(8,128)(2,1)S(1)}, u32[]{:S(2)}, u32[]{:S(2)}) collective-permute-start(bf16[32,2816]{1,0:T(8,128)(2,1)S(1)} %copy-done.37), channel_id=1, source_target_pairs={{8,0},{10,2},{16,8},{18,10},{24,16},{26,18},{28,24},{30,26},{20,28... | collective-permute-start | bytes 540680 | tf_op jit(solution)/shard_map/ppermute | solution.py:489
  363.1 12.4 %collective-permute-start.83 = (bf16[64,3080]{1,0:T(8,128)(2,1)S(1)}, bf16[64,3080]{1,0:T(8,128)(2,1)S(1)}, u32[]{:S(2)}, u32[]{:S(2)}) collective-permute-start(bf16[64,3080]{1,0:T(8,128)(2,1)S(1)} %copy-done.20), channel_id=1, source_target_pairs={{0,2},{2,0},{4,6},{6,4},{8,10},{10,8},{12,14},{14,12},{16,18},{18,... | collective-permute-start | bytes 1182728 | tf_op jit(solution)/shard_map/ppermute | solution.py:492
  365.3 12.6 %collective-permute-start.87 = (bf16[64,3080]{1,0:T(8,128)(2,1)S(1)}, bf16[64,3080]{1,0:T(8,128)(2,1)S(1)}, u32[]{:S(2)}, u32[]{:S(2)}) collective-permute-start(bf16[64,3080]{1,0:T(8,128)(2,1)S(1)} %pad_maximum_fusion.3), channel_id=1, source_target_pairs={{0,8},{2,10},{8,16},{10,18},{16,24},{18,26},{24,28},{26,30},{28,20... | collective-permute-start | bytes 1182728 | tf_op jit(solution)/shard_map/ppermute | solution.py:486
  369.1 56.5 %collective-permute-start.113 = (bf16[64,2816]{1,0:T(8,128)(2,1)S(1)}, bf16[64,2816]{1,0:T(8,128)(2,1)S(1)}, u32[]{:S(2)}, u32[]{:S(2)}) collective-permute-start(bf16[64,2816]{1,0:T(8,128)(2,1)S(1)} %copy-done.24), channel_id=1, source_target_pairs={{0,2},{2,0},{4,6},{6,4},{8,10},{10,8},{12,14},{14,12},{16,18},{18,... | collective-permute-start | bytes 1081352 | tf_op jit(solution)/shard_map/ppermute | solution.py:492
  370.0 10.1 %collective-permute-start.123 = (bf16[64,2816]{1,0:T(8,128)(2,1)S(1)}, bf16[64,2816]{1,0:T(8,128)(2,1)S(1)}, u32[]{:S(2)}, u32[]{:S(2)}) collective-permute-start(bf16[64,2816]{1,0:T(8,128)(2,1)S(1)} %copy-done.26), channel_id=1, source_target_pairs={{0,2},{2,0},{4,6},{6,4},{8,10},{10,8},{12,14},{14,12},{16,18},{18,... | collective-permute-start | bytes 1081352 | tf_op jit(solution)/shard_map/ppermute | solution.py:492
  373.8 30.9 %collective-permute-start.122 = (bf16[64,2816]{1,0:T(8,128)(2,1)S(1)}, bf16[64,2816]{1,0:T(8,128)(2,1)S(1)}, u32[]{:S(2)}, u32[]{:S(2)}) collective-permute-start(bf16[64,2816]{1,0:T(8,128)(2,1)S(1)} %copy-done.25), channel_id=1, source_target_pairs={{0,2},{2,0},{4,6},{6,4},{8,10},{10,8},{12,14},{14,12},{16,18},{18,... | collective-permute-start | bytes 1081352 | tf_op jit(solution)/shard_map/ppermute | solution.py:492
  375.5 14.9 %collective-permute-start.92 = (bf16[64,3080]{1,0:T(8,128)(2,1)S(1)}, bf16[64,3080]{1,0:T(8,128)(2,1)S(1)}, u32[]{:S(2)}, u32[]{:S(2)}) collective-permute-start(bf16[64,3080]{1,0:T(8,128)(2,1)S(1)} %copy-done.19), channel_id=1, source_target_pairs={{0,2},{2,0},{4,6},{6,4},{8,10},{10,8},{12,14},{14,12},{16,18},{18,... | collective-permute-start | bytes 1182728 | tf_op jit(solution)/shard_map/ppermute | solution.py:492
  377.9 9.5 %collective-permute-start.126 = (bf16[64,2816]{1,0:T(8,128)(2,1)S(1)}, bf16[64,2816]{1,0:T(8,128)(2,1)S(1)}, u32[]{:S(2)}, u32[]{:S(2)}) collective-permute-start(bf16[64,2816]{1,0:T(8,128)(2,1)S(1)} %pad_maximum_fusion.7), channel_id=1, source_target_pairs={{8,0},{10,2},{16,8},{18,10},{24,16},{26,18},{28,24},{30,26},{20,28... | collective-permute-start | bytes 1081352 | tf_op jit(solution)/shard_map/ppermute | solution.py:489
  380.2 10.3 %collective-permute-start.82 = (bf16[64,3080]{1,0:T(8,128)(2,1)S(1)}, bf16[64,3080]{1,0:T(8,128)(2,1)S(1)}, u32[]{:S(2)}, u32[]{:S(2)}) collective-permute-start(bf16[64,3080]{1,0:T(8,128)(2,1)S(1)} %copy-done.18), channel_id=1, source_target_pairs={{0,2},{2,0},{4,6},{6,4},{8,10},{10,8},{12,14},{14,12},{16,18},{18,... | collective-permute-start | bytes 1182728 | tf_op jit(solution)/shard_map/ppermute | solution.py:492
  387.4 9.7 %collective-permute-start.88 = (bf16[64,3080]{1,0:T(8,128)(2,1)S(1)}, bf16[64,3080]{1,0:T(8,128)(2,1)S(1)}, u32[]{:S(2)}, u32[]{:S(2)}) collective-permute-start(bf16[64,3080]{1,0:T(8,128)(2,1)S(1)} %add_convert_fusion.3), channel_id=1, source_target_pairs={{0,8},{2,10},{8,16},{10,18},{16,24},{18,26},{24,28},{26,30},{28,20... | collective-permute-start | bytes 1182728 | tf_op jit(solution)/shard_map/ppermute | solution.py:486
  390.4 52.4 %collective-permute-start.81 = (bf16[64,3080]{1,0:T(8,128)(2,1)S(1)}, bf16[64,3080]{1,0:T(8,128)(2,1)S(1)}, u32[]{:S(2)}, u32[]{:S(2)}) collective-permute-start(bf16[64,3080]{1,0:T(8,128)(2,1)S(1)} %copy-done.15), channel_id=1, source_target_pairs={{0,2},{2,0},{4,6},{6,4},{8,10},{10,8},{12,14},{14,12},{16,18},{18,... | collective-permute-start | bytes 1182728 | tf_op jit(solution)/shard_map/ppermute | solution.py:492
  390.5 24.4 %collective-permute-start.91 = (bf16[64,3080]{1,0:T(8,128)(2,1)S(1)}, bf16[64,3080]{1,0:T(8,128)(2,1)S(1)}, u32[]{:S(2)}, u32[]{:S(2)}) collective-permute-start(bf16[64,3080]{1,0:T(8,128)(2,1)S(1)} %copy-done.17), channel_id=1, source_target_pairs={{0,2},{2,0},{4,6},{6,4},{8,10},{10,8},{12,14},{14,12},{16,18},{18,... | collective-permute-start | bytes 1182728 | tf_op jit(solution)/shard_map/ppermute | solution.py:492
  404.8 29.7 %collective-permute-start.90 = (bf16[64,3080]{1,0:T(8,128)(2,1)S(1)}, bf16[64,3080]{1,0:T(8,128)(2,1)S(1)}, u32[]{:S(2)}, u32[]{:S(2)}) collective-permute-start(bf16[64,3080]{1,0:T(8,128)(2,1)S(1)} %copy-done.16), channel_id=1, source_target_pairs={{0,2},{2,0},{4,6},{6,4},{8,10},{10,8},{12,14},{14,12},{16,18},{18,... | collective-permute-start | bytes 1182728 | tf_op jit(solution)/shard_map/ppermute | solution.py:492
  413.0 11.2 %collective-permute-start.94 = (bf16[64,3080]{1,0:T(8,128)(2,1)S(1)}, bf16[64,3080]{1,0:T(8,128)(2,1)S(1)}, u32[]{:S(2)}, u32[]{:S(2)}) collective-permute-start(bf16[64,3080]{1,0:T(8,128)(2,1)S(1)} %pad_maximum_fusion.4), channel_id=1, source_target_pairs={{8,0},{10,2},{16,8},{18,10},{24,16},{26,18},{28,24},{30,26},{20,28... | collective-permute-start | bytes 1182728 | tf_op jit(solution)/shard_map/ppermute | solution.py:489
  414.9 12.8 %collective-permute-start.121 = (bf16[64,2816]{1,0:T(8,128)(2,1)S(1)}, bf16[64,2816]{1,0:T(8,128)(2,1)S(1)}, u32[]{:S(2)}, u32[]{:S(2)}) collective-permute-start(bf16[64,2816]{1,0:T(8,128)(2,1)S(1)} %get-tuple-element.134), channel_id=1, source_target_pairs={{0,8},{2,10},{8,16},{10,18},{16,24},{18,26},{24,28},{26,30},{28,20... | collective-permute-start | bytes 1081352 | tf_op jit(solution)/shard_map/ppermute | solution.py:486
  425.6 17.2 %collective-permute-start.89 = (bf16[64,3080]{1,0:T(8,128)(2,1)S(1)}, bf16[64,3080]{1,0:T(8,128)(2,1)S(1)}, u32[]{:S(2)}, u32[]{:S(2)}) collective-permute-start(bf16[64,3080]{1,0:T(8,128)(2,1)S(1)} %get-tuple-element.122), channel_id=1, source_target_pairs={{0,8},{2,10},{8,16},{10,18},{16,24},{18,26},{24,28},{26,30},{28,20... | collective-permute-start | bytes 1182728 | tf_op jit(solution)/shard_map/ppermute | solution.py:486
  427.7 12.6 %collective-permute-start.95 = (bf16[64,3080]{1,0:T(8,128)(2,1)S(1)}, bf16[64,3080]{1,0:T(8,128)(2,1)S(1)}, u32[]{:S(2)}, u32[]{:S(2)}) collective-permute-start(bf16[64,3080]{1,0:T(8,128)(2,1)S(1)} %add_convert_fusion.1), channel_id=1, source_target_pairs={{8,0},{10,2},{16,8},{18,10},{24,16},{26,18},{28,24},{30,26},{20,28... | collective-permute-start | bytes 1182728 | tf_op jit(solution)/shard_map/ppermute | solution.py:489
  (135 other events, 1080.1 us)

commit v2 on v1

v2 whole, which is shorter than its diff:
```python
import functools

import jax
import jax.numpy as jnp
from jax import lax
from jax.experimental import pallas as pl
from jax.experimental.pallas import tpu as pltpu
from jax.sharding import PartitionSpec as P


SUB = 128
LANES = 128
UNROLLED_CHIPS = 16
bf16 = jnp.bfloat16
f32 = jnp.float32


def dims_of(kind):
    return {
        "nn": (((1,), (0,)), ((), ())),
        "nt": (((1,), (1,)), ((), ())),
        "tn": (((0,), (0,)), ((), ())),
    }[kind]


def dot1(left, right, kind="nn"):
    return lax.dot_general(left, right, dims_of(kind), preferred_element_type=f32)


def cut(array):
    high = array.astype(bf16)
    return (high, (array - high.astype(f32)).astype(bf16))


def dot3(left, right, kind="nn"):
    return (
        dot1(left[0], right[0], kind)
        + dot1(left[0], right[1], kind)
        + dot1(left[1], right[0], kind)
    )


def shift_down(array, amount):
    if amount == 0:
        return array
    rows = lax.broadcasted_iota(jnp.int32, array.shape, 0)
    return jnp.where(rows >= amount, pltpu.roll(array, amount, 0), 0.0)


def shift_up(array, amount):
    if amount == 0:
        return array
    length = array.shape[0]
    rows = lax.broadcasted_iota(jnp.int32, array.shape, 0)
    return jnp.where(rows < length - amount, pltpu.roll(array, length - amount, 0), 0.0)


def conv_rows(projected, kernel):
    taps = kernel.shape[0]
    summed = kernel[taps - 1 : taps] * projected
    for offset in range(1, taps):
        tap = taps - 1 - offset
        summed = summed + kernel[tap : tap + 1] * shift_down(projected, offset)
    return summed


def conv_back(grad_conv, projected, kernel):
    taps = kernel.shape[0]
    grad_proj = kernel[taps - 1 : taps] * grad_conv
    for offset in range(1, taps):
        tap = taps - 1 - offset
        grad_proj = grad_proj + kernel[tap : tap + 1] * shift_up(grad_conv, offset)
    terms = []
    for tap in range(taps):
        moved = shift_down(projected, taps - 1 - tap)
        terms.append(jnp.sum(grad_conv * moved, 0, keepdims=True))
    return grad_proj, jnp.concatenate(terms, 0)


def silu_slope(values, sigma):
    return sigma * (1.0 + values * (1.0 - sigma))


def gate_rows(small, lanes_ref, heads):
    lane = lax.broadcasted_iota(jnp.int32, small.shape, 1)
    rate = jnp.exp(lanes_ref[0:1, :])
    shifted = small + lanes_ref[1:2, :]
    soft = jnp.maximum(shifted, 0.0) + jnp.log1p(jnp.exp(-jnp.abs(shifted)))
    gates = jnp.where(lane >= heads, -rate * soft, 0.0)
    slope = jnp.where(lane >= heads, -rate * jax.nn.sigmoid(shifted), 0.0)
    return jax.nn.sigmoid(small), gates, slope


def sum_gates(gates):
    length = gates.shape[0]
    row = lax.broadcasted_iota(jnp.int32, (length, length), 0)
    col = lax.broadcasted_iota(jnp.int32, (length, length), 1)
    lower = (row >= col).astype(f32)
    upper = (row <= col).astype(f32)
    kwargs = dict(precision=lax.Precision.HIGHEST, preferred_element_type=f32)
    by_row = lax.dot_general(lower, gates, dims_of("nn"), **kwargs)
    by_col = lax.dot_general(gates, upper, dims_of("tn"), **kwargs)
    return by_row, by_col


def lane_pick(array, index):
    lane = lax.broadcasted_iota(jnp.int32, array.shape, 1)
    return jnp.sum(jnp.where(lane == index, array, 0.0), 1, keepdims=True)


def row_pick(array, index):
    row = lax.broadcasted_iota(jnp.int32, array.shape, 0)
    return jnp.sum(jnp.where(row == index, array, 0.0), 0, keepdims=True)


def decay_square(cum_col, cum_row):
    length = cum_col.shape[0]
    row = lax.broadcasted_iota(jnp.int32, (length, length), 0)
    col = lax.broadcasted_iota(jnp.int32, (length, length), 1)
    keep = row >= col
    square = jnp.where(keep, jnp.exp(jnp.where(keep, cum_col - cum_row, 0.0)), 0.0)
    return square, keep, row > col


def unit_rows(raw, kernel):
    conv = conv_rows(raw, kernel)
    sigma = jax.nn.sigmoid(conv)
    act = conv * sigma
    inverse = lax.rsqrt(jnp.sum(act * act, -1, keepdims=True) + 1e-06)
    return conv, sigma, act, inverse


def fetch(pieces, starts_ref, target, sems, cols):
    copies = []
    for i, piece in enumerate(pieces):
        rows = piece.shape[0]
        start = pl.multiple_of(starts_ref[i], rows)
        copies.append(
            pltpu.make_async_copy(
                piece.at[:, cols], target.at[pl.ds(start, rows), :], sems.at[i]
            )
        )
    for copy in copies:
        copy.start()
    return copies


def spill(chunks, starts_ref, source, sems):
    copies = []
    for i, chunk in enumerate(chunks):
        rows = chunk.shape[0]
        start = pl.multiple_of(starts_ref[i], rows)
        copies.append(pltpu.make_async_copy(source.at[pl.ds(start, rows), :], chunk, sems.at[i]))
    for copy in copies:
        copy.start()
    return copies


def wait_all(copies):
    for copy in copies:
        copy.wait()


def outer(left_ref, right, target_ref):
    total = left_ref.shape[1]
    step = 256 if total % 256 == 0 else total
    for start in range(0, total, step):
        span = slice(start, start + step)
        target_ref[span, :] = dot1(left_ref[:, span], right, "tn").astype(bf16)


def head_cuts(local, per_step, key_dim, value_dim):
    wide_key = per_step * key_dim
    wide_value = per_step * value_dim
    kcut = slice(local * key_dim, (local + 1) * key_dim)
    vcut = slice(local * value_dim, (local + 1) * value_dim)
    starts = (
        local * key_dim,
        wide_key + local * key_dim,
        2 * wide_key + local * value_dim,
        2 * wide_key + wide_value + local * value_dim,
    )
    widths = (key_dim, key_dim, value_dim, value_dim)
    pieces = [slice(start, start + width) for start, width in zip(starts, widths)]
    return kcut, vcut, pieces


def forward_kernel(
    heads, group, per_step, key_dim, value_dim, count,
    starts_ref, x_ref, lanes_ref, conv_query_ref, conv_key_ref, conv_value_ref, gain_ref, *refs
):
    pieces = refs[:count]
    proj_ref, small_ref, half_ref, mixed_ref, update_ref, inverse_ref = refs[count : count + 6]
    weight_ref, small_weight_ref, sems = refs[count + 6 :]
    width = proj_ref.shape[1]
    end = pieces[0].shape[1]
    copies = fetch(
        pieces, starts_ref, weight_ref, sems.at[0], slice(group * width, (group + 1) * width)
    )
    copies += fetch(pieces, starts_ref, small_weight_ref, sems.at[1], slice(end - LANES, end))
    wait_all(copies)
    small_ref[...] = dot1(x_ref[...], small_weight_ref[...])
    proj_ref[...] = dot1(x_ref[...], weight_ref[...])
    length = proj_ref.shape[0]
    blocks = length // SUB
    beta_all, gates_all, _ = gate_rows(small_ref[...], lanes_ref, heads)
    cum_all, cum_rows = sum_gates(gates_all)
    sub_row = lax.broadcasted_iota(jnp.int32, (SUB, SUB), 0)
    sub_col = lax.broadcasted_iota(jnp.int32, (SUB, SUB), 1)
    state = []
    for local in range(per_step):
        head = group * per_step + local
        kcut, vcut, pieces = head_cuts(local, per_step, key_dim, value_dim)
        _, _, query_act, query_inv = unit_rows(proj_ref[:, pieces[0]], conv_query_ref[:, kcut])
        query = query_act * query_inv * key_dim ** (-0.5)
        _, _, key_act, key_inv = unit_rows(proj_ref[:, pieces[1]], conv_key_ref[:, kcut])
        key = key_act * key_inv
        value_conv = conv_rows(proj_ref[:, pieces[2]], conv_value_ref[:, vcut])
        value = value_conv * jax.nn.sigmoid(value_conv)
        beta = lane_pick(beta_all, head)
        decay, _, strict = decay_square(
            lane_pick(cum_all, heads + head), row_pick(cum_rows, heads + head)
        )
        key_parts = cut(key)
        coupling = jnp.where(strict, beta * dot3(key_parts, key_parts, "nt") * decay, 0.0)
        mix = dot3(cut(query), key_parts, "nt") * decay
        state.append((coupling, mix, beta * value))
    inverses = []
    for coupling, _, _ in state:
        parts = []
        for block in range(blocks):
            span = slice(block * SUB, (block + 1) * SUB)
            parts.append(coupling[span, span])
        inverses.append(parts)
    squares = [[part for part in parts] for parts in inverses]
    eye = (sub_row == sub_col).astype(f32)
    size = 1
    current = [[None] * blocks for _ in state]
    while size < SUB:
        member = ((sub_row // (2 * size)) == (sub_col // (2 * size))) & (
            (sub_row // size) != (sub_col // size)
        )
        for h in range(per_step):
            for block in range(blocks):
                cross = jnp.where(member, squares[h][block], 0.0)
                if size == 1:
                    current[h][block] = eye - cross
                else:
                    now = cut(current[h][block])
                    inner = dot3(cut(cross), now)
                    current[h][block] = current[h][block] - dot3(now, cut(inner))
        size = 2 * size
    for local in range(per_step):
        _, vcut, pieces = head_cuts(local, per_step, key_dim, value_dim)
        coupling, mix, target = state[local]
        solved = []
        for block in range(blocks):
            span = slice(block * SUB, (block + 1) * SUB)
            rest = target[span]
            for before in range(block):
                past = slice(before * SUB, (before + 1) * SUB)
                rest = rest - dot3(cut(coupling[span, past]), cut(solved[before]))
            solved.append(dot3(cut(current[local][block]), cut(rest)))
            inverse_ref[local, block] = current[local][block]
        updates = jnp.concatenate(solved, 0)
        mixed = dot3(cut(mix), cut(updates))
        update_ref[:, vcut] = updates
        mixed_ref[:, vcut] = mixed
        inverse = lax.rsqrt(jnp.mean(mixed * mixed, -1, keepdims=True) + 1e-05)
        gate = proj_ref[:, pieces[3]]
        half_ref[:, vcut] = (
            mixed * inverse * gain_ref[...] * (gate * jax.nn.sigmoid(gate))
        ).astype(bf16)


def unit_back(grad, conv, sigma, act, inverse, scale):
    inner = jnp.sum(grad * act, -1, keepdims=True)
    grad_act = scale * inverse * (grad - act * (inverse * inverse) * inner)
    return grad_act * silu_slope(conv, sigma)


def backward_kernel(
    heads, group, per_step, key_dim, value_dim, last, count, out_count,
    starts_ref, x_ref, grad_rows_ref, proj_ref, small_ref, lanes_ref,
    conv_query_ref, conv_key_ref, conv_value_ref, gain_ref,
    mixed_ref, update_ref, inverse_ref, carry_ref, hidden_ref, *refs
):
    pieces = refs[:count]
    out_pieces = refs[count : count + out_count]
    refs = refs[count + out_count :]
    chunks = refs[:count]
    conv_query_out, conv_key_out, conv_value_out, gain_out, carry_out, lanes_out, hidden_out = refs[
        count : count + 7
    ]
    weight_ref, out_weight_ref, grads_ref, sum_ref, sems = refs[count + 7 :]
    width = grads_ref.shape[1]
    value_width = mixed_ref.shape[1]
    grouped = 2 * per_step * (key_dim + value_dim)
    out_copies = fetch(
        out_pieces, starts_ref, out_weight_ref, sems.at[0],
        slice(group * value_width, (group + 1) * value_width),
    )
    copies = fetch(
        pieces, starts_ref, weight_ref, sems.at[1], slice(group * grouped, group * grouped + width)
    )
    wait_all(out_copies)
    grad_all = dot1(grad_rows_ref[...], out_weight_ref[...])
    length = proj_ref.shape[0]
    blocks = length // SUB
    small = small_ref[...]
    beta_all, gates_all, slope_all = gate_rows(small, lanes_ref, heads)
    cum_all, cum_rows = sum_gates(gates_all)
    lane = lax.broadcasted_iota(jnp.int32, small.shape, 1)
    upper = (
        lax.broadcasted_iota(jnp.int32, (length, length), 0)
        <= lax.broadcasted_iota(jnp.int32, (length, length), 1)
    ).astype(bf16)

    carry = carry_ref[...]
    gain_sum = jnp.zeros((1, value_dim), f32)
    for local in range(per_step):
        head = group * per_step + local
        kcut, vcut, pieces = head_cuts(local, per_step, key_dim, value_dim)
        scale = key_dim ** (-0.5)
        query_raw = proj_ref[:, pieces[0]]
        key_raw = proj_ref[:, pieces[1]]
        value_raw = proj_ref[:, pieces[2]]
        query_conv, query_sigma, query_act, query_inv = unit_rows(
            query_raw, conv_query_ref[:, kcut]
        )
        query = query_act * query_inv * scale
        key_conv, key_sigma, key_act, key_inv = unit_rows(key_raw, conv_key_ref[:, kcut])
        key = key_act * key_inv
        value_conv = conv_rows(value_raw, conv_value_ref[:, vcut])
        value_sigma = jax.nn.sigmoid(value_conv)
        value = value_conv * value_sigma
        mixed = mixed_ref[:, vcut]
        inverse = lax.rsqrt(jnp.mean(mixed * mixed, -1, keepdims=True) + 1e-05)
        gate = proj_ref[:, pieces[3]]
        gate_sigma = jax.nn.sigmoid(gate)
        gain = gain_ref[...]
        normed = mixed * inverse
        grad_out = grad_all[:, vcut]
        through = grad_out * normed
        grad_gate = through * gain * silu_slope(gate, gate_sigma)
        swish = gate * gate_sigma
        gain_sum = gain_sum + jnp.sum(through * swish, 0, keepdims=True)
        grad_normed = grad_out * gain * swish
        grad_mixed = inverse * (
            grad_normed - normed * jnp.mean(grad_normed * normed, -1, keepdims=True)
        )
        beta = lane_pick(beta_all, head)
        decay, keep, strict = decay_square(
            lane_pick(cum_all, heads + head), row_pick(cum_rows, heads + head)
        )
        key_parts = cut(key)
        query_parts = cut(query)
        pair = dot3(key_parts, key_parts, "nt") * decay
        coupling = jnp.where(strict, beta * pair, 0.0)
        mix = dot3(query_parts, key_parts, "nt") * decay
        updates = cut(update_ref[:, vcut])
        grad_parts = cut(grad_mixed)
        grad_mix = jnp.where(keep, dot3(grad_parts, updates, "nt"), 0.0)
        grad_updates = dot3(cut(mix), grad_parts, "tn")
        solved = [None] * blocks
        for block in reversed(range(blocks)):
            span = slice(block * SUB, (block + 1) * SUB)
            rest = grad_updates[span]
            for after in range(block + 1, blocks):
                later = slice(after * SUB, (after + 1) * SUB)
                rest = rest - dot3(cut(coupling[later, span]), cut(solved[after]), "tn")
            solved[block] = dot3(cut(inverse_ref[local, block]), cut(rest), "tn")
        grad_target = jnp.concatenate(solved, 0)
        grad_coupling = jnp.where(strict, -dot3(cut(grad_target), updates, "nt"), 0.0)
        grad_value = beta * grad_target
        grad_beta = jnp.sum(grad_target * value, -1, keepdims=True) + jnp.sum(
            grad_coupling * pair, -1, keepdims=True
        )
        flow = cut(grad_coupling * coupling + grad_mix * mix)
        run = dot1(upper, flow[0]) + dot1(upper, flow[1])
        grad_log = jnp.sum(jnp.where(strict, run, 0.0), -1, keepdims=True)
        grad_pair = cut(grad_coupling * beta * decay)
        grad_cross = cut(grad_mix * decay)
        grad_query = dot3(grad_cross, key_parts)
        grad_key = (
            dot3(grad_cross, query_parts, "tn")
            + dot3(grad_pair, key_parts)
            + dot3(grad_pair, key_parts, "tn")
        )
        grad_query_raw, grad_conv = conv_back(
            unit_back(grad_query, query_conv, query_sigma, query_act, query_inv, scale),
            query_raw, conv_query_ref[:, kcut],
        )
        conv_query_out[:, kcut] = grad_conv
        grad_key_raw, grad_conv = conv_back(
            unit_back(grad_key, key_conv, key_sigma, key_act, key_inv, 1.0),
            key_raw, conv_key_ref[:, kcut],
        )
        conv_key_out[:, kcut] = grad_conv
        grad_value_raw, grad_conv = conv_back(
            grad_value * silu_slope(value_conv, value_sigma), value_raw, conv_value_ref[:, vcut]
        )
        conv_value_out[:, vcut] = grad_conv
        grads_ref[:, pieces[0]] = grad_query_raw.astype(bf16)
        grads_ref[:, pieces[1]] = grad_key_raw.astype(bf16)
        grads_ref[:, pieces[2]] = grad_value_raw.astype(bf16)
        grads_ref[:, pieces[3]] = grad_gate.astype(bf16)
        carry = carry + jnp.where(lane == head, grad_beta, 0.0)
        carry = carry + jnp.where(lane == heads + head, grad_log, 0.0)

    gain_out[...] = gain_sum
    carry_out[...] = carry
    is_gate = lane >= heads
    grad_small = jnp.where(is_gate, carry * slope_all, carry * beta_all * (1.0 - beta_all))
    if last:
        end = 2 * per_step * (key_dim + value_dim)
        grads_ref[:, end : end + LANES] = jnp.where(lane < 2 * heads, grad_small, 0.0).astype(bf16)
    lanes_out[0:1, :] = jnp.sum(jnp.where(is_gate, carry * gates_all, 0.0), 0, keepdims=True)
    lanes_out[1:2, :] = jnp.sum(grad_small, 0, keepdims=True)
    grads = grads_ref[...]
    outer(x_ref, grads, sum_ref)
    out_copies = spill(chunks, starts_ref, sum_ref, sems.at[0])
    wait_all(copies)
    hidden_out[...] = hidden_ref[...] + dot1(grads, weight_ref[...], "nt")
    wait_all(out_copies)


def ffn_kernel(
    count, starts_ref, x_ref, cot_ref, *refs
):
    gate_pieces = refs[:count]
    down_pieces = refs[count : 2 * count]
    inner_ref, grads_ref, hidden_ref, weight_ref, down_ref, sems = refs[2 * count :]
    hidden = inner_ref.shape[1]
    copies = fetch(gate_pieces, starts_ref, weight_ref, sems.at[0], slice(0, 2 * hidden))
    down_copies = fetch(down_pieces, starts_ref, down_ref, sems.at[1], slice(0, hidden))
    wait_all(copies)
    rows = x_ref[...]
    gate_pre = dot1(rows, weight_ref[:, :hidden])
    up_pre = dot1(rows, weight_ref[:, hidden:])
    sigma = jax.nn.sigmoid(gate_pre)
    gate_act = gate_pre * sigma
    inner_ref[...] = (gate_act * up_pre).astype(bf16)
    wait_all(down_copies)
    grad_inner = dot1(cot_ref[...], down_ref[...])
    grads_ref[:, :hidden] = (grad_inner * up_pre * silu_slope(gate_pre, sigma)).astype(bf16)
    grads_ref[:, hidden:] = (grad_inner * gate_act).astype(bf16)
    hidden_ref[...] = dot1(grads_ref[...], weight_ref[...], "nt")


def outer_kernel(count, starts_ref, left_ref, right_ref, *refs):
    chunks = refs[:count]
    sum_ref, sems = refs[count:]
    outer(left_ref, right_ref[...], sum_ref)
    wait_all(spill(chunks, starts_ref, sum_ref, sems))


def branch_kernel(count, starts_ref, left_ref, *refs):
    pieces = refs[:count]
    out_ref, weight_ref, sems = refs[count:]
    copies = fetch(pieces, starts_ref, weight_ref, sems, slice(0, left_ref.shape[1]))
    wait_all(copies)
    out_ref[...] = dot1(left_ref[...], weight_ref[...], "nt")


VMEM_SPEC = pl.BlockSpec(memory_space=pltpu.VMEM)
HBM_SPEC = pl.BlockSpec(memory_space=pl.ANY)
SMEM_SPEC = pl.BlockSpec(memory_space=pltpu.SMEM)


def call(kernel, starts, inside, outside, out_inside, out_outside, scratch):
    shapes = list(out_outside) + list(out_inside)
    return pl.pallas_call(
        kernel,
        in_specs=[SMEM_SPEC] + [VMEM_SPEC] * len(inside) + [HBM_SPEC] * len(outside),
        out_specs=[HBM_SPEC] * len(out_outside) + [VMEM_SPEC] * len(out_inside),
        out_shape=shapes,
        scratch_shapes=scratch,
    )(starts, *inside, *outside)


def shape(dims, dtype):
    return jax.ShapeDtypeStruct(dims, dtype)


def mixer_forward(starts, pieces, rows, lanes, convs, gain, heads, group, per_step):
    length, model = rows.shape
    key_dim = convs[0].shape[1] // per_step
    value_dim = convs[2].shape[1] // per_step
    wide = per_step * value_dim
    width = 2 * per_step * (key_dim + value_dim)
    count = len(pieces)
    return call(
        functools.partial(forward_kernel, heads, group, per_step, key_dim, value_dim, count),
        starts, (rows, lanes, *convs, gain), pieces,
        [
            shape((length, width), f32),
            shape((length, LANES), f32),
            shape((length, wide), bf16),
            shape((length, wide), f32),
            shape((length, wide), f32),
            shape((per_step, length // SUB, SUB, SUB), f32),
        ],
        [],
        [
            pltpu.VMEM((model, width), bf16),
            pltpu.VMEM((model, LANES), bf16),
            pltpu.SemaphoreType.DMA((2, count)),
        ],
    )


def mixer_backward(
    starts, pieces, out_pieces, rows, grad_rows, proj, small, lanes, convs, gain, saved,
    carry, hidden, heads, group, per_step, last,
):
    length, model = rows.shape
    taps = convs[0].shape[0]
    key_dim = convs[0].shape[1] // per_step
    value_dim = convs[2].shape[1] // per_step
    width = proj.shape[1] + (LANES if last else 0)
    count = len(pieces)
    results = call(
        functools.partial(
            backward_kernel, heads, group, per_step, key_dim, value_dim, last, count,
            len(out_pieces),
        ),
        starts,
        (rows, grad_rows, proj, small, lanes, *convs, gain, *saved, carry, hidden),
        list(pieces) + list(out_pieces),
        [
            shape((taps, per_step * key_dim), f32),
            shape((taps, per_step * key_dim), f32),
            shape((taps, per_step * value_dim), f32),
            shape((1, value_dim), f32),
            shape(carry.shape, f32),
            shape((2, LANES), f32),
            shape(hidden.shape, f32),
        ],
        [shape((piece.shape[0], width), bf16) for piece in pieces],
        [
            pltpu.VMEM((model, width), bf16),
            pltpu.VMEM((model, per_step * value_dim), bf16),
            pltpu.VMEM((length, width), bf16),
            pltpu.VMEM((model, width), bf16),
            pltpu.SemaphoreType.DMA((2, count)),
        ],
    )
    return results[:count], results[count : count + 3], results[count + 3 :]


def ffn_pass(starts, gate_pieces, down_pieces, rows, cotangent):
    length, model = rows.shape
    hidden = down_pieces[0].shape[1]
    count = len(gate_pieces)
    return call(
        functools.partial(ffn_kernel, count), starts, (rows, cotangent),
        list(gate_pieces) + list(down_pieces),
        [
            shape((length, hidden), bf16),
            shape((length, 2 * hidden), bf16),
            shape((length, model), f32),
        ],
        [],
        [
            pltpu.VMEM((model, 2 * hidden), bf16),
            pltpu.VMEM((model, hidden), bf16),
            pltpu.SemaphoreType.DMA((2, count)),
        ],
    )


def outer_chunks(starts, like, left, right):
    count = len(like)
    width = right.shape[1]
    return call(
        functools.partial(outer_kernel, count), starts, (left, right), [],
        [], [shape((piece.shape[0], width), bf16) for piece in like],
        [pltpu.VMEM((left.shape[1], width), bf16), pltpu.SemaphoreType.DMA((count,))],
    )


def branch_rows(starts, pieces, left):
    count = len(pieces)
    model = left.shape[0]
    model = sum(piece.shape[0] for piece in pieces)
    return call(
        functools.partial(branch_kernel, count), starts, (left,), pieces,
        [shape((left.shape[0], model), f32)], [],
        [pltpu.VMEM((model, left.shape[1]), bf16), pltpu.SemaphoreType.DMA((count,))],
    )[0]


def rms_rows(inputs, gain):
    wide_rows = inputs.astype(f32)
    inverse = lax.rsqrt(jnp.mean(wide_rows * wide_rows, -1, keepdims=True) + 1e-05)
    normed = wide_rows * inverse
    return (normed, inverse, (normed * gain).astype(bf16))


def rms_back(grad_rows, normed, inverse, gain):
    scaled = grad_rows * gain
    grad_in = inverse * (scaled - normed * jnp.mean(scaled * normed, -1, keepdims=True))
    return (grad_in, jnp.sum(grad_rows * normed, 0))


def by_core(core, mine, other):
    return jnp.where(
        core == 0, jnp.concatenate([mine, other], 0), jnp.concatenate([other, mine], 0)
    )


def spread(core, array):
    return by_core(core, array, jnp.zeros_like(array))


class Ring:
    def __init__(self, axis):
        self.axis = axis
        self.chips = lax.axis_size(axis) // 2
        evens = [chip for chip in range(self.chips) if chip % 2 == 0]
        odds = [chip for chip in range(self.chips) if chip % 2 == 1]
        order = evens + odds[::-1]
        following = [(order[i], order[(i + 1) % self.chips]) for i in range(self.chips)]
        self.moves = [(2 * a, 2 * b) for a, b in following]
        self.moves += [(2 * b + 1, 2 * a + 1) for a, b in following]
        self.plain = self.chips > UNROLLED_CHIPS
        self.pairs = [(i, i ^ 1) for i in range(2 * self.chips)]
        index = lax.axis_index(axis)
        self.core = index % 2
        self.sign = 1 - 2 * self.core
        chip = index // 2
        self.position = jnp.where(
            chip % 2 == 0, chip // 2, self.chips - 1 - (chip - 1) // 2
        )

    def chip_at(self, shift):
        spot = (self.position + shift) % self.chips
        evens = (self.chips + 1) // 2
        return jnp.where(spot < evens, 2 * spot, 2 * (self.chips - 1 - spot) + 1)

    def starts(self, rows):
        if self.plain:
            return jnp.zeros((1,), jnp.int32)
        half = self.chips // 2
        chips = [self.chip_at(0)]
        chips += [self.chip_at(-self.sign * step) for step in range(1, half)]
        chips += [self.chip_at(self.sign * step) for step in range(1, half)]
        far = 2 * rows * self.chip_at(half)
        edges = [2 * rows * chip for chip in chips]
        edges += [far + self.core * rows, far + (1 - self.core) * rows]
        return jnp.stack(edges).astype(jnp.int32)

    def onward(self, array):
        return lax.ppermute(array, self.axis, self.moves)

    def partner(self, array):
        return lax.ppermute(array, self.axis, self.pairs)

    def total(self, array, marks):
        size = 1
        marks = list(marks)
        while size < 2 * self.chips:
            flips = [(i, i ^ size) for i in range(2 * self.chips)]
            if marks:
                array = after(array, marks.pop(0))
            array = array + lax.ppermute(array, self.axis, flips)
            size = 2 * size
        return array


class Gather:
    def __init__(self, ring, shard, *deps):
        shard = after(shard, *deps)
        self.ring = ring
        self.rows = shard.shape[0]
        self.half = ring.chips // 2
        self.step = 0
        self.piece = shard
        if ring.plain:
            self.pieces = [lax.all_gather(shard, ring.axis, axis=0, tiled=True)]
            self.step = self.half
            return
        other = ring.partner(shard)
        self.piece = by_core(ring.core, shard, other)
        self.pieces = [self.piece]
        self.echoes = []

    def advance(self, *deps):
        if self.step == self.half:
            return self
        self.step = self.step + 1
        ring, rows = self.ring, self.rows
        piece = after(self.piece, *deps)
        if self.step == self.half:
            piece = lax.dynamic_slice_in_dim(piece, ring.core * rows, rows, 0)
        piece = ring.onward(piece)
        echo = ring.partner(piece)
        self.pieces.append(piece)
        self.echoes.append(echo)
        self.piece = piece
        return self

    def finish(self):
        while self.step < self.half:
            self.advance()
        if self.ring.plain:
            return self.pieces
        return self.pieces[:-1] + self.echoes[:-1] + [self.pieces[-1], self.echoes[-1]]


class Scatter:
    def __init__(self, ring, chunks):
        self.ring = ring
        self.chunks = chunks
        self.half = ring.chips // 2
        self.step = 0 if ring.plain else self.half
        self.arrived = chunks[0]

    def advance(self, *deps):
        if self.step == 0:
            return self
        ring, half, chunks = self.ring, self.half, self.chunks
        if self.step == half:
            echo = ring.partner(chunks[2 * half])
            moving = chunks[2 * half - 1].astype(f32) + echo.astype(f32)
        else:
            echo = ring.partner(chunks[self.step]).astype(f32)
            arrived = self.arrived.astype(f32)
            if self.step == half - 1:
                arrived = spread(ring.core, arrived)
            moving = chunks[half - 1 + self.step].astype(f32) + echo + arrived
        self.arrived = ring.onward(after(moving.astype(bf16), *deps))
        self.step = self.step - 1
        return self

    def finish(self):
        ring = self.ring
        if ring.plain:
            return lax.psum_scatter(
                self.chunks[0].astype(f32), ring.axis, scatter_dimension=0, tiled=True
            )
        while self.step > 0:
            self.advance()
        arrived = self.arrived.astype(f32)
        if self.half == 1:
            arrived = spread(ring.core, arrived)
        own = self.chunks[0].astype(f32) + arrived
        rows = own.shape[0] // 2
        give = lax.dynamic_slice_in_dim(own, (1 - ring.core) * rows, rows, 0).astype(bf16)
        keep = lax.dynamic_slice_in_dim(own, ring.core * rows, rows, 0)
        return keep + ring.partner(give).astype(f32)


def others_of(array, axis):
    count = lax.axis_size(axis)
    received = []
    for shift in range(1, count):
        moves = [(i, (i + shift) % count) for i in range(count)]
        received.append(lax.ppermute(array, axis, moves))
    return received


def by_index(axis, pieces, dim):
    count = lax.axis_size(axis)
    index = lax.axis_index(axis)
    joined = None
    for value in range(count):
        here = jnp.concatenate([pieces[(value - i) % count] for i in range(count)], dim)
        joined = here if joined is None else jnp.where(index == value, here, joined)
    return joined


def gather_rows(array, axis):
    return by_index(axis, [array] + others_of(array, axis), 0)


def scatter_rows(partial, axis):
    count = lax.axis_size(axis)
    index = lax.axis_index(axis)
    rows = partial.shape[0] // count
    total = lax.dynamic_slice_in_dim(partial, index * rows, rows, 0)
    for shift in range(1, count):
        target = (index + shift) % count
        part = lax.dynamic_slice_in_dim(partial, target * rows, rows, 0).astype(bf16)
        moves = [(i, (i + shift) % count) for i in range(count)]
        total = total + lax.ppermute(part, axis, moves).astype(f32)
    return total


def after(array, *done):
    return lax.optimization_barrier((array, *done))[0] if done else array


def on_device(
    tokens, out_cotangent, seq_lengths, norm_gain1, query_weight, key_weight, value_weight,
    out_gate_weight, beta_weight, decay_weight, conv_query, conv_key, conv_value,
    decay_log_rate, decay_bias, out_gain, out_weight, norm_gain2, ffn_gate_weight,
    ffn_up_weight, ffn_down_weight,
):
    ring = Ring("dp")
    local_rows = tokens.shape[0]
    tensor_index = lax.axis_index("tensor")
    seq_length = seq_lengths[0]
    local_pos = tensor_index * local_rows + jnp.arange(local_rows, dtype=jnp.int32)
    local_mask = (local_pos < seq_length).astype(f32)[:, None]
    key_cols = query_weight.shape[1]
    value_cols = value_weight.shape[1]
    heads = beta_weight.shape[1]
    hidden_cols = ffn_gate_weight.shape[1]
    per_step = max(1, heads // 2)
    groups = heads // per_step
    wide_key = key_cols // groups
    wide_value = value_cols // groups
    grouped = 2 * (wide_key + wide_value)

    def group_of(array, group):
        wide = array.shape[1] // groups
        return array[:, group * wide : (group + 1) * wide]

    starts = ring.starts(query_weight.shape[0])
    proj_weights = (query_weight, key_weight, value_weight, out_gate_weight)
    narrow = jnp.concatenate([beta_weight, decay_weight], 1)
    parts = [group_of(weight, group) for group in range(groups) for weight in proj_weights]
    parts.append(jnp.pad(narrow, ((0, 0), (0, LANES - 2 * heads))))
    proj_joined = jnp.concatenate(parts, 1)
    ffn_joined = jnp.concatenate([ffn_gate_weight, ffn_up_weight], 1)
    normed1, inverse1, hidden1 = rms_rows(tokens, norm_gain1)
    whole1 = gather_rows(hidden1, "tensor")
    grad_local = (local_mask * out_cotangent.astype(f32)).astype(bf16)
    grad_whole = gather_rows(grad_local, "tensor")
    lanes = jnp.pad(
        jnp.stack([decay_log_rate, decay_bias]), ((0, 0), (heads, LANES - 2 * heads))
    )
    gain_wide = out_gain[None]
    convs = [
        tuple(group_of(conv, group) for conv in (conv_query, conv_key, conv_value))
        for group in range(groups)
    ]

    proj_gather = Gather(ring, proj_joined)
    proj_gather.advance().advance()
    out_gather = Gather(ring, out_weight, proj_gather.piece)
    proj_gather.advance()
    out_gather.advance()
    late = proj_gather.piece
    proj_pieces = proj_gather.finish()
    out_pieces = out_gather.finish()
    ffn_gather = Gather(ring, ffn_joined, late)
    down_gather = Gather(ring, ffn_down_weight, late)
    ffn_pieces = ffn_gather.finish()
    down_pieces = down_gather.finish()
    projections = []
    halves = []
    saved = []
    for group in range(groups):
        proj, small, half, *kept = mixer_forward(
            starts, proj_pieces, whole1, lanes, convs[group], gain_wide, heads, group, per_step
        )
        projections.append(proj)
        halves.append(half)
        saved.append(kept)
    mixed_half = jnp.concatenate(halves, 1)
    branch = scatter_rows(branch_rows(starts, out_pieces, mixed_half), "tensor")
    residual = tokens.astype(f32) + branch
    normed2, inverse2, hidden2 = rms_rows(residual, norm_gain2)
    whole2 = gather_rows(hidden2, "tensor")

    inner_act, grad_pre_both, partial_hidden2 = ffn_pass(
        starts, ffn_pieces, down_pieces, whole2, grad_whole
    )
    grad_hidden2 = scatter_rows(partial_hidden2, "tensor")
    ffn_chunks = outer_chunks(starts, ffn_pieces, whole2, grad_pre_both)
    down_chunks = outer_chunks(starts, ffn_pieces, grad_whole, inner_act)
    ffn_scatter = Scatter(ring, ffn_chunks)
    down_scatter = Scatter(ring, down_chunks)
    grad_normed2, second_gain_gradient = rms_back(grad_hidden2, normed2, inverse2, norm_gain2)
    grad_residual = local_mask * out_cotangent.astype(f32) + grad_normed2
    grad_whole1 = gather_rows(grad_residual.astype(bf16), "tensor")
    ffn_branch = scatter_rows(
        branch_rows(starts, down_pieces, after(inner_act, grad_residual)), "tensor"
    )
    output = (local_mask * (residual + ffn_branch)).astype(bf16)
    down_shard = down_scatter.finish()
    ffn_shard = ffn_scatter.finish()
    out_chunks = outer_chunks(starts, out_pieces, grad_whole1, mixed_half)
    out_shard = Scatter(ring, out_chunks).finish()
    carry = jnp.zeros((whole1.shape[0], LANES), f32)
    partial_hidden = jnp.zeros(whole1.shape, f32)
    conv_grads = []
    gain_sum = 0.0
    scatters = []
    for group in range(groups):
        chunks, conv_grad, (gain_part, carry, lane_sums, partial_hidden) = mixer_backward(
            starts, proj_pieces, out_pieces, whole1, grad_whole1, projections[group], small,
            lanes, convs[group], gain_wide, saved[group], carry, partial_hidden, heads, group,
            per_step, group == groups - 1,
        )
        conv_grads.append(conv_grad)
        gain_sum = gain_sum + gain_part
        scatters.append(Scatter(ring, chunks))
    grad_hidden1 = scatter_rows(partial_hidden, "tensor")
    grad_normed1, first_gain_gradient = rms_back(grad_hidden1, normed1, inverse1, norm_gain1)
    grad_tokens = (grad_residual + grad_normed1).astype(bf16)
    marks = []
    while scatters[-1].step > 0:
        scatters[-1].advance()
        marks.append(scatters[-1].arrived)
    proj_shards = [scatter.finish() for scatter in scatters]
    edges = [0, wide_key, 2 * wide_key, 2 * wide_key + wide_value, grouped]
    mixer_grads = [
        jnp.concatenate([shard[:, edges[i] : edges[i + 1]] for shard in proj_shards], 1)
        for i in range(4)
    ]
    mixer_grads.append(proj_shards[-1][:, grouped : grouped + heads])
    mixer_grads.append(proj_shards[-1][:, grouped + heads : grouped + 2 * heads])
    ffn_grads = [ffn_shard[:, :hidden_cols], ffn_shard[:, hidden_cols:]]
    grad_conv_query, grad_conv_key, grad_conv_value = [
        jnp.concatenate([conv_grad[i] for conv_grad in conv_grads], 1) for i in range(3)
    ]

    taps = conv_query.shape[0]
    blocks = [
        jnp.concatenate([grad_conv_query, grad_conv_key], 1),
        grad_conv_value,
        first_gain_gradient[None],
        second_gain_gradient[None],
        gain_sum,
        lane_sums[:, : 2 * heads],
    ]
    wide = max(block.shape[1] for block in blocks)
    tall = sum(block.shape[0] for block in blocks)
    blocks = [jnp.pad(block, ((0, 0), (0, wide - block.shape[1]))) for block in blocks]
    blocks.append(jnp.zeros((-tall % 8, wide), f32))
    packed = ring.total(jnp.concatenate(blocks, 0), marks)
    pieces = [packed] + others_of(packed, "tensor")
    summed = pieces[0]
    for member in pieces[1:]:
        summed = summed + member

    def joined(row, rows, start, cols):
        parts = [member[row : row + rows, start : start + cols] for member in pieces]
        return by_index("tensor", parts, 1)

    gain_row = 2 * taps
    return (
        output,
        grad_tokens,
        summed[gain_row, : norm_gain1.shape[0]],
        mixer_grads[0],
        mixer_grads[1],
        mixer_grads[2],
        mixer_grads[3],
        mixer_grads[4],
        mixer_grads[5],
        joined(0, taps, 0, key_cols),
        joined(0, taps, key_cols, key_cols),
        joined(taps, taps, 0, value_cols),
        joined(gain_row + 3, 1, heads, heads)[0],
        joined(gain_row + 4, 1, heads, heads)[0],
        summed[gain_row + 2, : out_gain.shape[0]],
        out_shard,
        summed[gain_row + 1, : norm_gain2.shape[0]],
        ffn_grads[0],
        ffn_grads[1],
        down_shard,
    )


def solution(mesh):
    in_specs = (
        P(("dp", "tensor"), None),
        P(("dp", "tensor"), None),
        P("dp"),
        P(),
        P("dp", "tensor"),
        P("dp", "tensor"),
        P("dp", "tensor"),
        P("dp", "tensor"),
        P("dp", "tensor"),
        P("dp", "tensor"),
        P(None, "tensor"),
        P(None, "tensor"),
        P(None, "tensor"),
        P("tensor"),
        P("tensor"),
        P(),
        P("dp", "tensor"),
        P(),
        P("dp", "tensor"),
        P("dp", "tensor"),
        P("dp", "tensor"),
    )
    out_specs = (
        P(("dp", "tensor"), None),
        P(("dp", "tensor"), None),
        P(),
        P("dp", "tensor"),
        P("dp", "tensor"),
        P("dp", "tensor"),
        P("dp", "tensor"),
        P("dp", "tensor"),
        P("dp", "tensor"),
        P(),
        P(),
        P(),
        P(),
        P(),
        P(),
        P("dp", "tensor"),
        P(),
        P("dp", "tensor"),
        P("dp", "tensor"),
        P("dp", "tensor"),
    )

    return jax.shard_map(
        on_device, mesh=mesh, in_specs=in_specs, out_specs=out_specs, check_vma=False
    )
```

time: 463 us -> 379 us (0.82)
  the two profiles are of different devices: /device:TPU:8 before, /device:TPU:7 now
where the time goes in v2:
time: 379 us; the launch traced here: 374 us
  waiting for transfers between devices  138 us (36%)
  starting transfers between devices  82.1 us (22%)
  Pallas kernels  79.5 us (21%)
  other arithmetic  42.6 us (11%)
  local copies, waits for them, and re-layouts  28.9 us (8%)
    ppermute x36, waiting for transfers between devices, onward(): return lax.ppermute(array, self.axis, self.moves)  94.4 us
    pallas_call x10, Pallas kernels, call(): pl.pallas_call(kernel, in_specs=[SMEM_SPEC] + [VMEM_SPEC] * len(inside) +...  79.5 us
    ppermute x45, starting transfers between devices, partner(): return lax.ppermute(array, self.axis, self.pairs)  46.7 us
    ppermute x36, starting transfers between devices, onward(): return lax.ppermute(array, self.axis, self.moves)  27 us
    ppermute x4, waiting for transfers between devices, total(): array = array + lax.ppermute(array, self.axis, flips)  18 us
    ppermute x4, waiting for transfers between devices, scatter_rows(): total = total + lax.ppermute(part, axis, moves).astype(f32)  17.7 us
    convert_element_type x20, other arithmetic, advance(): self.arrived = ring.onward(after(moving.astype(bf16), *deps))  13 us
    unnamed x177, local copies, waits for them, and re-layouts  12.4 us
  transfers between devices with their start and end apart: 94, of which 34 were waited for; matrix products, arithmetic and copies ran while one was open for 16% of the time, Pallas kernels for 18%

profile of v2, /device:TPU:7, one launch (start us, length us, event | category | flops | bytes accessed | tf_op | source)
XLA Modules:
  0.0 374.0 jit_solution(16772228198280123536)
XLA Ops:
  8.7 1.4 collective-permute-done.1
  10.2 1.3 collective-permute-start.2
  11.6 10.2 %collective-permute-done.2.refs_1_ = bf16[128,3200]{1,0:T(8,128)(2,1)S(1)} collective-permute-done((bf16[128,3200]{1,0:T(8,128)(2,1)S(1)}, bf16[128,3200]{1,0:T(8,128)(2,1)S(1)}, u32[]{:S(2)}, u32[]{:S(2)}) %collective-permute-start.2) | collective-permute-done | bytes 819232 | tf_op jit(solution)/shard_map/ppermute | solution.py:655
  23.2 10.0 %collective-permute-done.3.refs_2_ = bf16[128,3200]{1,0:T(8,128)(2,1)S(1)} collective-permute-done((bf16[128,3200]{1,0:T(8,128)(2,1)S(1)}, bf16[128,3200]{1,0:T(8,128)(2,1)S(1)}, u32[]{:S(2)}, u32[]{:S(2)}) %collective-permute-start.3) | collective-permute-done | bytes 819232 | tf_op jit(solution)/shard_map/ppermute | solution.py:655
  33.3 2.1 collective-permute-start.10
  37.7 1.7 maximum_select_fusion.7.refs_0_.refs_9_
  42.7 7.1 %collective-permute-done.11.refs_1_.refs_10_ = bf16[128,1024]{1,0:T(8,128)(2,1)} collective-permute-done((bf16[128,1024]{1,0:T(8,128)(2,1)}, bf16[128,1024]{1,0:T(8,128)(2,1)}, u32[]{:S(2)}, u32[]{:S(2)}) %collective-permute-start.11) | collective-permute-done | bytes 262176 | tf_op jit(solution)/shard_map/ppermute | solution.py:655
  52.0 3.6 collective-permute-done.12.refs_2_.refs_11_
  55.6 1.7 collective-permute-start.14
  58.6 2.1 maximum_select_fusion.1.refs_0_
  60.7 1.3 collective-permute-start.8
  62.1 1.3 collective-permute-start.23
  66.6 1.6 collective-permute-done.8.refs_7_
  69.7 1.6 constant_dynamic-slice_fusion.2
  75.9 1.4 collective-permute-start.24
  77.4 2.2 maximum_select_fusion.2.x_ref
  79.5 9.6 %shard_map.356 = (f32[256,1536]{1,0:T(8,128)}, f32[256,128]{1,0:T(8,128)}, bf16[256,512]{1,0:T(8,128)(2,1)}, f32[256,512]{1,0:T(8,128)}, f32[256,512]{1,0:T(8,128)}, /*index=5*/f32[2,2,128,128]{3,2,1,0:T(8,128)}) custom-call(s32[9]{0:T(128)} %stack.48.starts_ref, bf16[256,1024]{1,0:T(8,128)(2,1)} %maximum_select_fusion.2.x_ref, ...), custom_call_target="tpu_custom_call" | custom-call | tf_op jit(solution)/shard_map/pallas_call | solution.py:473
  90.6 9.7 %shard_map.357 = (f32[256,1536]{1,0:T(8,128)}, f32[256,128]{1,0:T(8,128)}, bf16[256,512]{1,0:T(8,128)(2,1)}, f32[256,512]{1,0:T(8,128)}, f32[256,512]{1,0:T(8,128)}, /*index=5*/f32[2,2,128,128]{3,2,1,0:T(8,128)}) custom-call(s32[9]{0:T(128)} %stack.48.starts_ref, bf16[256,1024]{1,0:T(8,128)(2,1)} %maximum_select_fusion.2.x_ref, ...), custom_call_target="tpu_custom_call" | custom-call | tf_op jit(solution)/shard_map/pallas_call | solution.py:473
  103.0 4.4 %shard_map.358 = f32[256,1024]{1,0:T(8,128)} custom-call(s32[9]{0:T(128)} %stack.48.starts_ref, bf16[256,1024]{1,0:T(8,128)(2,1)} %copy-done.7, bf16[128,1024]{1,0:T(8,128)(2,1)} %maximum_select_fusion.7.refs_0_.refs_9_, bf16[128,1024]{1,0:T(8,128)(2,1)} %collective-permute-done.11.refs_1_.refs_10_, ...), custom_call_target="tpu_custom_call" | custom-call | tf_op jit(solution)/shard_map/pallas_call | solution.py:473
  111.8 4.1 %collective-permute-done.19 = bf16[128,1024]{1,0:T(8,128)(2,1)S(1)} collective-permute-done((bf16[128,1024]{1,0:T(8,128)(2,1)S(1)}, bf16[128,1024]{1,0:T(8,128)(2,1)S(1)}, u32[]{:S(2)}, u32[]{:S(2)}) %collective-permute-start.19) | collective-permute-done | bytes 262176 | tf_op jit(solution)/shard_map/ppermute | solution.py:787
  115.9 2.6 collective-permute-start.36
  120.8 8.5 %collective-permute-done.25.refs_3_ = bf16[128,2816]{1,0:T(8,128)(2,1)S(1)} collective-permute-done((bf16[128,2816]{1,0:T(8,128)(2,1)}, bf16[128,2816]{1,0:T(8,128)(2,1)S(1)}, u32[]{:S(2)}, u32[]{:S(2)}) %collective-permute-start.25) | collective-permute-done | bytes 720928 | tf_op jit(solution)/shard_map/ppermute | solution.py:655
  129.3 1.5 collective-permute-start.26
  132.7 1.4 collective-permute-start.28
  134.1 1.4 collective-permute-done.38.refs_16_.refs_7_
  137.9 1.6 collective-permute-done.29.refs_7_
  140.3 2.0 maximum_select_fusion.4.cot_ref.left_ref
  145.3 9.5 %shard_map.359 = (bf16[256,1408]{1,0:T(8,128)(2,1)}, bf16[256,2816]{1,0:T(8,128)(2,1)}, f32[256,1024]{1,0:T(8,128)}) custom-call(s32[9]{0:T(128)} %stack.48.starts_ref, bf16[256,1024]{1,0:T(8,128)(2,1)} %maximum_select_fusion.3.x_ref.left_ref, bf16[256,1024]{1,0:T(8,128)(2,1)} %maximum_select_fusion.4.cot_ref.left_ref, ...), custom_call_target="tpu_custom_call" | custom-call | tf_op jit(solution)/shard_map/pallas_call | solution.py:473
  154.9 4.2 %shard_map.365 = (bf16[128,1408]{1,0:T(8,128)(2,1)}, bf16[128,1408]{1,0:T(8,128)(2,1)}, bf16[128,1408]{1,0:T(8,128)(2,1)}, bf16[128,1408]{1,0:T(8,128)(2,1)}, bf...) custom-call(s32[9]{0:T(128)} %stack.48.starts_ref, ...), custom_call_target="tpu_custom_call" | custom-call | tf_op jit(solution)/shard_map/pallas_call | solution.py:473
  160.1 5.8 %shard_map.364 = (bf16[128,2816]{1,0:T(8,128)(2,1)}, bf16[128,2816]{1,0:T(8,128)(2,1)}, bf16[128,2816]{1,0:T(8,128)(2,1)}, bf16[128,2816]{1,0:T(8,128)(2,1)}, bf...) custom-call(s32[9]{0:T(128)} %stack.48.starts_ref, ...), custom_call_target="tpu_custom_call" | custom-call | tf_op jit(solution)/shard_map/pallas_call | solution.py:473
  166.5 7.1 %collective-permute-done.40 = bf16[128,1024]{1,0:T(8,128)(2,1)S(1)} collective-permute-done((bf16[128,1024]{1,0:T(8,128)(2,1)S(1)}, bf16[128,1024]{1,0:T(8,128)(2,1)S(1)}, u32[]{:S(2)}, u32[]{:S(2)}) %collective-permute-start.40) | collective-permute-done | bytes 262176 | tf_op jit(solution)/shard_map/ppermute | solution.py:787
  174.5 5.0 %shard_map.360 = f32[256,1024]{1,0:T(8,128)} custom-call(s32[9]{0:T(128)} %stack.48.starts_ref, bf16[256,1408]{1,0:T(8,128)(2,1)} %get-tuple-element.106.left_ref.right_ref, bf16[128,1408]{1,0:T(8,128)(2,1)} %copy-done.8, bf16[128,1408]{1,0:T(8,128)(2,1)} %collective-permute-done.32.refs_10_.refs_1_, bf16[128,1408]{1,0:T(8,128)(2,1)} %copy-done.15, ...), custom_call_target="tpu_custom_call" | custom-call | tf_op jit(solution)/shard_map/pallas_call | solution.py:473
  179.5 1.8 dynamic-slice_convert_fusion.2
  182.9 1.9 add_convert_fusion.11
  186.1 1.8 add_convert_fusion.12
  187.9 1.6 collective-permute-start.80
  190.4 3.3 shard_map.363
  195.5 13.6 %shard_map.361 = (bf16[128,1536]{1,0:T(8,128)(2,1)}, bf16[128,1536]{1,0:T(8,128)(2,1)}, bf16[128,1536]{1,0:T(8,128)(2,1)}, bf16[128,1536]{1,0:T(8,128)(2,1)}, bf...) custom-call(s32[9]{0:T(128)} %stack.48.starts_ref, ...), custom_call_target="tpu_custom_call" | custom-call | tf_op jit(solution)/shard_map/pallas_call | solution.py:473
  209.2 14.4 %shard_map.362 = (bf16[128,1664]{1,0:T(8,128)(2,1)}, bf16[128,1664]{1,0:T(8,128)(2,1)}, bf16[128,1664]{1,0:T(8,128)(2,1)}, bf16[128,1664]{1,0:T(8,128)(2,1)}, bf...) custom-call(s32[9]{0:T(128)} %stack.48.starts_ref, ...), custom_call_target="tpu_custom_call" | custom-call | tf_op jit(solution)/shard_map/pallas_call | solution.py:473
  224.6 5.3 %collective-permute-start.70 = (bf16[64,1024]{1,0:T(8,128)(2,1)}, bf16[64,1024]{1,0:T(8,128)(2,1)S(1)}, u32[]{:S(2)}, u32[]{:S(2)}) collective-permute-start(bf16[64,1024]{1,0:T(8,128)(2,1)} %get-tuple-element.158), channel_id=1, source_target_pairs={{0,2},{2,0},{4,6},{6,4},{8,10},{10,8},{12,14},{14,12},{16,18},{18,... | collective-permute-start | bytes 393224 | tf_op jit(solution)/shard_map/ppermute | solution.py:658
  229.8 1.7 multiply_convert_fusion
  235.2 2.0 add_convert_fusion.10
  240.5 6.5 %collective-permute-done.43 = bf16[128,1024]{1,0:T(8,128)(2,1)S(1)} collective-permute-done((bf16[128,1024]{1,0:T(8,128)(2,1)S(1)}, bf16[128,1024]{1,0:T(8,128)(2,1)S(1)}, u32[]{:S(2)}, u32[]{:S(2)}) %collective-permute-start.43) | collective-permute-done | bytes 262176 | tf_op jit(solution)/shard_map/ppermute | solution.py:787
  248.1 2.0 concatenate.183
  251.7 2.4 collective-permute-start.59
  255.0 1.7 fusion.9
  258.2 3.5 collective-permute-done.61
  262.7 7.9 %collective-permute-done.45 = bf16[64,1664]{1,0:T(8,128)(2,1)S(1)} collective-permute-done((bf16[64,1664]{1,0:T(8,128)(2,1)S(1)}, bf16[64,1664]{1,0:T(8,128)(2,1)S(1)}, u32[]{:S(2)}, u32[]{:S(2)}) %collective-permute-start.45) | collective-permute-done | bytes 213024 | tf_op jit(solution)/shard_map/ppermute | solution.py:655
  271.0 2.4 collective-permute-start.46
  276.1 2.6 collective-permute-start.58
  282.4 7.3 %collective-permute-done.73 = bf16[128,1024]{1,0:T(8,128)(2,1)S(1)} collective-permute-done((bf16[128,1024]{1,0:T(8,128)(2,1)S(1)}, bf16[128,1024]{1,0:T(8,128)(2,1)S(1)}, u32[]{:S(2)}, u32[]{:S(2)}) %collective-permute-start.73) | collective-permute-done | bytes 262176 | tf_op jit(solution)/shard_map/ppermute | solution.py:655
  291.3 6.8 %collective-permute-done.48 = bf16[128,1664]{1,0:T(8,128)(2,1)S(1)} collective-permute-done((bf16[128,1664]{1,0:T(8,128)(2,1)S(1)}, bf16[128,1664]{1,0:T(8,128)(2,1)S(1)}, u32[]{:S(2)}, u32[]{:S(2)}) %collective-permute-start.48) | collective-permute-done | bytes 426016 | tf_op jit(solution)/shard_map/ppermute | solution.py:655
  298.9 13.4 %collective-permute-done.92 = bf16[128,1408]{1,0:T(8,128)(2,1)S(1)} collective-permute-done((bf16[128,1408]{1,0:T(8,128)(2,1)S(1)}, bf16[128,1408]{1,0:T(8,128)(2,1)S(1)}, u32[]{:S(2)}, u32[]{:S(2)}) %collective-permute-start.92) | collective-permute-done | bytes 360480 | tf_op jit(solution)/shard_map/ppermute | solution.py:655
  313.1 2.3 collective-permute-done.49
  315.5 3.3 collective-permute-start.57
  319.8 4.5 %collective-permute-done.74 = bf16[128,1024]{1,0:T(8,128)(2,1)S(1)} collective-permute-done((bf16[128,1024]{1,0:T(8,128)(2,1)S(1)}, bf16[128,1024]{1,0:T(8,128)(2,1)S(1)}, u32[]{:S(2)}, u32[]{:S(2)}) %collective-permute-start.74) | collective-permute-done | bytes 262176 | tf_op jit(solution)/shard_map/ppermute | solution.py:655
  331.8 1.7 collective-permute-done.51
  335.2 9.8 %collective-permute-done.52 = f32[16,1024]{1,0:T(8,128)S(1)} collective-permute-done((f32[16,1024]{1,0:T(8,128)S(1)}, f32[16,1024]{1,0:T(8,128)S(1)}, u32[]{:S(2)}, u32[]{:S(2)}) %collective-permute-start.52) | collective-permute-done | bytes 65568 | tf_op jit(solution)/shard_map/ppermute | solution.py:667
  345.6 2.7 collective-permute-start.65
  348.7 1.3 collective-permute-done.54
  350.6 3.0 collective-permute-start.66
  353.5 5.2 %collective-permute-done.55 = f32[16,1024]{1,0:T(8,128)S(1)} collective-permute-done((f32[16,1024]{1,0:T(8,128)S(1)}, f32[16,1024]{1,0:T(8,128)S(1)}, u32[]{:S(2)}, u32[]{:S(2)}) %collective-permute-start.55) | collective-permute-done | bytes 65568 | tf_op jit(solution)/shard_map/ppermute | solution.py:667
  359.2 2.7 collective-permute-done.56
  365.4 4.6 %collective-permute-start.84 = (bf16[64,2816]{1,0:T(8,128)(2,1)S(1)}, bf16[64,2816]{1,0:T(8,128)(2,1)S(1)}, u32[]{:S(2)}, u32[]{:S(2)}) collective-permute-start(bf16[64,2816]{1,0:T(8,128)(2,1)S(1)} %dynamic-slice_convert_fusion), channel_id=1, source_target_pairs={{0,2},{2,0},{4,6},{6,4},{8,10},{10,8},{12,14},{14,12},{16,18},{18,... | collective-permute-start | bytes 1081352 | tf_op jit(solution)/shard_map/ppermute | solution.py:658
  (425 shorter events, 97.0 us)
Async XLA Ops:
  10.2 11.5 %collective-permute-start.2 = (bf16[128,3200]{1,0:T(8,128)(2,1)S(1)}, bf16[128,3200]{1,0:T(8,128)(2,1)S(1)}, u32[]{:S(2)}, u32[]{:S(2)}) collective-permute-start(bf16[128,3200]{1,0:T(8,128)(2,1)S(1)} %maximum_select_fusion.refs_0_), channel_id=1, source_target_pairs={{0,8},{8,16},{16,24},{24,28},{28,20},{20,12},{12,4},{4,0},{10,2},{... | collective-permute-start | bytes 2457608 | tf_op jit(solution)/shard_map/ppermute | solution.py:655
  21.8 11.5 %collective-permute-start.3 = (bf16[128,3200]{1,0:T(8,128)(2,1)S(1)}, bf16[128,3200]{1,0:T(8,128)(2,1)S(1)}, u32[]{:S(2)}, u32[]{:S(2)}) collective-permute-start(bf16[128,3200]{1,0:T(8,128)(2,1)S(1)} %collective-permute-done.2.refs_1_), channel_id=1, source_target_pairs={{0,8},{8,16},{16,24},{24,28},{28,20},{20,12},{12,4},{4,0},{10,2},{... | collective-permute-start | bytes 2457608 | tf_op jit(solution)/shard_map/ppermute | solution.py:655
  35.3 15.7 %collective-permute-start.4 = (bf16[128,3200]{1,0:T(8,128)(2,1)S(1)}, bf16[128,3200]{1,0:T(8,128)(2,1)S(1)}, u32[]{:S(2)}, u32[]{:S(2)}) collective-permute-start(bf16[128,3200]{1,0:T(8,128)(2,1)S(1)} %collective-permute-done.3.refs_2_), channel_id=1, source_target_pairs={{0,8},{8,16},{16,24},{24,28},{28,20},{20,12},{12,4},{4,0},{10,2},{... | collective-permute-start | bytes 2457608 | tf_op jit(solution)/shard_map/ppermute | solution.py:655
  37.5 23.2 %collective-permute-start = (bf16[128,1024]{1,0:T(8,128)(2,1)}, bf16[128,1024]{1,0:T(8,128)(2,1)}, u32[]{:S(2)}, u32[]{:S(2)}) collective-permute-start(bf16[128,1024]{1,0:T(8,128)(2,1)} %fusion.4), channel_id=1, source_target_pairs={{0,1},{1,0},{2,3},{3,2},{4,5},{5,4},{6,7},{7,6},{8,9},{9,8},{10,11... | collective-permute-start | bytes 786440 | tf_op jit(solution)/shard_map/ppermute | solution.py:760
  39.5 10.3 %collective-permute-start.11 = (bf16[128,1024]{1,0:T(8,128)(2,1)}, bf16[128,1024]{1,0:T(8,128)(2,1)}, u32[]{:S(2)}, u32[]{:S(2)}) collective-permute-start(bf16[128,1024]{1,0:T(8,128)(2,1)} %maximum_select_fusion.7.refs_0_.refs_9_), channel_id=1, source_target_pairs={{0,8},{8,16},{16,24},{24,28},{28,20},{20,12},{12,4},{4,0},{10,2},{... | collective-permute-start | bytes 786440 | tf_op jit(solution)/shard_map/ppermute | solution.py:655
  41.5 20.5 %collective-permute-start.5 = (bf16[128,3200]{1,0:T(8,128)(2,1)S(1)}, bf16[128,3200]{1,0:T(8,128)(2,1)}, u32[]{:S(2)}, u32[]{:S(2)}) collective-permute-start(bf16[128,3200]{1,0:T(8,128)(2,1)S(1)} %collective-permute-done.2.refs_1_), channel_id=1, source_target_pairs={{0,2},{2,0},{4,6},{6,4},{8,10},{10,8},{12,14},{14,12},{16,18},{18,... | collective-permute-start | bytes 2457608 | tf_op jit(solution)/shard_map/ppermute | solution.py:658
  42.2 31.5 %collective-permute-start.6 = (bf16[128,3200]{1,0:T(8,128)(2,1)S(1)}, bf16[128,3200]{1,0:T(8,128)(2,1)}, u32[]{:S(2)}, u32[]{:S(2)}) collective-permute-start(bf16[128,3200]{1,0:T(8,128)(2,1)S(1)} %collective-permute-done.3.refs_2_), channel_id=1, source_target_pairs={{0,2},{2,0},{4,6},{6,4},{8,10},{10,8},{12,14},{14,12},{16,18},{18,... | collective-permute-start | bytes 2457608 | tf_op jit(solution)/shard_map/ppermute | solution.py:658
  57.3 9.3 %collective-permute-start.13 = (bf16[128,1024]{1,0:T(8,128)(2,1)}, bf16[128,1024]{1,0:T(8,128)(2,1)}, u32[]{:S(2)}, u32[]{:S(2)}) collective-permute-start(bf16[128,1024]{1,0:T(8,128)(2,1)} %collective-permute-done.12.refs_2_.refs_11_), channel_id=1, source_target_pairs={{0,8},{8,16},{16,24},{24,28},{28,20},{20,12},{12,4},{4,0},{10,2},{... | collective-permute-start | bytes 786440 | tf_op jit(solution)/shard_map/ppermute | solution.py:655
  60.7 7.5 %collective-permute-start.8 = (bf16[64,3200]{1,0:T(8,128)(2,1)}, bf16[64,3200]{1,0:T(8,128)(2,1)}, u32[]{:S(2)}, u32[]{:S(2)}) collective-permute-start(bf16[64,3200]{1,0:T(8,128)(2,1)} %constant_dynamic-slice_fusion.3), channel_id=1, source_target_pairs={{0,8},{8,16},{16,24},{24,28},{28,20},{20,12},{12,4},{4,0},{10,2},{... | collective-permute-start | bytes 1228808 | tf_op jit(solution)/shard_map/ppermute | solution.py:655
  62.1 12.2 %collective-permute-start.7 = (bf16[128,3200]{1,0:T(8,128)(2,1)S(1)}, bf16[128,3200]{1,0:T(8,128)(2,1)S(1)}, u32[]{:S(2)}, u32[]{:S(2)}) collective-permute-start(bf16[128,3200]{1,0:T(8,128)(2,1)S(1)} %collective-permute-done.4.refs_3_), channel_id=1, source_target_pairs={{0,2},{2,0},{4,6},{6,4},{8,10},{10,8},{12,14},{14,12},{16,18},{18,... | collective-permute-start | bytes 2457608 | tf_op jit(solution)/shard_map/ppermute | solution.py:658
  62.1 13.8 %collective-permute-start.23 = (bf16[128,2816]{1,0:T(8,128)(2,1)}, bf16[128,2816]{1,0:T(8,128)(2,1)}, u32[]{:S(2)}, u32[]{:S(2)}) collective-permute-start(bf16[128,2816]{1,0:T(8,128)(2,1)} %maximum_select_fusion.1.refs_0_), channel_id=1, source_target_pairs={{0,8},{8,16},{16,24},{24,28},{28,20},{20,12},{12,4},{4,0},{10,2},{... | collective-permute-start | bytes 2162696 | tf_op jit(solution)/shard_map/ppermute | solution.py:655
  71.2 18.0 %collective-permute-start.17 = (bf16[64,1024]{1,0:T(8,128)(2,1)}, bf16[64,1024]{1,0:T(8,128)(2,1)}, u32[]{:S(2)}, u32[]{:S(2)}) collective-permute-start(bf16[64,1024]{1,0:T(8,128)(2,1)} %constant_dynamic-slice_fusion.2), channel_id=1, source_target_pairs={{0,8},{8,16},{16,24},{24,28},{28,20},{20,12},{12,4},{4,0},{10,2},{... | collective-permute-start | bytes 393224 | tf_op jit(solution)/shard_map/ppermute | solution.py:655
  73.6 28.7 %collective-permute-start.15 = (bf16[128,1024]{1,0:T(8,128)(2,1)}, bf16[128,1024]{1,0:T(8,128)(2,1)S(1)}, u32[]{:S(2)}, u32[]{:S(2)}) collective-permute-start(bf16[128,1024]{1,0:T(8,128)(2,1)} %collective-permute-done.12.refs_2_.refs_11_), channel_id=1, source_target_pairs={{0,2},{2,0},{4,6},{6,4},{8,10},{10,8},{12,14},{14,12},{16,18},{18,... | collective-permute-start | bytes 786440 | tf_op jit(solution)/shard_map/ppermute | solution.py:658
  73.9 28.4 %collective-permute-start.16 = (bf16[128,1024]{1,0:T(8,128)(2,1)}, bf16[128,1024]{1,0:T(8,128)(2,1)}, u32[]{:S(2)}, u32[]{:S(2)}) collective-permute-start(bf16[128,1024]{1,0:T(8,128)(2,1)} %collective-permute-done.13.refs_3_.refs_12_), channel_id=1, source_target_pairs={{0,2},{2,0},{4,6},{6,4},{8,10},{10,8},{12,14},{14,12},{16,18},{18,... | collective-permute-start | bytes 786440 | tf_op jit(solution)/shard_map/ppermute | solution.py:658
  74.2 27.0 %collective-permute-start.32 = (bf16[128,1408]{1,0:T(8,128)(2,1)S(1)}, bf16[128,1408]{1,0:T(8,128)(2,1)}, u32[]{:S(2)}, u32[]{:S(2)}) collective-permute-start(bf16[128,1408]{1,0:T(8,128)(2,1)S(1)} %maximum_select_fusion.6.refs_9_.refs_0_), channel_id=1, source_target_pairs={{0,8},{8,16},{16,24},{24,28},{28,20},{20,12},{12,4},{4,0},{10,2},{... | collective-permute-start | bytes 1081352 | tf_op jit(solution)/shard_map/ppermute | solution.py:655
  75.9 42.5 %collective-permute-start.24 = (bf16[128,2816]{1,0:T(8,128)(2,1)}, bf16[128,2816]{1,0:T(8,128)(2,1)}, u32[]{:S(2)}, u32[]{:S(2)}) collective-permute-start(bf16[128,2816]{1,0:T(8,128)(2,1)} %collective-permute-done.23.refs_1_), channel_id=1, source_target_pairs={{0,8},{8,16},{16,24},{24,28},{28,20},{20,12},{12,4},{4,0},{10,2},{... | collective-permute-start | bytes 2162696 | tf_op jit(solution)/shard_map/ppermute | solution.py:655
  89.2 13.1 %collective-permute-start.18 = (bf16[64,1024]{1,0:T(8,128)(2,1)}, bf16[64,1024]{1,0:T(8,128)(2,1)S(1)}, u32[]{:S(2)}, u32[]{:S(2)}) collective-permute-start(bf16[64,1024]{1,0:T(8,128)(2,1)} %collective-permute-done.17.refs_7_.refs_16_), channel_id=1, source_target_pairs={{0,2},{2,0},{4,6},{6,4},{8,10},{10,8},{12,14},{14,12},{16,18},{18,... | collective-permute-start | bytes 393224 | tf_op jit(solution)/shard_map/ppermute | solution.py:658
  101.3 10.2 %collective-permute-start.33 = (bf16[128,1408]{1,0:T(8,128)(2,1)}, bf16[128,1408]{1,0:T(8,128)(2,1)S(1)}, u32[]{:S(2)}, u32[]{:S(2)}) collective-permute-start(bf16[128,1408]{1,0:T(8,128)(2,1)} %collective-permute-done.32.refs_10_.refs_1_), channel_id=1, source_target_pairs={{0,8},{8,16},{16,24},{24,28},{28,20},{20,12},{12,4},{4,0},{10,2},{... | collective-permute-start | bytes 1081352 | tf_op jit(solution)/shard_map/ppermute | solution.py:655
  109.0 21.9 %collective-permute-start.21 = (bf16[128,1024]{1,0:T(8,128)(2,1)S(1)}, bf16[128,1024]{1,0:T(8,128)(2,1)}, u32[]{:S(2)}, u32[]{:S(2)}) collective-permute-start(bf16[128,1024]{1,0:T(8,128)(2,1)S(1)} %fusion.12), channel_id=1, source_target_pairs={{0,1},{1,0},{2,3},{3,2},{4,5},{5,4},{6,7},{7,6},{8,9},{9,8},{10,11... | collective-permute-start | bytes 786440 | tf_op jit(solution)/shard_map/ppermute | solution.py:760
  110.3 21.0 %collective-permute-start.35 = (bf16[128,1408]{1,0:T(8,128)(2,1)}, bf16[128,1408]{1,0:T(8,128)(2,1)S(1)}, u32[]{:S(2)}, u32[]{:S(2)}) collective-permute-start(bf16[128,1408]{1,0:T(8,128)(2,1)} %collective-permute-done.32.refs_10_.refs_1_), channel_id=1, source_target_pairs={{0,2},{2,0},{4,6},{6,4},{8,10},{10,8},{12,14},{14,12},{16,18},{18,... | collective-permute-start | bytes 1081352 | tf_op jit(solution)/shard_map/ppermute | solution.py:658
  111.5 8.9 %collective-permute-start.34 = (bf16[128,1408]{1,0:T(8,128)(2,1)S(1)}, bf16[128,1408]{1,0:T(8,128)(2,1)S(1)}, u32[]{:S(2)}, u32[]{:S(2)}) collective-permute-start(bf16[128,1408]{1,0:T(8,128)(2,1)S(1)} %collective-permute-done.33.refs_11_.refs_2_), channel_id=1, source_target_pairs={{0,8},{8,16},{16,24},{24,28},{28,20},{20,12},{12,4},{4,0},{10,2},{... | collective-permute-start | bytes 1081352 | tf_op jit(solution)/shard_map/ppermute | solution.py:655
  115.9 16.7 %collective-permute-start.36 = (bf16[128,1408]{1,0:T(8,128)(2,1)S(1)}, bf16[128,1408]{1,0:T(8,128)(2,1)S(1)}, u32[]{:S(2)}, u32[]{:S(2)}) collective-permute-start(bf16[128,1408]{1,0:T(8,128)(2,1)S(1)} %collective-permute-done.33.refs_11_.refs_2_), channel_id=1, source_target_pairs={{0,2},{2,0},{4,6},{6,4},{8,10},{10,8},{12,14},{14,12},{16,18},{18,... | collective-permute-start | bytes 1081352 | tf_op jit(solution)/shard_map/ppermute | solution.py:658
  118.4 10.8 %collective-permute-start.25 = (bf16[128,2816]{1,0:T(8,128)(2,1)}, bf16[128,2816]{1,0:T(8,128)(2,1)S(1)}, u32[]{:S(2)}, u32[]{:S(2)}) collective-permute-start(bf16[128,2816]{1,0:T(8,128)(2,1)} %collective-permute-done.24.refs_2_), channel_id=1, source_target_pairs={{0,8},{8,16},{16,24},{24,28},{28,20},{20,12},{12,4},{4,0},{10,2},{... | collective-permute-start | bytes 2162696 | tf_op jit(solution)/shard_map/ppermute | solution.py:655
  120.4 12.3 %collective-permute-start.20 = (bf16[128,1024]{1,0:T(8,128)(2,1)S(1)}, bf16[128,1024]{1,0:T(8,128)(2,1)S(1)}, u32[]{:S(2)}, u32[]{:S(2)}) collective-permute-start(bf16[128,1024]{1,0:T(8,128)(2,1)S(1)} %multiply_convert_fusion.1), channel_id=1, source_target_pairs={{0,1},{1,0},{2,3},{3,2},{4,5},{5,4},{6,7},{7,6},{8,9},{9,8},{10,11... | collective-permute-start | bytes 786440 | tf_op jit(solution)/shard_map/ppermute | solution.py:760
  129.3 14.0 %collective-permute-start.26 = (bf16[128,2816]{1,0:T(8,128)(2,1)}, bf16[128,2816]{1,0:T(8,128)(2,1)S(1)}, u32[]{:S(2)}, u32[]{:S(2)}) collective-permute-start(bf16[128,2816]{1,0:T(8,128)(2,1)} %collective-permute-done.23.refs_1_), channel_id=1, source_target_pairs={{0,2},{2,0},{4,6},{6,4},{8,10},{10,8},{12,14},{14,12},{16,18},{18,... | collective-permute-start | bytes 2162696 | tf_op jit(solution)/shard_map/ppermute | solution.py:658
  131.3 12.1 %collective-permute-start.27 = (bf16[128,2816]{1,0:T(8,128)(2,1)}, bf16[128,2816]{1,0:T(8,128)(2,1)S(1)}, u32[]{:S(2)}, u32[]{:S(2)}) collective-permute-start(bf16[128,2816]{1,0:T(8,128)(2,1)} %collective-permute-done.24.refs_2_), channel_id=1, source_target_pairs={{0,2},{2,0},{4,6},{6,4},{8,10},{10,8},{12,14},{14,12},{16,18},{18,... | collective-permute-start | bytes 2162696 | tf_op jit(solution)/shard_map/ppermute | solution.py:658
  132.7 10.6 %collective-permute-start.28 = (bf16[128,2816]{1,0:T(8,128)(2,1)S(1)}, bf16[128,2816]{1,0:T(8,128)(2,1)S(1)}, u32[]{:S(2)}, u32[]{:S(2)}) collective-permute-start(bf16[128,2816]{1,0:T(8,128)(2,1)S(1)} %collective-permute-done.25.refs_3_), channel_id=1, source_target_pairs={{0,2},{2,0},{4,6},{6,4},{8,10},{10,8},{12,14},{14,12},{16,18},{18,... | collective-permute-start | bytes 2162696 | tf_op jit(solution)/shard_map/ppermute | solution.py:658
  159.2 22.4 %collective-permute-start.87 = (bf16[128,1408]{1,0:T(8,128)(2,1)}, bf16[128,1408]{1,0:T(8,128)(2,1)}, u32[]{:S(2)}, u32[]{:S(2)}) collective-permute-start(bf16[128,1408]{1,0:T(8,128)(2,1)} %get-tuple-element.175), channel_id=1, source_target_pairs={{0,2},{2,0},{4,6},{6,4},{8,10},{10,8},{12,14},{14,12},{16,18},{18,... | collective-permute-start | bytes 1081352 | tf_op jit(solution)/shard_map/ppermute | solution.py:658
  159.6 75.0 %collective-permute-start.86 = (bf16[128,1408]{1,0:T(8,128)(2,1)}, bf16[128,1408]{1,0:T(8,128)(2,1)}, u32[]{:S(2)}, u32[]{:S(2)}) collective-permute-start(bf16[128,1408]{1,0:T(8,128)(2,1)} %get-tuple-element.173), channel_id=1, source_target_pairs={{0,2},{2,0},{4,6},{6,4},{8,10},{10,8},{12,14},{14,12},{16,18},{18,... | collective-permute-start | bytes 1081352 | tf_op jit(solution)/shard_map/ppermute | solution.py:658
  159.7 120.1 %collective-permute-start.85 = (bf16[128,1408]{1,0:T(8,128)(2,1)}, bf16[128,1408]{1,0:T(8,128)(2,1)}, u32[]{:S(2)}, u32[]{:S(2)}) collective-permute-start(bf16[128,1408]{1,0:T(8,128)(2,1)} %get-tuple-element.171), channel_id=1, source_target_pairs={{0,2},{2,0},{4,6},{6,4},{8,10},{10,8},{12,14},{14,12},{16,18},{18,... | collective-permute-start | bytes 1081352 | tf_op jit(solution)/shard_map/ppermute | solution.py:658
  165.9 18.8 %collective-permute-start.79 = (bf16[64,2816]{1,0:T(8,128)(2,1)}, bf16[64,2816]{1,0:T(8,128)(2,1)}, u32[]{:S(2)}, u32[]{:S(2)}) collective-permute-start(bf16[64,2816]{1,0:T(8,128)(2,1)} %get-tuple-element.168), channel_id=1, source_target_pairs={{0,2},{2,0},{4,6},{6,4},{8,10},{10,8},{12,14},{14,12},{16,18},{18,... | collective-permute-start | bytes 1081352 | tf_op jit(solution)/shard_map/ppermute | solution.py:658
  166.1 7.5 %collective-permute-start.40 = (bf16[128,1024]{1,0:T(8,128)(2,1)S(1)}, bf16[128,1024]{1,0:T(8,128)(2,1)S(1)}, u32[]{:S(2)}, u32[]{:S(2)}) collective-permute-start(bf16[128,1024]{1,0:T(8,128)(2,1)S(1)} %dynamic-slice_convert_fusion.3), channel_id=1, source_target_pairs={{0,1},{1,0},{2,3},{3,2},{4,5},{5,4},{6,7},{7,6},{8,9},{9,8},{10,11... | collective-permute-start | bytes 786440 | tf_op jit(solution)/shard_map/ppermute | solution.py:787
  173.6 7.7 %collective-permute-start.89 = (bf16[64,1408]{1,0:T(8,128)(2,1)S(1)}, bf16[64,1408]{1,0:T(8,128)(2,1)S(1)}, u32[]{:S(2)}, u32[]{:S(2)}) collective-permute-start(bf16[64,1408]{1,0:T(8,128)(2,1)S(1)} %add_convert_fusion.18), channel_id=1, source_target_pairs={{0,8},{8,16},{16,24},{24,28},{28,20},{20,12},{12,4},{4,0},{10,2},{... | collective-permute-start | bytes 540680 | tf_op jit(solution)/shard_map/ppermute | solution.py:655
  181.6 42.9 %collective-permute-start.41 = (bf16[128,1024]{1,0:T(8,128)(2,1)}, bf16[128,1024]{1,0:T(8,128)(2,1)}, u32[]{:S(2)}, u32[]{:S(2)}) collective-permute-start(bf16[128,1024]{1,0:T(8,128)(2,1)} %dynamic-slice_convert_fusion.2), channel_id=1, source_target_pairs={{0,1},{1,0},{2,3},{3,2},{4,5},{5,4},{6,7},{7,6},{8,9},{9,8},{10,11... | collective-permute-start | bytes 786440 | tf_op jit(solution)/shard_map/ppermute | solution.py:787
  184.8 50.0 %collective-permute-start.90 = (bf16[128,1408]{1,0:T(8,128)(2,1)}, bf16[128,1408]{1,0:T(8,128)(2,1)}, u32[]{:S(2)}, u32[]{:S(2)}) collective-permute-start(bf16[128,1408]{1,0:T(8,128)(2,1)} %add_convert_fusion.11), channel_id=1, source_target_pairs={{0,8},{8,16},{16,24},{24,28},{28,20},{20,12},{12,4},{4,0},{10,2},{... | collective-permute-start | bytes 1081352 | tf_op jit(solution)/shard_map/ppermute | solution.py:655
  187.9 45.3 %collective-permute-start.80 = (bf16[64,2816]{1,0:T(8,128)(2,1)}, bf16[64,2816]{1,0:T(8,128)(2,1)}, u32[]{:S(2)}, u32[]{:S(2)}) collective-permute-start(bf16[64,2816]{1,0:T(8,128)(2,1)} %add_convert_fusion.12), channel_id=1, source_target_pairs={{0,8},{8,16},{16,24},{24,28},{28,20},{20,12},{12,4},{4,0},{10,2},{... | collective-permute-start | bytes 1081352 | tf_op jit(solution)/shard_map/ppermute | solution.py:655
  224.6 7.7 %collective-permute-start.70 = (bf16[64,1024]{1,0:T(8,128)(2,1)}, bf16[64,1024]{1,0:T(8,128)(2,1)S(1)}, u32[]{:S(2)}, u32[]{:S(2)}) collective-permute-start(bf16[64,1024]{1,0:T(8,128)(2,1)} %get-tuple-element.158), channel_id=1, source_target_pairs={{0,2},{2,0},{4,6},{6,4},{8,10},{10,8},{12,14},{14,12},{16,18},{18,... | collective-permute-start | bytes 393224 | tf_op jit(solution)/shard_map/ppermute | solution.py:658
  233.2 23.6 %collective-permute-start.69 = (bf16[128,1024]{1,0:T(8,128)(2,1)}, bf16[128,1024]{1,0:T(8,128)(2,1)}, u32[]{:S(2)}, u32[]{:S(2)}) collective-permute-start(bf16[128,1024]{1,0:T(8,128)(2,1)} %get-tuple-element.156), channel_id=1, source_target_pairs={{0,2},{2,0},{4,6},{6,4},{8,10},{10,8},{12,14},{14,12},{16,18},{18,... | collective-permute-start | bytes 786440 | tf_op jit(solution)/shard_map/ppermute | solution.py:658
  234.6 40.0 %collective-permute-start.68 = (bf16[128,1024]{1,0:T(8,128)(2,1)}, bf16[128,1024]{1,0:T(8,128)(2,1)}, u32[]{:S(2)}, u32[]{:S(2)}) collective-permute-start(bf16[128,1024]{1,0:T(8,128)(2,1)} %get-tuple-element.154), channel_id=1, source_target_pairs={{0,2},{2,0},{4,6},{6,4},{8,10},{10,8},{12,14},{14,12},{16,18},{18,... | collective-permute-start | bytes 786440 | tf_op jit(solution)/shard_map/ppermute | solution.py:658
  238.6 32.4 %collective-permute-start.47 = (bf16[128,1664]{1,0:T(8,128)(2,1)}, bf16[128,1664]{1,0:T(8,128)(2,1)S(1)}, u32[]{:S(2)}, u32[]{:S(2)}) collective-permute-start(bf16[128,1664]{1,0:T(8,128)(2,1)} %get-tuple-element.132), channel_id=1, source_target_pairs={{0,2},{2,0},{4,6},{6,4},{8,10},{10,8},{12,14},{14,12},{16,18},{18,... | collective-permute-start | bytes 1277960 | tf_op jit(solution)/shard_map/ppermute | solution.py:658
  239.5 7.5 %collective-permute-start.43 = (bf16[128,1024]{1,0:T(8,128)(2,1)S(1)}, bf16[128,1024]{1,0:T(8,128)(2,1)S(1)}, u32[]{:S(2)}, u32[]{:S(2)}) collective-permute-start(bf16[128,1024]{1,0:T(8,128)(2,1)S(1)} %dynamic-slice_convert_fusion.1), channel_id=1, source_target_pairs={{0,1},{1,0},{2,3},{3,2},{4,5},{5,4},{6,7},{7,6},{8,9},{9,8},{10,11... | collective-permute-start | bytes 786440 | tf_op jit(solution)/shard_map/ppermute | solution.py:787
  251.7 10.4 %collective-permute-start.59 = (bf16[128,1536]{1,0:T(8,128)(2,1)}, bf16[128,1536]{1,0:T(8,128)(2,1)S(1)}, u32[]{:S(2)}, u32[]{:S(2)}) collective-permute-start(bf16[128,1536]{1,0:T(8,128)(2,1)} %get-tuple-element.146), channel_id=1, source_target_pairs={{0,2},{2,0},{4,6},{6,4},{8,10},{10,8},{12,14},{14,12},{16,18},{18,... | collective-permute-start | bytes 1179656 | tf_op jit(solution)/shard_map/ppermute | solution.py:658
  261.8 18.4 %collective-permute-start.91 = (bf16[128,1408]{1,0:T(8,128)(2,1)S(1)}, bf16[128,1408]{1,0:T(8,128)(2,1)S(1)}, u32[]{:S(2)}, u32[]{:S(2)}) collective-permute-start(bf16[128,1408]{1,0:T(8,128)(2,1)S(1)} %copy-done.43), channel_id=1, source_target_pairs={{0,8},{8,16},{16,24},{24,28},{28,20},{20,12},{12,4},{4,0},{10,2},{... | collective-permute-start | bytes 1081352 | tf_op jit(solution)/shard_map/ppermute | solution.py:655
  262.2 8.5 %collective-permute-start.45 = (bf16[64,1664]{1,0:T(8,128)(2,1)S(1)}, bf16[64,1664]{1,0:T(8,128)(2,1)S(1)}, u32[]{:S(2)}, u32[]{:S(2)}) collective-permute-start(bf16[64,1664]{1,0:T(8,128)(2,1)S(1)} %copy-done.51), channel_id=1, source_target_pairs={{0,8},{8,16},{16,24},{24,28},{28,20},{20,12},{12,4},{4,0},{10,2},{... | collective-permute-start | bytes 638984 | tf_op jit(solution)/shard_map/ppermute | solution.py:655
  274.3 44.5 %collective-permute-start.77 = (bf16[128,2816]{1,0:T(8,128)(2,1)S(1)}, bf16[128,2816]{1,0:T(8,128)(2,1)S(1)}, u32[]{:S(2)}, u32[]{:S(2)}) collective-permute-start(bf16[128,2816]{1,0:T(8,128)(2,1)S(1)} %copy-done.74), channel_id=1, source_target_pairs={{0,2},{2,0},{4,6},{6,4},{8,10},{10,8},{12,14},{14,12},{16,18},{18,... | collective-permute-start | bytes 2162696 | tf_op jit(solution)/shard_map/ppermute | solution.py:658
  276.1 14.5 %collective-permute-start.58 = (bf16[128,1536]{1,0:T(8,128)(2,1)S(1)}, bf16[128,1536]{1,0:T(8,128)(2,1)S(1)}, u32[]{:S(2)}, u32[]{:S(2)}) collective-permute-start(bf16[128,1536]{1,0:T(8,128)(2,1)S(1)} %copy-done.79), channel_id=1, source_target_pairs={{0,2},{2,0},{4,6},{6,4},{8,10},{10,8},{12,14},{14,12},{16,18},{18,... | collective-permute-start | bytes 1179656 | tf_op jit(solution)/shard_map/ppermute | solution.py:658
  279.8 10.9 %collective-permute-start.62 = (bf16[128,1536]{1,0:T(8,128)(2,1)S(1)}, bf16[128,1536]{1,0:T(8,128)(2,1)S(1)}, u32[]{:S(2)}, u32[]{:S(2)}) collective-permute-start(bf16[128,1536]{1,0:T(8,128)(2,1)S(1)} %add_convert_fusion.8), channel_id=1, source_target_pairs={{0,8},{8,16},{16,24},{24,28},{28,20},{20,12},{12,4},{4,0},{10,2},{... | collective-permute-start | bytes 1179656 | tf_op jit(solution)/shard_map/ppermute | solution.py:655
  280.2 9.4 %collective-permute-start.73 = (bf16[128,1024]{1,0:T(8,128)(2,1)S(1)}, bf16[128,1024]{1,0:T(8,128)(2,1)S(1)}, u32[]{:S(2)}, u32[]{:S(2)}) collective-permute-start(bf16[128,1024]{1,0:T(8,128)(2,1)S(1)} %add_convert_fusion.14), channel_id=1, source_target_pairs={{0,8},{8,16},{16,24},{24,28},{28,20},{20,12},{12,4},{4,0},{10,2},{... | collective-permute-start | bytes 786440 | tf_op jit(solution)/shard_map/ppermute | solution.py:655
  281.7 66.6 %collective-permute-start.76 = (bf16[128,2816]{1,0:T(8,128)(2,1)S(1)}, bf16[128,2816]{1,0:T(8,128)(2,1)S(1)}, u32[]{:S(2)}, u32[]{:S(2)}) collective-permute-start(bf16[128,2816]{1,0:T(8,128)(2,1)S(1)} %copy-done.73), channel_id=1, source_target_pairs={{0,2},{2,0},{4,6},{6,4},{8,10},{10,8},{12,14},{14,12},{16,18},{18,... | collective-permute-start | bytes 2162696 | tf_op jit(solution)/shard_map/ppermute | solution.py:658
  289.6 8.8 %collective-permute-start.50 = (bf16[128,1664]{1,0:T(8,128)(2,1)S(1)}, bf16[128,1664]{1,0:T(8,128)(2,1)S(1)}, u32[]{:S(2)}, u32[]{:S(2)}) collective-permute-start(bf16[128,1664]{1,0:T(8,128)(2,1)S(1)} %copy-done.77), channel_id=1, source_target_pairs={{0,2},{2,0},{4,6},{6,4},{8,10},{10,8},{12,14},{14,12},{16,18},{18,... | collective-permute-start | bytes 1277960 | tf_op jit(solution)/shard_map/ppermute | solution.py:658
  290.6 43.2 %collective-permute-start.53 = (bf16[128,1664]{1,0:T(8,128)(2,1)S(1)}, bf16[128,1664]{1,0:T(8,128)(2,1)S(1)}, u32[]{:S(2)}, u32[]{:S(2)}) collective-permute-start(bf16[128,1664]{1,0:T(8,128)(2,1)S(1)} %copy-done.76), channel_id=1, source_target_pairs={{0,2},{2,0},{4,6},{6,4},{8,10},{10,8},{12,14},{14,12},{16,18},{18,... | collective-permute-start | bytes 1277960 | tf_op jit(solution)/shard_map/ppermute | solution.py:658
  298.0 21.1 %collective-permute-start.81 = (bf16[128,2816]{1,0:T(8,128)(2,1)S(1)}, bf16[128,2816]{1,0:T(8,128)(2,1)S(1)}, u32[]{:S(2)}, u32[]{:S(2)}) collective-permute-start(bf16[128,2816]{1,0:T(8,128)(2,1)S(1)} %add_convert_fusion.2), channel_id=1, source_target_pairs={{0,8},{8,16},{16,24},{24,28},{28,20},{20,12},{12,4},{4,0},{10,2},{... | collective-permute-start | bytes 2162696 | tf_op jit(solution)/shard_map/ppermute | solution.py:655
  298.4 14.0 %collective-permute-start.92 = (bf16[128,1408]{1,0:T(8,128)(2,1)S(1)}, bf16[128,1408]{1,0:T(8,128)(2,1)S(1)}, u32[]{:S(2)}, u32[]{:S(2)}) collective-permute-start(bf16[128,1408]{1,0:T(8,128)(2,1)S(1)} %add_convert_fusion.9), channel_id=1, source_target_pairs={{0,8},{8,16},{16,24},{24,28},{28,20},{20,12},{12,4},{4,0},{10,2},{... | collective-permute-start | bytes 1081352 | tf_op jit(solution)/shard_map/ppermute | solution.py:655
  315.5 11.9 %collective-permute-start.57 = (bf16[128,1536]{1,0:T(8,128)(2,1)S(1)}, bf16[128,1536]{1,0:T(8,128)(2,1)S(1)}, u32[]{:S(2)}, u32[]{:S(2)}) collective-permute-start(bf16[128,1536]{1,0:T(8,128)(2,1)S(1)} %copy-done.78), channel_id=1, source_target_pairs={{0,2},{2,0},{4,6},{6,4},{8,10},{10,8},{12,14},{14,12},{16,18},{18,... | collective-permute-start | bytes 1179656 | tf_op jit(solution)/shard_map/ppermute | solution.py:658
  319.2 9.4 %collective-permute-start.63 = (bf16[128,1536]{1,0:T(8,128)(2,1)S(1)}, bf16[128,1536]{1,0:T(8,128)(2,1)S(1)}, u32[]{:S(2)}, u32[]{:S(2)}) collective-permute-start(bf16[128,1536]{1,0:T(8,128)(2,1)S(1)} %add_convert_fusion.7), channel_id=1, source_target_pairs={{0,8},{8,16},{16,24},{24,28},{28,20},{20,12},{12,4},{4,0},{10,2},{... | collective-permute-start | bytes 1179656 | tf_op jit(solution)/shard_map/ppermute | solution.py:655
  327.4 21.0 %collective-permute-start.82 = (bf16[128,2816]{1,0:T(8,128)(2,1)S(1)}, bf16[128,2816]{1,0:T(8,128)(2,1)S(1)}, u32[]{:S(2)}, u32[]{:S(2)}) collective-permute-start(bf16[128,2816]{1,0:T(8,128)(2,1)S(1)} %add_convert_fusion.1), channel_id=1, source_target_pairs={{0,8},{8,16},{16,24},{24,28},{28,20},{20,12},{12,4},{4,0},{10,2},{... | collective-permute-start | bytes 2162696 | tf_op jit(solution)/shard_map/ppermute | solution.py:655
  330.4 15.1 %collective-permute-start.64 = (bf16[128,1536]{1,0:T(8,128)(2,1)S(1)}, bf16[128,1536]{1,0:T(8,128)(2,1)S(1)}, u32[]{:S(2)}, u32[]{:S(2)}) collective-permute-start(bf16[128,1536]{1,0:T(8,128)(2,1)S(1)} %add_convert_fusion.6), channel_id=1, source_target_pairs={{0,8},{8,16},{16,24},{24,28},{28,20},{20,12},{12,4},{4,0},{10,2},{... | collective-permute-start | bytes 1179656 | tf_op jit(solution)/shard_map/ppermute | solution.py:655
  333.5 11.5 %collective-permute-start.52 = (f32[16,1024]{1,0:T(8,128)S(1)}, f32[16,1024]{1,0:T(8,128)S(1)}, u32[]{:S(2)}, u32[]{:S(2)}) collective-permute-start(f32[16,1024]{1,0:T(8,128)S(1)} %add.408), channel_id=1, source_target_pairs={{0,8},{2,10},{4,12},{6,14},{8,0},{10,2},{12,4},{14,6},{16,24},{18,... | collective-permute-start | bytes 196616 | tf_op jit(solution)/shard_map/ppermute | solution.py:667
  334.0 16.0 %collective-permute-start.54 = (bf16[128,1664]{1,0:T(8,128)(2,1)S(1)}, bf16[128,1664]{1,0:T(8,128)(2,1)S(1)}, u32[]{:S(2)}, u32[]{:S(2)}) collective-permute-start(bf16[128,1664]{1,0:T(8,128)(2,1)S(1)} %add_convert_fusion.3), channel_id=1, source_target_pairs={{0,8},{8,16},{16,24},{24,28},{28,20},{20,12},{12,4},{4,0},{10,2},{... | collective-permute-start | bytes 1277960 | tf_op jit(solution)/shard_map/ppermute | solution.py:655
  345.6 13.5 %collective-permute-start.65 = (bf16[64,1536]{1,0:T(8,128)(2,1)S(1)}, bf16[64,1536]{1,0:T(8,128)(2,1)S(1)}, u32[]{:S(2)}, u32[]{:S(2)}) collective-permute-start(bf16[64,1536]{1,0:T(8,128)(2,1)S(1)} %dynamic-slice_convert_fusion.6), channel_id=1, source_target_pairs={{0,2},{2,0},{4,6},{6,4},{8,10},{10,8},{12,14},{14,12},{16,18},{18,... | collective-permute-start | bytes 589832 | tf_op jit(solution)/shard_map/ppermute | solution.py:658
  348.6 16.5 %collective-permute-start.83 = (bf16[128,2816]{1,0:T(8,128)(2,1)S(1)}, bf16[128,2816]{1,0:T(8,128)(2,1)S(1)}, u32[]{:S(2)}, u32[]{:S(2)}) collective-permute-start(bf16[128,2816]{1,0:T(8,128)(2,1)S(1)} %add_convert_fusion), channel_id=1, source_target_pairs={{0,8},{8,16},{16,24},{24,28},{28,20},{20,12},{12,4},{4,0},{10,2},{... | collective-permute-start | bytes 2162696 | tf_op jit(solution)/shard_map/ppermute | solution.py:655
  350.0 8.7 %collective-permute-start.55 = (f32[16,1024]{1,0:T(8,128)S(1)}, f32[16,1024]{1,0:T(8,128)S(1)}, u32[]{:S(2)}, u32[]{:S(2)}) collective-permute-start(f32[16,1024]{1,0:T(8,128)S(1)} %add.411), channel_id=1, source_target_pairs={{0,16},{2,18},{4,20},{6,22},{8,24},{10,26},{12,28},{14,30},{16,0},... | collective-permute-start | bytes 196616 | tf_op jit(solution)/shard_map/ppermute | solution.py:667
  350.6 14.4 %collective-permute-start.66 = (bf16[64,1664]{1,0:T(8,128)(2,1)S(1)}, bf16[64,1664]{1,0:T(8,128)(2,1)S(1)}, u32[]{:S(2)}, u32[]{:S(2)}) collective-permute-start(bf16[64,1664]{1,0:T(8,128)(2,1)S(1)} %dynamic-slice_convert_fusion.5), channel_id=1, source_target_pairs={{0,2},{2,0},{4,6},{6,4},{8,10},{10,8},{12,14},{14,12},{16,18},{18,... | collective-permute-start | bytes 638984 | tf_op jit(solution)/shard_map/ppermute | solution.py:658
  365.4 7.5 %collective-permute-start.84 = (bf16[64,2816]{1,0:T(8,128)(2,1)S(1)}, bf16[64,2816]{1,0:T(8,128)(2,1)S(1)}, u32[]{:S(2)}, u32[]{:S(2)}) collective-permute-start(bf16[64,2816]{1,0:T(8,128)(2,1)S(1)} %dynamic-slice_convert_fusion), channel_id=1, source_target_pairs={{0,2},{2,0},{4,6},{6,4},{8,10},{10,8},{12,14},{14,12},{16,18},{18,... | collective-permute-start | bytes 1081352 | tf_op jit(solution)/shard_map/ppermute | solution.py:658
  (113 other events, 1182.1 us)

commit v3 on v2

--- a/solution.py
+++ b/solution.py
@@ -130,19 +130,33 @@
     return conv, sigma, act, inverse
 
 
-def fetch(pieces, starts_ref, target, sems, cols):
+def fetch(pieces, starts_ref, target, sems, segments):
     copies = []
-    for i, piece in enumerate(pieces):
-        rows = piece.shape[0]
-        start = pl.multiple_of(starts_ref[i], rows)
-        copies.append(
-            pltpu.make_async_copy(
-                piece.at[:, cols], target.at[pl.ds(start, rows), :], sems.at[i]
+    for j, (source, place, width) in enumerate(segments):
+        for i, piece in enumerate(pieces):
+            rows = piece.shape[0]
+            start = pl.multiple_of(starts_ref[i], rows)
+            copies.append(
+                pltpu.make_async_copy(
+                    piece.at[:, source : source + width],
+                    target.at[pl.ds(start, rows), place : place + width],
+                    sems.at[j, i],
+                )
             )
-        )
     for copy in copies:
         copy.start()
     return copies
+
+
+def proj_segments(group, groups, wide_key, wide_value):
+    key_cols = groups * wide_key
+    value_cols = groups * wide_value
+    return [
+        (group * wide_key, 0, wide_key),
+        (key_cols + group * wide_key, wide_key, wide_key),
+        (2 * key_cols + group * wide_value, 2 * wide_key, wide_value),
+        (2 * key_cols + value_cols + group * wide_value, 2 * wide_key + wide_value, wide_value),
+    ]
 
 
 def spill(chunks, starts_ref, source, sems):
@@ -161,12 +175,13 @@
         copy.wait()
 
 
-def outer(left_ref, right, target_ref):
+def outer(left_ref, right, target_ref, place):
+    cols = slice(place, place + right.shape[1])
     total = left_ref.shape[1]
     step = 256 if total % 256 == 0 else total
     for start in range(0, total, step):
         span = slice(start, start + step)
-        target_ref[span, :] = dot1(left_ref[:, span], right, "tn").astype(bf16)
+        target_ref[span, cols] = dot1(left_ref[:, span], right, "tn").astype(bf16)
 
 
 def head_cuts(local, per_step, key_dim, value_dim):
@@ -192,12 +207,13 @@
     pieces = refs[:count]
     proj_ref, small_ref, half_ref, mixed_ref, update_ref, inverse_ref = refs[count : count + 6]
     weight_ref, small_weight_ref, sems = refs[count + 6 :]
-    width = proj_ref.shape[1]
-    end = pieces[0].shape[1]
-    copies = fetch(
-        pieces, starts_ref, weight_ref, sems.at[0], slice(group * width, (group + 1) * width)
-    )
-    copies += fetch(pieces, starts_ref, small_weight_ref, sems.at[1], slice(end - LANES, end))
+    end = 2 * heads * (key_dim + value_dim)
+    segments = proj_segments(
+        group, heads // per_step, per_step * key_dim, per_step * value_dim
+    )
+    copies = fetch(pieces, starts_ref, weight_ref, sems.at[0:4], segments)
+    small_cols = [(end, 0, LANES)]
+    copies += fetch(pieces, starts_ref, small_weight_ref, sems.at[4:5], small_cols)
     wait_all(copies)
     small_ref[...] = dot1(x_ref[...], small_weight_ref[...])
     proj_ref[...] = dot1(x_ref[...], weight_ref[...])
@@ -280,29 +296,34 @@
 
 
 def backward_kernel(
-    heads, group, per_step, key_dim, value_dim, last, count, out_count,
+    heads, group, per_step, key_dim, value_dim, last, count,
     starts_ref, x_ref, grad_rows_ref, proj_ref, small_ref, lanes_ref,
     conv_query_ref, conv_key_ref, conv_value_ref, gain_ref,
-    mixed_ref, update_ref, inverse_ref, carry_ref, hidden_ref, *refs
+    mixed_ref, update_ref, inverse_ref, *refs
 ):
+    taken = refs[: 2 if group > 0 else heads // per_step]
+    refs = refs[len(taken) :]
     pieces = refs[:count]
-    out_pieces = refs[count : count + out_count]
-    refs = refs[count + out_count :]
+    refs = refs[count:]
     chunks = refs[:count]
     conv_query_out, conv_key_out, conv_value_out, gain_out, carry_out, lanes_out, hidden_out = refs[
         count : count + 7
     ]
-    weight_ref, out_weight_ref, grads_ref, sum_ref, sems = refs[count + 7 :]
+    weight_ref, out_weight_ref, grads_ref, sum_ref, sems, out_sems = refs[count + 7 :]
     width = grads_ref.shape[1]
     value_width = mixed_ref.shape[1]
     grouped = 2 * per_step * (key_dim + value_dim)
+    end = 2 * heads * (key_dim + value_dim)
     out_copies = fetch(
-        out_pieces, starts_ref, out_weight_ref, sems.at[0],
-        slice(group * value_width, (group + 1) * value_width),
-    )
-    copies = fetch(
-        pieces, starts_ref, weight_ref, sems.at[1], slice(group * grouped, group * grouped + width)
-    )
+        pieces, starts_ref, out_weight_ref, out_sems,
+        [(end + LANES + group * value_width, 0, value_width)],
+    )
+    segments = proj_segments(
+        group, heads // per_step, per_step * key_dim, per_step * value_dim
+    )
+    if last:
+        segments.append((end, grouped, LANES))
+    copies = fetch(pieces, starts_ref, weight_ref, sems, segments)
     wait_all(out_copies)
     grad_all = dot1(grad_rows_ref[...], out_weight_ref[...])
     length = proj_ref.shape[0]
@@ -316,7 +337,7 @@
         <= lax.broadcasted_iota(jnp.int32, (length, length), 1)
     ).astype(bf16)
 
-    carry = carry_ref[...]
+    carry = taken[0][...] if group > 0 else jnp.zeros(small.shape, f32)
     gain_sum = jnp.zeros((1, value_dim), f32)
     for local in range(per_step):
         head = group * per_step + local
@@ -413,54 +434,70 @@
     is_gate = lane >= heads
     grad_small = jnp.where(is_gate, carry * slope_all, carry * beta_all * (1.0 - beta_all))
     if last:
-        end = 2 * per_step * (key_dim + value_dim)
-        grads_ref[:, end : end + LANES] = jnp.where(lane < 2 * heads, grad_small, 0.0).astype(bf16)
+        grads_ref[:, grouped : grouped + LANES] = jnp.where(lane < 2 * heads, grad_small, 0.0).astype(bf16)
     lanes_out[0:1, :] = jnp.sum(jnp.where(is_gate, carry * gates_all, 0.0), 0, keepdims=True)
     lanes_out[1:2, :] = jnp.sum(grad_small, 0, keepdims=True)
     grads = grads_ref[...]
-    outer(x_ref, grads, sum_ref)
-    out_copies = spill(chunks, starts_ref, sum_ref, sems.at[0])
+    outer(x_ref, grads, sum_ref, 0)
+    if group == 0:
+        for i, half_ref in enumerate(taken):
+            outer(grad_rows_ref, half_ref[...], sum_ref, width + i * value_width)
+    out_copies = spill(chunks, starts_ref, sum_ref, out_sems.at[0])
     wait_all(copies)
-    hidden_out[...] = hidden_ref[...] + dot1(grads, weight_ref[...], "nt")
+    hidden = dot1(grads, weight_ref[...], "nt")
+    hidden_out[...] = taken[1][...] + hidden if group > 0 else hidden
     wait_all(out_copies)
 
 
-def ffn_kernel(
-    count, starts_ref, x_ref, cot_ref, *refs
-):
-    gate_pieces = refs[:count]
+def ffn_kernel(count, starts_ref, x_ref, cot_ref, *refs):
+    pieces = refs[:count]
     down_pieces = refs[count : 2 * count]
-    inner_ref, grads_ref, hidden_ref, weight_ref, down_ref, sems = refs[2 * count :]
+    inner_ref, grads_ref, hidden_ref, weight_ref, sems = refs[2 * count :]
     hidden = inner_ref.shape[1]
-    copies = fetch(gate_pieces, starts_ref, weight_ref, sems.at[0], slice(0, 2 * hidden))
-    down_copies = fetch(down_pieces, starts_ref, down_ref, sems.at[1], slice(0, hidden))
+    copies = fetch(pieces, starts_ref, weight_ref, sems.at[0:1], [(0, 0, 2 * hidden)])
+    down_cols = [(0, 2 * hidden, hidden)]
+    down_copies = fetch(down_pieces, starts_ref, weight_ref, sems.at[1:2], down_cols)
     wait_all(copies)
     rows = x_ref[...]
     gate_pre = dot1(rows, weight_ref[:, :hidden])
-    up_pre = dot1(rows, weight_ref[:, hidden:])
+    up_pre = dot1(rows, weight_ref[:, hidden : 2 * hidden])
     sigma = jax.nn.sigmoid(gate_pre)
     gate_act = gate_pre * sigma
     inner_ref[...] = (gate_act * up_pre).astype(bf16)
     wait_all(down_copies)
-    grad_inner = dot1(cot_ref[...], down_ref[...])
+    grad_inner = dot1(cot_ref[...], weight_ref[:, 2 * hidden :])
     grads_ref[:, :hidden] = (grad_inner * up_pre * silu_slope(gate_pre, sigma)).astype(bf16)
     grads_ref[:, hidden:] = (grad_inner * gate_act).astype(bf16)
-    hidden_ref[...] = dot1(grads_ref[...], weight_ref[...], "nt")
-
-
-def outer_kernel(count, starts_ref, left_ref, right_ref, *refs):
-    chunks = refs[:count]
-    sum_ref, sems = refs[count:]
-    outer(left_ref, right_ref[...], sum_ref)
+    hidden_ref[...] = dot1(grads_ref[...], weight_ref[:, : 2 * hidden], "nt")
+
+
+def outer_kernel(count, starts_ref, *refs):
+    pairs = (len(refs) - count - 2) // 2
+    operands = refs[: 2 * pairs]
+    chunks = refs[2 * pairs : 2 * pairs + count]
+    sum_ref, sems = refs[2 * pairs + count :]
+    place = 0
+    for i in range(pairs):
+        right = operands[2 * i + 1][...]
+        outer(operands[2 * i], right, sum_ref, place)
+        place = place + right.shape[1]
     wait_all(spill(chunks, starts_ref, sum_ref, sems))
 
 
-def branch_kernel(count, starts_ref, left_ref, *refs):
-    pieces = refs[:count]
-    out_ref, weight_ref, sems = refs[count:]
-    copies = fetch(pieces, starts_ref, weight_ref, sems, slice(0, left_ref.shape[1]))
-    wait_all(copies)
-    out_ref[...] = dot1(left_ref[...], weight_ref[...], "nt")
+def branch_kernel(count, first, starts_ref, *refs):
+    lefts = refs[: len(refs) - count - 3]
+    pieces = refs[len(lefts) : len(lefts) + count]
+    out_ref, weight_ref, sems = refs[len(lefts) + count :]
+    width = weight_ref.shape[1]
+    wait_all(fetch(pieces, starts_ref, weight_ref, sems, [(first, 0, width)]))
+    total = None
+    place = 0
+    for left_ref in lefts:
+        cols = slice(place, place + left_ref.shape[1])
+        part = dot1(left_ref[...], weight_ref[:, cols], "nt")
+        total = part if total is None else total + part
+        place = place + left_ref.shape[1]
+    out_ref[...] = total
 
 
 VMEM_SPEC = pl.BlockSpec(memory_space=pltpu.VMEM)
@@ -505,89 +542,86 @@
         [
             pltpu.VMEM((model, width), bf16),
             pltpu.VMEM((model, LANES), bf16),
-            pltpu.SemaphoreType.DMA((2, count)),
+            pltpu.SemaphoreType.DMA((5, count)),
         ],
     )
 
 
 def mixer_backward(
-    starts, pieces, out_pieces, rows, grad_rows, proj, small, lanes, convs, gain, saved,
-    carry, hidden, heads, group, per_step, last,
+    starts, pieces, rows, grad_rows, proj, small, lanes, convs, gain, saved,
+    taken, heads, group, per_step, last,
 ):
     length, model = rows.shape
     taps = convs[0].shape[0]
     key_dim = convs[0].shape[1] // per_step
     value_dim = convs[2].shape[1] // per_step
     width = proj.shape[1] + (LANES if last else 0)
+    extra = sum(half.shape[1] for half in taken) if group == 0 else 0
     count = len(pieces)
     results = call(
         functools.partial(
-            backward_kernel, heads, group, per_step, key_dim, value_dim, last, count,
-            len(out_pieces),
+            backward_kernel, heads, group, per_step, key_dim, value_dim, last, count
         ),
         starts,
-        (rows, grad_rows, proj, small, lanes, *convs, gain, *saved, carry, hidden),
-        list(pieces) + list(out_pieces),
+        (rows, grad_rows, proj, small, lanes, *convs, gain, *saved, *taken),
+        pieces,
         [
             shape((taps, per_step * key_dim), f32),
             shape((taps, per_step * key_dim), f32),
             shape((taps, per_step * value_dim), f32),
             shape((1, value_dim), f32),
-            shape(carry.shape, f32),
+            shape((length, LANES), f32),
             shape((2, LANES), f32),
-            shape(hidden.shape, f32),
+            shape((length, model), f32),
         ],
-        [shape((piece.shape[0], width), bf16) for piece in pieces],
+        [shape((piece.shape[0], width + extra), bf16) for piece in pieces],
         [
             pltpu.VMEM((model, width), bf16),
             pltpu.VMEM((model, per_step * value_dim), bf16),
             pltpu.VMEM((length, width), bf16),
-            pltpu.VMEM((model, width), bf16),
-            pltpu.SemaphoreType.DMA((2, count)),
+            pltpu.VMEM((model, width + extra), bf16),
+            pltpu.SemaphoreType.DMA((5, count)),
+            pltpu.SemaphoreType.DMA((1, count)),
         ],
     )
     return results[:count], results[count : count + 3], results[count + 3 :]
 
 
-def ffn_pass(starts, gate_pieces, down_pieces, rows, cotangent):
+def ffn_pass(starts, pieces, down_pieces, rows, cotangent):
     length, model = rows.shape
     hidden = down_pieces[0].shape[1]
-    count = len(gate_pieces)
+    count = len(pieces)
     return call(
         functools.partial(ffn_kernel, count), starts, (rows, cotangent),
-        list(gate_pieces) + list(down_pieces),
+        list(pieces) + list(down_pieces),
         [
             shape((length, hidden), bf16),
             shape((length, 2 * hidden), bf16),
             shape((length, model), f32),
         ],
         [],
-        [
-            pltpu.VMEM((model, 2 * hidden), bf16),
-            pltpu.VMEM((model, hidden), bf16),
-            pltpu.SemaphoreType.DMA((2, count)),
-        ],
-    )
-
-
-def outer_chunks(starts, like, left, right):
+        [pltpu.VMEM((model, 3 * hidden), bf16), pltpu.SemaphoreType.DMA((2, count))],
+    )
+
+
+def outer_chunks(starts, like, *operands):
     count = len(like)
-    width = right.shape[1]
+    width = sum(right.shape[1] for right in operands[1::2])
     return call(
-        functools.partial(outer_kernel, count), starts, (left, right), [],
+        functools.partial(outer_kernel, count), starts, operands, [],
         [], [shape((piece.shape[0], width), bf16) for piece in like],
-        [pltpu.VMEM((left.shape[1], width), bf16), pltpu.SemaphoreType.DMA((count,))],
-    )
-
-
-def branch_rows(starts, pieces, left):
+        [pltpu.VMEM((operands[0].shape[1], width), bf16), pltpu.SemaphoreType.DMA((count,))],
+    )
+
+
+def branch_rows(starts, pieces, first, *lefts):
     count = len(pieces)
-    model = left.shape[0]
     model = sum(piece.shape[0] for piece in pieces)
+    width = sum(left.shape[1] for left in lefts)
     return call(
-        functools.partial(branch_kernel, count), starts, (left,), pieces,
-        [shape((left.shape[0], model), f32)], [],
-        [pltpu.VMEM((model, left.shape[1]), bf16), pltpu.SemaphoreType.DMA((count,))],
+        functools.partial(branch_kernel, count, first), starts, lefts, pieces,
+        [shape((lefts[0].shape[0], model), f32)], [],
+        [pltpu.VMEM((model, width), bf16), pltpu.SemaphoreType.DMA((1, count))],
     )[0]
 
 
@@ -657,13 +691,10 @@
     def partner(self, array):
         return lax.ppermute(array, self.axis, self.pairs)
 
-    def total(self, array, marks):
+    def total(self, array):
         size = 1
-        marks = list(marks)
         while size < 2 * self.chips:
             flips = [(i, i ^ size) for i in range(2 * self.chips)]
-            if marks:
-                array = after(array, marks.pop(0))
             array = array + lax.ppermute(array, self.axis, flips)
             size = 2 * size
         return array
@@ -790,6 +821,15 @@
 
 def after(array, *done):
     return lax.optimization_barrier((array, *done))[0] if done else array
+
+
+def split_columns(array, widths):
+    pieces = []
+    offset = 0
+    for width in widths:
+        pieces.append(array[:, offset : offset + width])
+        offset = offset + width
+    return pieces
 
 
 def on_device(
@@ -821,9 +861,9 @@
     starts = ring.starts(query_weight.shape[0])
     proj_weights = (query_weight, key_weight, value_weight, out_gate_weight)
     narrow = jnp.concatenate([beta_weight, decay_weight], 1)
-    parts = [group_of(weight, group) for group in range(groups) for weight in proj_weights]
-    parts.append(jnp.pad(narrow, ((0, 0), (0, LANES - 2 * heads))))
-    proj_joined = jnp.concatenate(parts, 1)
+    blank = jnp.zeros((narrow.shape[0], LANES - 2 * heads), bf16)
+    proj_joined = jnp.concatenate([*proj_weights, narrow, blank, out_weight], 1)
+    out_at = proj_joined.shape[1] - value_cols
     ffn_joined = jnp.concatenate([ffn_gate_weight, ffn_up_weight], 1)
     normed1, inverse1, hidden1 = rms_rows(tokens, norm_gain1)
     whole1 = gather_rows(hidden1, "tensor")
@@ -839,17 +879,12 @@
     ]
 
     proj_gather = Gather(ring, proj_joined)
-    proj_gather.advance().advance()
-    out_gather = Gather(ring, out_weight, proj_gather.piece)
-    proj_gather.advance()
-    out_gather.advance()
+    proj_gather.advance().advance().advance()
     late = proj_gather.piece
+    down_pieces = Gather(ring, ffn_down_weight).finish()
     proj_pieces = proj_gather.finish()
-    out_pieces = out_gather.finish()
     ffn_gather = Gather(ring, ffn_joined, late)
-    down_gather = Gather(ring, ffn_down_weight, late)
     ffn_pieces = ffn_gather.finish()
-    down_pieces = down_gather.finish()
     projections = []
     halves = []
     saved = []
@@ -860,8 +895,8 @@
         projections.append(proj)
         halves.append(half)
         saved.append(kept)
-    mixed_half = jnp.concatenate(halves, 1)
-    branch = scatter_rows(branch_rows(starts, out_pieces, mixed_half), "tensor")
+    partial_branch = branch_rows(starts, proj_pieces, out_at, *halves)
+    branch = scatter_rows(partial_branch, "tensor")
     residual = tokens.astype(f32) + branch
     normed2, inverse2, hidden2 = rms_rows(residual, norm_gain2)
     whole2 = gather_rows(hidden2, "tensor")
@@ -870,42 +905,35 @@
         starts, ffn_pieces, down_pieces, whole2, grad_whole
     )
     grad_hidden2 = scatter_rows(partial_hidden2, "tensor")
-    ffn_chunks = outer_chunks(starts, ffn_pieces, whole2, grad_pre_both)
-    down_chunks = outer_chunks(starts, ffn_pieces, grad_whole, inner_act)
-    ffn_scatter = Scatter(ring, ffn_chunks)
-    down_scatter = Scatter(ring, down_chunks)
+    ffn_chunks = outer_chunks(
+        starts, ffn_pieces, whole2, grad_pre_both, grad_whole, inner_act
+    )
+    ffn_shard = Scatter(ring, ffn_chunks).finish()
     grad_normed2, second_gain_gradient = rms_back(grad_hidden2, normed2, inverse2, norm_gain2)
     grad_residual = local_mask * out_cotangent.astype(f32) + grad_normed2
     grad_whole1 = gather_rows(grad_residual.astype(bf16), "tensor")
-    ffn_branch = scatter_rows(
-        branch_rows(starts, down_pieces, after(inner_act, grad_residual)), "tensor"
-    )
-    output = (local_mask * (residual + ffn_branch)).astype(bf16)
-    down_shard = down_scatter.finish()
-    ffn_shard = ffn_scatter.finish()
-    out_chunks = outer_chunks(starts, out_pieces, grad_whole1, mixed_half)
-    out_shard = Scatter(ring, out_chunks).finish()
-    carry = jnp.zeros((whole1.shape[0], LANES), f32)
-    partial_hidden = jnp.zeros(whole1.shape, f32)
+    taken = halves
     conv_grads = []
     gain_sum = 0.0
     scatters = []
     for group in range(groups):
         chunks, conv_grad, (gain_part, carry, lane_sums, partial_hidden) = mixer_backward(
-            starts, proj_pieces, out_pieces, whole1, grad_whole1, projections[group], small,
-            lanes, convs[group], gain_wide, saved[group], carry, partial_hidden, heads, group,
-            per_step, group == groups - 1,
-        )
+            starts, proj_pieces, whole1, grad_whole1, projections[group], small,
+            lanes, convs[group], gain_wide, saved[group], taken, heads, group, per_step,
+            group == groups - 1,
+        )
+        taken = (carry, partial_hidden)
         conv_grads.append(conv_grad)
         gain_sum = gain_sum + gain_part
         scatters.append(Scatter(ring, chunks))
     grad_hidden1 = scatter_rows(partial_hidden, "tensor")
+    partial_ffn = branch_rows(
+        starts, down_pieces, 0, after(inner_act, partial_hidden)
+    )
+    ffn_branch = scatter_rows(partial_ffn, "tensor")
+    output = (local_mask * (residual + ffn_branch)).astype(bf16)
     grad_normed1, first_gain_gradient = rms_back(grad_hidden1, normed1, inverse1, norm_gain1)
     grad_tokens = (grad_residual + grad_normed1).astype(bf16)
-    marks = []
-    while scatters[-1].step > 0:
-        scatters[-1].advance()
-        marks.append(scatters[-1].arrived)
     proj_shards = [scatter.finish() for scatter in scatters]
     edges = [0, wide_key, 2 * wide_key, 2 * wide_key + wide_value, grouped]
     mixer_grads = [
@@ -914,12 +942,15 @@
     ]
     mixer_grads.append(proj_shards[-1][:, grouped : grouped + heads])
     mixer_grads.append(proj_shards[-1][:, grouped + heads : grouped + 2 * heads])
-    ffn_grads = [ffn_shard[:, :hidden_cols], ffn_shard[:, hidden_cols:]]
+    ffn_grads = split_columns(ffn_shard, [hidden_cols] * 3)
     grad_conv_query, grad_conv_key, grad_conv_value = [
         jnp.concatenate([conv_grad[i] for conv_grad in conv_grads], 1) for i in range(3)
     ]
 
     taps = conv_query.shape[0]
+    grad_conv_query, grad_conv_key, grad_conv_value, gain_sum, lane_sums = lax.optimization_barrier(
+        (grad_conv_query, grad_conv_key, grad_conv_value, gain_sum, lane_sums, grad_hidden1)
+    )[:5]
     blocks = [
         jnp.concatenate([grad_conv_query, grad_conv_key], 1),
         grad_conv_value,
@@ -932,7 +963,7 @@
     tall = sum(block.shape[0] for block in blocks)
     blocks = [jnp.pad(block, ((0, 0), (0, wide - block.shape[1]))) for block in blocks]
     blocks.append(jnp.zeros((-tall % 8, wide), f32))
-    packed = ring.total(jnp.concatenate(blocks, 0), marks)
+    packed = ring.total(jnp.concatenate(blocks, 0))
     pieces = [packed] + others_of(packed, "tensor")
     summed = pieces[0]
     for member in pieces[1:]:
@@ -959,11 +990,11 @@
         joined(gain_row + 3, 1, heads, heads)[0],
         joined(gain_row + 4, 1, heads, heads)[0],
         summed[gain_row + 2, : out_gain.shape[0]],
-        out_shard,
+        proj_shards[0][:, -value_cols:],
         summed[gain_row + 1, : norm_gain2.shape[0]],
         ffn_grads[0],
         ffn_grads[1],
-        down_shard,
+        ffn_grads[2],
     )
 
 

time: 379 us -> 351 us (0.926)
  the two profiles are of different devices: /device:TPU:7 before, /device:TPU:8 now
where the time goes in v3:
time: 351 us; the launch traced here: 346 us
  waiting for transfers between devices  149 us (42%)
  Pallas kernels  78.5 us (22%)
  starting transfers between devices  58.8 us (17%)
  other arithmetic  35 us (10%)
  local copies, waits for them, and re-layouts  21.3 us (6%)
    ppermute x24, waiting for transfers between devices, onward(): return lax.ppermute(array, self.axis, self.moves)  109 us
    pallas_call x8, Pallas kernels, call(): pl.pallas_call(kernel, in_specs=[SMEM_SPEC] + [VMEM_SPEC] * len(inside) +...  78.5 us
    ppermute x24, starting transfers between devices, onward(): return lax.ppermute(array, self.axis, self.moves)  40.3 us
    ppermute x4, waiting for transfers between devices, scatter_rows(): total = total + lax.ppermute(part, axis, moves).astype(f32)  22 us
    ppermute x4, waiting for transfers between devices, total(): array = array + lax.ppermute(array, self.axis, flips)  9.62 us
    select_n x7, other arithmetic, by_index(): joined = here if joined is None else jnp.where(index == value, here, joined)  7.93 us
    convert_element_type x12, other arithmetic, advance(): self.arrived = ring.onward(after(moving.astype(bf16), *deps))  7.92 us
    unnamed x138, local copies, waits for them, and re-layouts  7.81 us
  transfers between devices with their start and end apart: 67, of which 27 were waited for; matrix products, arithmetic and copies ran while one was open for 12% of the time, Pallas kernels for 20%

profile of v3, /device:TPU:8, one launch (start us, length us, event | category | flops | bytes accessed | tf_op | source)
XLA Modules:
  0.0 345.6 jit_solution(18397435944133062595)
XLA Ops:
  3.5 1.9 collective-permute-done.1
  5.6 1.6 collective-permute-start.2
  7.2 13.6 %collective-permute-done.2.refs_1_.refs_3_ = bf16[128,4224]{1,0:T(8,128)(2,1)S(1)} collective-permute-done((bf16[128,4224]{1,0:T(8,128)(2,1)S(1)}, bf16[128,4224]{1,0:T(8,128)(2,1)S(1)}, u32[]{:S(2)}, u32[]{:S(2)}) %collective-permute-start.2) | collective-permute-done | bytes 1081376 | tf_op jit(solution)/shard_map/ppermute | solution.py:689
  20.8 1.6 collective-permute-start.3
  22.4 13.7 %collective-permute-done.3.refs_2_.refs_4_ = bf16[128,4224]{1,0:T(8,128)(2,1)} collective-permute-done((bf16[128,4224]{1,0:T(8,128)(2,1)S(1)}, bf16[128,4224]{1,0:T(8,128)(2,1)}, u32[]{:S(2)}, u32[]{:S(2)}) %collective-permute-start.3) | collective-permute-done | bytes 1081376 | tf_op jit(solution)/shard_map/ppermute | solution.py:689
  36.1 1.6 collective-permute-start.4
  37.7 1.8 pad_maximum_fusion
  40.4 1.6 collective-permute-start.23
  42.0 9.5 %collective-permute-done.4.refs_3_.refs_5_ = bf16[128,4224]{1,0:T(8,128)(2,1)S(1)} collective-permute-done((bf16[128,4224]{1,0:T(8,128)(2,1)}, bf16[128,4224]{1,0:T(8,128)(2,1)S(1)}, u32[]{:S(2)}, u32[]{:S(2)}) %collective-permute-start.4) | collective-permute-done | bytes 1081376 | tf_op jit(solution)/shard_map/ppermute | solution.py:689
  52.5 1.5 collective-permute-start
  55.4 1.6 collective-permute-start.24
  57.0 2.3 maximum_select_fusion.1.refs_0_
  59.3 1.6 collective-permute-start.14
  61.7 1.5 collective-permute-start.8
  65.7 5.2 %collective-permute-done.14.refs_1_ = bf16[128,2816]{1,0:T(8,128)(2,1)} collective-permute-done((bf16[128,2816]{1,0:T(8,128)(2,1)}, bf16[128,2816]{1,0:T(8,128)(2,1)}, u32[]{:S(2)}, u32[]{:S(2)}) %collective-permute-start.14) | collective-permute-done | bytes 720928 | tf_op jit(solution)/shard_map/ppermute | solution.py:689
  70.9 1.6 collective-permute-start.15
  73.2 3.5 %collective-permute-done.8.refs_7_.refs_9_ = bf16[64,4224]{1,0:T(8,128)(2,1)} collective-permute-done((bf16[64,4224]{1,0:T(8,128)(2,1)}, bf16[64,4224]{1,0:T(8,128)(2,1)}, u32[]{:S(2)}, u32[]{:S(2)}) %collective-permute-start.8) | collective-permute-done | bytes 540704 | tf_op jit(solution)/shard_map/ppermute | solution.py:689
  77.9 1.7 collective-permute-start.25
  79.7 2.2 maximum_select_fusion.2.x_ref
  82.9 10.0 %shard_map.356 = (f32[256,1536]{1,0:T(8,128)}, f32[256,128]{1,0:T(8,128)}, bf16[256,512]{1,0:T(8,128)(2,1)}, f32[256,512]{1,0:T(8,128)}, f32[256,512]{1,0:T(8,128)}, /*index=5*/f32[2,2,128,128]{3,2,1,0:T(8,128)}) custom-call(s32[9]{0:T(128)} %stack.48.starts_ref, bf16[256,1024]{1,0:T(8,128)(2,1)} %maximum_select_fusion.2.x_ref, ...), custom_call_target="tpu_custom_call" | custom-call | tf_op jit(solution)/shard_map/pallas_call | solution.py:510
  92.9 10.0 %shard_map.357 = (f32[256,1536]{1,0:T(8,128)}, f32[256,128]{1,0:T(8,128)}, bf16[256,512]{1,0:T(8,128)(2,1)}, f32[256,512]{1,0:T(8,128)}, f32[256,512]{1,0:T(8,128)}, /*index=5*/f32[2,2,128,128]{3,2,1,0:T(8,128)}) custom-call(s32[9]{0:T(128)} %stack.48.starts_ref, bf16[256,1024]{1,0:T(8,128)(2,1)} %maximum_select_fusion.2.x_ref, ...), custom_call_target="tpu_custom_call" | custom-call | tf_op jit(solution)/shard_map/pallas_call | solution.py:510
  102.9 4.4 %shard_map.358 = f32[256,1024]{1,0:T(8,128)} custom-call(s32[9]{0:T(128)} %stack.48.starts_ref, bf16[256,512]{1,0:T(8,128)(2,1)} %get-tuple-element.80.refs_0_, bf16[256,512]{1,0:T(8,128)(2,1)} %get-tuple-element.81.refs_1_, bf16[128,4224]{1,0:T(8,128)(2,1)} %copy-done, bf16[128,4224]{1,0:T(8,128)(2,1)} %copy-done.2, ...), custom_call_target="tpu_custom_call" | custom-call | tf_op jit(solution)/shard_map/pallas_call | solution.py:510
  108.5 1.6 collective-permute-start.10
  110.0 1.5 collective-permute-start.16
  112.8 5.0 %collective-permute-done.10 = bf16[128,1024]{1,0:T(8,128)(2,1)} collective-permute-done((bf16[128,1024]{1,0:T(8,128)(2,1)S(1)}, bf16[128,1024]{1,0:T(8,128)(2,1)}, u32[]{:S(2)}, u32[]{:S(2)}) %collective-permute-start.10) | collective-permute-done | bytes 262176 | tf_op jit(solution)/shard_map/ppermute | solution.py:818
  117.8 1.5 collective-permute-start.29
  122.2 1.9 collective-permute-start.20
  125.8 4.3 %collective-permute-done.20.refs_7_ = bf16[64,2816]{1,0:T(8,128)(2,1)S(1)} collective-permute-done((bf16[64,2816]{1,0:T(8,128)(2,1)S(1)}, bf16[64,2816]{1,0:T(8,128)(2,1)S(1)}, u32[]{:S(2)}, u32[]{:S(2)}) %collective-permute-start.20) | collective-permute-done | bytes 360480 | tf_op jit(solution)/shard_map/ppermute | solution.py:689
  130.1 3.0 collective-permute-done.11
  133.1 2.0 maximum_select_fusion.4.cot_ref.refs_2_
  138.9 9.5 %shard_map.359 = (bf16[256,1408]{1,0:T(8,128)(2,1)}, bf16[256,2816]{1,0:T(8,128)(2,1)}, f32[256,1024]{1,0:T(8,128)}) custom-call(s32[9]{0:T(128)} %stack.48.starts_ref, bf16[256,1024]{1,0:T(8,128)(2,1)} %maximum_select_fusion.3.x_ref.refs_0_, bf16[256,1024]{1,0:T(8,128)(2,1)} %maximum_select_fusion.4.cot_ref.refs_2_, ...), custom_call_target="tpu_custom_call" | custom-call | tf_op jit(solution)/shard_map/pallas_call | solution.py:510
  151.1 7.3 %collective-permute-done.31 = bf16[128,1024]{1,0:T(8,128)(2,1)S(1)} collective-permute-done((bf16[128,1024]{1,0:T(8,128)(2,1)S(1)}, bf16[128,1024]{1,0:T(8,128)(2,1)S(1)}, u32[]{:S(2)}, u32[]{:S(2)}) %collective-permute-start.31) | collective-permute-done | bytes 262176 | tf_op jit(solution)/shard_map/ppermute | solution.py:818
  161.4 7.8 %shard_map.363 = (bf16[128,4224]{1,0:T(8,128)(2,1)}, bf16[128,4224]{1,0:T(8,128)(2,1)}, bf16[128,4224]{1,0:T(8,128)(2,1)}, bf16[128,4224]{1,0:T(8,128)(2,1)}, bf...) custom-call(s32[9]{0:T(128)} %stack.48.starts_ref, ...), custom_call_target="tpu_custom_call" | custom-call | tf_op jit(solution)/shard_map/pallas_call | solution.py:510
  170.8 16.0 %shard_map.360 = (bf16[128,2560]{1,0:T(8,128)(2,1)}, bf16[128,2560]{1,0:T(8,128)(2,1)}, bf16[128,2560]{1,0:T(8,128)(2,1)}, bf16[128,2560]{1,0:T(8,128)(2,1)}, bf...) custom-call(s32[9]{0:T(128)} %stack.48.starts_ref, ...), custom_call_target="tpu_custom_call" | custom-call | tf_op jit(solution)/shard_map/pallas_call | solution.py:510
  186.8 15.5 %shard_map.361 = (bf16[128,1664]{1,0:T(8,128)(2,1)}, bf16[128,1664]{1,0:T(8,128)(2,1)}, bf16[128,1664]{1,0:T(8,128)(2,1)}, bf16[128,1664]{1,0:T(8,128)(2,1)}, bf...) custom-call(s32[9]{0:T(128)} %stack.48.starts_ref, ...), custom_call_target="tpu_custom_call" | custom-call | tf_op jit(solution)/shard_map/pallas_call | solution.py:510
  202.5 5.3 %shard_map.362 = f32[256,1024]{1,0:T(8,128)} custom-call(s32[9]{0:T(128)} %stack.48.starts_ref, bf16[256,1408]{1,0:T(8,128)(2,1)} %get-tuple-element.97.refs_0_.refs_3_, bf16[128,1408]{1,0:T(8,128)(2,1)} %maximum_select_fusion.6.refs_9_.refs_1_, bf16[128,1408]{1,0:T(8,128)(2,1)} %collective-permute-done.23.refs_10_.refs_2_, ...), custom_call_target="tpu_custom_call" | custom-call | tf_op jit(solution)/shard_map/pallas_call | solution.py:510
  207.8 1.9 dynamic-slice_convert_fusion.3
  212.1 1.5 collective-permute-done.52
  214.5 9.6 %collective-permute-done.34 = bf16[128,1024]{1,0:T(8,128)(2,1)S(1)} collective-permute-done((bf16[128,1024]{1,0:T(8,128)(2,1)S(1)}, bf16[128,1024]{1,0:T(8,128)(2,1)S(1)}, u32[]{:S(2)}, u32[]{:S(2)}) %collective-permute-start.34) | collective-permute-done | bytes 262176 | tf_op jit(solution)/shard_map/ppermute | solution.py:818
  226.9 1.6 fusion.9
  230.5 1.7 multiply_convert_fusion
  233.5 1.6 collective-permute-start.53
  236.7 2.7 collective-permute-done.53
  241.0 1.8 collective-permute-start.38
  243.0 7.7 %collective-permute-done.38 = f32[16,1024]{1,0:T(8,128)S(1)} collective-permute-done((f32[16,1024]{1,0:T(8,128)S(1)}, f32[16,1024]{1,0:T(8,128)S(1)}, u32[]{:S(2)}, u32[]{:S(2)}) %collective-permute-start.38) | collective-permute-done | bytes 65568 | tf_op jit(solution)/shard_map/ppermute | solution.py:698
  250.8 1.7 collective-permute-start.44
  253.3 1.7 add_convert_fusion.2
  255.0 1.9 collective-permute-done.39
  256.9 2.3 collective-permute-start.54
  261.3 3.8 %collective-permute-done.54 = bf16[128,1664]{1,0:T(8,128)(2,1)S(1)} collective-permute-done((bf16[128,1664]{1,0:T(8,128)(2,1)S(1)}, bf16[128,1664]{1,0:T(8,128)(2,1)S(1)}, u32[]{:S(2)}, u32[]{:S(2)}) %collective-permute-start.54) | collective-permute-done | bytes 426016 | tf_op jit(solution)/shard_map/ppermute | solution.py:689
  265.2 2.3 collective-permute-start.55
  270.0 3.4 collective-permute-done.55
  273.4 2.3 collective-permute-start.63
  276.0 4.5 %collective-permute-done.45 = bf16[128,2560]{1,0:T(8,128)(2,1)S(1)} collective-permute-done((bf16[128,2560]{1,0:T(8,128)(2,1)S(1)}, bf16[128,2560]{1,0:T(8,128)(2,1)S(1)}, u32[]{:S(2)}, u32[]{:S(2)}) %collective-permute-start.45) | collective-permute-done | bytes 655392 | tf_op jit(solution)/shard_map/ppermute | solution.py:689
  280.4 2.3 collective-permute-start.56
  283.3 8.7 %collective-permute-done.63 = bf16[128,4224]{1,0:T(8,128)(2,1)S(1)} collective-permute-done((bf16[128,4224]{1,0:T(8,128)(2,1)S(1)}, bf16[128,4224]{1,0:T(8,128)(2,1)S(1)}, u32[]{:S(2)}, u32[]{:S(2)}) %collective-permute-start.63) | collective-permute-done | bytes 1081376 | tf_op jit(solution)/shard_map/ppermute | solution.py:689
  292.0 1.7 add_convert_fusion.1
  293.7 2.3 collective-permute-start.64
  296.8 6.8 %collective-permute-done.46 = bf16[128,2560]{1,0:T(8,128)(2,1)S(1)} collective-permute-done((bf16[128,2560]{1,0:T(8,128)(2,1)S(1)}, bf16[128,2560]{1,0:T(8,128)(2,1)S(1)}, u32[]{:S(2)}, u32[]{:S(2)}) %collective-permute-start.46) | collective-permute-done | bytes 655392 | tf_op jit(solution)/shard_map/ppermute | solution.py:689
  303.9 2.3 collective-permute-start.47
  306.3 15.9 %collective-permute-done.47 = bf16[128,2560]{1,0:T(8,128)(2,1)S(1)} collective-permute-done((bf16[128,2560]{1,0:T(8,128)(2,1)S(1)}, bf16[128,2560]{1,0:T(8,128)(2,1)S(1)}, u32[]{:S(2)}, u32[]{:S(2)}) %collective-permute-start.47) | collective-permute-done | bytes 655392 | tf_op jit(solution)/shard_map/ppermute | solution.py:689
  324.8 2.3 collective-permute-start.65
  329.6 10.7 %collective-permute-done.65 = bf16[128,4224]{1,0:T(8,128)(2,1)} collective-permute-done((bf16[128,4224]{1,0:T(8,128)(2,1)}, bf16[128,4224]{1,0:T(8,128)(2,1)}, u32[]{:S(2)}, u32[]{:S(2)}) %collective-permute-start.65) | collective-permute-done | bytes 1081376 | tf_op jit(solution)/shard_map/ppermute | solution.py:689
  340.3 1.4 convert_add_fusion
  (311 shorter events, 58.1 us)
Async XLA Ops:
  3.4 2.0 collective-permute-start.1
  5.6 15.2 %collective-permute-start.2 = (bf16[128,4224]{1,0:T(8,128)(2,1)S(1)}, bf16[128,4224]{1,0:T(8,128)(2,1)S(1)}, u32[]{:S(2)}, u32[]{:S(2)}) collective-permute-start(bf16[128,4224]{1,0:T(8,128)(2,1)S(1)} %maximum_select_fusion.refs_0_.refs_2_), channel_id=1, source_target_pairs={{0,8},{8,16},{16,24},{24,28},{28,20},{20,12},{12,4},{4,0},{10,2},{... | collective-permute-start | bytes 3244040 | tf_op jit(solution)/shard_map/ppermute | solution.py:689
  20.8 15.3 %collective-permute-start.3 = (bf16[128,4224]{1,0:T(8,128)(2,1)S(1)}, bf16[128,4224]{1,0:T(8,128)(2,1)}, u32[]{:S(2)}, u32[]{:S(2)}) collective-permute-start(bf16[128,4224]{1,0:T(8,128)(2,1)S(1)} %collective-permute-done.2.refs_1_.refs_3_), channel_id=1, source_target_pairs={{0,8},{8,16},{16,24},{24,28},{28,20},{20,12},{12,4},{4,0},{10,2},{... | collective-permute-start | bytes 3244040 | tf_op jit(solution)/shard_map/ppermute | solution.py:689
  36.1 15.4 %collective-permute-start.4 = (bf16[128,4224]{1,0:T(8,128)(2,1)}, bf16[128,4224]{1,0:T(8,128)(2,1)S(1)}, u32[]{:S(2)}, u32[]{:S(2)}) collective-permute-start(bf16[128,4224]{1,0:T(8,128)(2,1)} %collective-permute-done.3.refs_2_.refs_4_), channel_id=1, source_target_pairs={{0,8},{8,16},{16,24},{24,28},{28,20},{20,12},{12,4},{4,0},{10,2},{... | collective-permute-start | bytes 3244040 | tf_op jit(solution)/shard_map/ppermute | solution.py:689
  40.4 15.0 %collective-permute-start.23 = (bf16[128,1408]{1,0:T(8,128)(2,1)}, bf16[128,1408]{1,0:T(8,128)(2,1)}, u32[]{:S(2)}, u32[]{:S(2)}) collective-permute-start(bf16[128,1408]{1,0:T(8,128)(2,1)} %maximum_select_fusion.6.refs_9_.refs_1_), channel_id=1, source_target_pairs={{0,8},{8,16},{16,24},{24,28},{28,20},{20,12},{12,4},{4,0},{10,2},{... | collective-permute-start | bytes 1081352 | tf_op jit(solution)/shard_map/ppermute | solution.py:689
  51.4 5.5 %collective-permute-start.13 = (bf16[64,2816]{1,0:T(8,128)(2,1)}, bf16[64,2816]{1,0:T(8,128)(2,1)}, u32[]{:S(2)}, u32[]{:S(2)}) collective-permute-start(bf16[64,2816]{1,0:T(8,128)(2,1)} %pad_maximum_fusion), channel_id=1, source_target_pairs={{0,2},{2,0},{4,6},{6,4},{8,10},{10,8},{12,14},{14,12},{16,18},{18,... | collective-permute-start | bytes 1081352 | tf_op jit(solution)/shard_map/ppermute | solution.py:692
  52.5 10.8 %collective-permute-start = (bf16[128,1024]{1,0:T(8,128)(2,1)}, bf16[128,1024]{1,0:T(8,128)(2,1)}, u32[]{:S(2)}, u32[]{:S(2)}) collective-permute-start(bf16[128,1024]{1,0:T(8,128)(2,1)} %fusion.4), channel_id=1, source_target_pairs={{0,1},{1,0},{2,3},{3,2},{4,5},{5,4},{6,7},{7,6},{8,9},{9,8},{10,11... | collective-permute-start | bytes 786440 | tf_op jit(solution)/shard_map/ppermute | solution.py:791
  55.4 7.9 %collective-permute-start.24 = (bf16[128,1408]{1,0:T(8,128)(2,1)}, bf16[128,1408]{1,0:T(8,128)(2,1)}, u32[]{:S(2)}, u32[]{:S(2)}) collective-permute-start(bf16[128,1408]{1,0:T(8,128)(2,1)} %collective-permute-done.23.refs_10_.refs_2_), channel_id=1, source_target_pairs={{0,8},{8,16},{16,24},{24,28},{28,20},{20,12},{12,4},{4,0},{10,2},{... | collective-permute-start | bytes 1081352 | tf_op jit(solution)/shard_map/ppermute | solution.py:689
  57.0 21.0 %collective-permute-start.5 = (bf16[128,4224]{1,0:T(8,128)(2,1)S(1)}, bf16[128,4224]{1,0:T(8,128)(2,1)}, u32[]{:S(2)}, u32[]{:S(2)}) collective-permute-start(bf16[128,4224]{1,0:T(8,128)(2,1)S(1)} %collective-permute-done.2.refs_1_.refs_3_), channel_id=1, source_target_pairs={{0,2},{2,0},{4,6},{6,4},{8,10},{10,8},{12,14},{14,12},{16,18},{18,... | collective-permute-start | bytes 3244040 | tf_op jit(solution)/shard_map/ppermute | solution.py:692
  59.3 11.6 %collective-permute-start.14 = (bf16[128,2816]{1,0:T(8,128)(2,1)}, bf16[128,2816]{1,0:T(8,128)(2,1)}, u32[]{:S(2)}, u32[]{:S(2)}) collective-permute-start(bf16[128,2816]{1,0:T(8,128)(2,1)} %maximum_select_fusion.1.refs_0_), channel_id=1, source_target_pairs={{0,8},{8,16},{16,24},{24,28},{28,20},{20,12},{12,4},{4,0},{10,2},{... | collective-permute-start | bytes 2162696 | tf_op jit(solution)/shard_map/ppermute | solution.py:689
  61.7 15.0 %collective-permute-start.8 = (bf16[64,4224]{1,0:T(8,128)(2,1)}, bf16[64,4224]{1,0:T(8,128)(2,1)}, u32[]{:S(2)}, u32[]{:S(2)}) collective-permute-start(bf16[64,4224]{1,0:T(8,128)(2,1)} %constant_dynamic-slice_fusion.2), channel_id=1, source_target_pairs={{0,8},{8,16},{16,24},{24,28},{28,20},{20,12},{12,4},{4,0},{10,2},{... | collective-permute-start | bytes 1622024 | tf_op jit(solution)/shard_map/ppermute | solution.py:689
  63.3 18.6 %collective-permute-start.6 = (bf16[128,4224]{1,0:T(8,128)(2,1)}, bf16[128,4224]{1,0:T(8,128)(2,1)S(1)}, u32[]{:S(2)}, u32[]{:S(2)}) collective-permute-start(bf16[128,4224]{1,0:T(8,128)(2,1)} %collective-permute-done.3.refs_2_.refs_4_), channel_id=1, source_target_pairs={{0,2},{2,0},{4,6},{6,4},{8,10},{10,8},{12,14},{14,12},{16,18},{18,... | collective-permute-start | bytes 3244040 | tf_op jit(solution)/shard_map/ppermute | solution.py:692
  63.3 18.6 %collective-permute-start.7 = (bf16[128,4224]{1,0:T(8,128)(2,1)S(1)}, bf16[128,4224]{1,0:T(8,128)(2,1)}, u32[]{:S(2)}, u32[]{:S(2)}) collective-permute-start(bf16[128,4224]{1,0:T(8,128)(2,1)S(1)} %collective-permute-done.4.refs_3_.refs_5_), channel_id=1, source_target_pairs={{0,2},{2,0},{4,6},{6,4},{8,10},{10,8},{12,14},{14,12},{16,18},{18,... | collective-permute-start | bytes 3244040 | tf_op jit(solution)/shard_map/ppermute | solution.py:692
  70.9 39.1 %collective-permute-start.15 = (bf16[128,2816]{1,0:T(8,128)(2,1)}, bf16[128,2816]{1,0:T(8,128)(2,1)}, u32[]{:S(2)}, u32[]{:S(2)}) collective-permute-start(bf16[128,2816]{1,0:T(8,128)(2,1)} %collective-permute-done.14.refs_1_), channel_id=1, source_target_pairs={{0,8},{8,16},{16,24},{24,28},{28,20},{20,12},{12,4},{4,0},{10,2},{... | collective-permute-start | bytes 2162696 | tf_op jit(solution)/shard_map/ppermute | solution.py:689
  76.7 5.2 %collective-permute-start.9 = (bf16[64,4224]{1,0:T(8,128)(2,1)}, bf16[64,4224]{1,0:T(8,128)(2,1)}, u32[]{:S(2)}, u32[]{:S(2)}) collective-permute-start(bf16[64,4224]{1,0:T(8,128)(2,1)} %collective-permute-done.8.refs_7_.refs_9_), channel_id=1, source_target_pairs={{0,2},{2,0},{4,6},{6,4},{8,10},{10,8},{12,14},{14,12},{16,18},{18,... | collective-permute-start | bytes 1622024 | tf_op jit(solution)/shard_map/ppermute | solution.py:692
  77.9 34.3 %collective-permute-start.25 = (bf16[128,1408]{1,0:T(8,128)(2,1)}, bf16[128,1408]{1,0:T(8,128)(2,1)S(1)}, u32[]{:S(2)}, u32[]{:S(2)}) collective-permute-start(bf16[128,1408]{1,0:T(8,128)(2,1)} %collective-permute-done.24.refs_11_.refs_3_), channel_id=1, source_target_pairs={{0,8},{8,16},{16,24},{24,28},{28,20},{20,12},{12,4},{4,0},{10,2},{... | collective-permute-start | bytes 1081352 | tf_op jit(solution)/shard_map/ppermute | solution.py:689
  108.5 9.4 %collective-permute-start.10 = (bf16[128,1024]{1,0:T(8,128)(2,1)S(1)}, bf16[128,1024]{1,0:T(8,128)(2,1)}, u32[]{:S(2)}, u32[]{:S(2)}) collective-permute-start(bf16[128,1024]{1,0:T(8,128)(2,1)S(1)} %dynamic-slice_convert_fusion.5), channel_id=1, source_target_pairs={{0,1},{1,0},{2,3},{3,2},{4,5},{5,4},{6,7},{7,6},{8,9},{9,8},{10,11... | collective-permute-start | bytes 786440 | tf_op jit(solution)/shard_map/ppermute | solution.py:818
  110.0 11.5 %collective-permute-start.16 = (bf16[128,2816]{1,0:T(8,128)(2,1)}, bf16[128,2816]{1,0:T(8,128)(2,1)S(1)}, u32[]{:S(2)}, u32[]{:S(2)}) collective-permute-start(bf16[128,2816]{1,0:T(8,128)(2,1)} %collective-permute-done.15.refs_2_), channel_id=1, source_target_pairs={{0,8},{8,16},{16,24},{24,28},{28,20},{20,12},{12,4},{4,0},{10,2},{... | collective-permute-start | bytes 2162696 | tf_op jit(solution)/shard_map/ppermute | solution.py:689
  111.7 9.9 %collective-permute-start.12 = (bf16[128,1024]{1,0:T(8,128)(2,1)S(1)}, bf16[128,1024]{1,0:T(8,128)(2,1)}, u32[]{:S(2)}, u32[]{:S(2)}) collective-permute-start(bf16[128,1024]{1,0:T(8,128)(2,1)S(1)} %fusion.12), channel_id=1, source_target_pairs={{0,1},{1,0},{2,3},{3,2},{4,5},{5,4},{6,7},{7,6},{8,9},{9,8},{10,11... | collective-permute-start | bytes 786440 | tf_op jit(solution)/shard_map/ppermute | solution.py:791
  112.3 9.9 %collective-permute-start.26 = (bf16[128,1408]{1,0:T(8,128)(2,1)}, bf16[128,1408]{1,0:T(8,128)(2,1)S(1)}, u32[]{:S(2)}, u32[]{:S(2)}) collective-permute-start(bf16[128,1408]{1,0:T(8,128)(2,1)} %collective-permute-done.23.refs_10_.refs_2_), channel_id=1, source_target_pairs={{0,2},{2,0},{4,6},{6,4},{8,10},{10,8},{12,14},{14,12},{16,18},{18,... | collective-permute-start | bytes 1081352 | tf_op jit(solution)/shard_map/ppermute | solution.py:692
  112.3 10.0 %collective-permute-start.27 = (bf16[128,1408]{1,0:T(8,128)(2,1)}, bf16[128,1408]{1,0:T(8,128)(2,1)S(1)}, u32[]{:S(2)}, u32[]{:S(2)}) collective-permute-start(bf16[128,1408]{1,0:T(8,128)(2,1)} %collective-permute-done.24.refs_11_.refs_3_), channel_id=1, source_target_pairs={{0,2},{2,0},{4,6},{6,4},{8,10},{10,8},{12,14},{14,12},{16,18},{18,... | collective-permute-start | bytes 1081352 | tf_op jit(solution)/shard_map/ppermute | solution.py:692
  117.8 6.3 %collective-permute-start.29 = (bf16[64,1408]{1,0:T(8,128)(2,1)S(1)}, bf16[64,1408]{1,0:T(8,128)(2,1)S(1)}, u32[]{:S(2)}, u32[]{:S(2)}) collective-permute-start(bf16[64,1408]{1,0:T(8,128)(2,1)S(1)} %constant_dynamic-slice_fusion), channel_id=1, source_target_pairs={{0,8},{8,16},{16,24},{24,28},{28,20},{20,12},{12,4},{4,0},{10,2},{... | collective-permute-start | bytes 540680 | tf_op jit(solution)/shard_map/ppermute | solution.py:689
  121.5 2.8 collective-permute-start.28
  121.6 14.5 %collective-permute-start.17 = (bf16[128,2816]{1,0:T(8,128)(2,1)}, bf16[128,2816]{1,0:T(8,128)(2,1)S(1)}, u32[]{:S(2)}, u32[]{:S(2)}) collective-permute-start(bf16[128,2816]{1,0:T(8,128)(2,1)} %collective-permute-done.14.refs_1_), channel_id=1, source_target_pairs={{0,2},{2,0},{4,6},{6,4},{8,10},{10,8},{12,14},{14,12},{16,18},{18,... | collective-permute-start | bytes 2162696 | tf_op jit(solution)/shard_map/ppermute | solution.py:692
  122.1 13.9 %collective-permute-start.18 = (bf16[128,2816]{1,0:T(8,128)(2,1)}, bf16[128,2816]{1,0:T(8,128)(2,1)S(1)}, u32[]{:S(2)}, u32[]{:S(2)}) collective-permute-start(bf16[128,2816]{1,0:T(8,128)(2,1)} %collective-permute-done.15.refs_2_), channel_id=1, source_target_pairs={{0,2},{2,0},{4,6},{6,4},{8,10},{10,8},{12,14},{14,12},{16,18},{18,... | collective-permute-start | bytes 2162696 | tf_op jit(solution)/shard_map/ppermute | solution.py:692
  122.2 7.8 %collective-permute-start.20 = (bf16[64,2816]{1,0:T(8,128)(2,1)S(1)}, bf16[64,2816]{1,0:T(8,128)(2,1)S(1)}, u32[]{:S(2)}, u32[]{:S(2)}) collective-permute-start(bf16[64,2816]{1,0:T(8,128)(2,1)S(1)} %constant_dynamic-slice_fusion.1), channel_id=1, source_target_pairs={{0,8},{8,16},{16,24},{24,28},{28,20},{20,12},{12,4},{4,0},{10,2},{... | collective-permute-start | bytes 1081352 | tf_op jit(solution)/shard_map/ppermute | solution.py:689
  124.2 11.9 %collective-permute-start.19 = (bf16[128,2816]{1,0:T(8,128)(2,1)S(1)}, bf16[128,2816]{1,0:T(8,128)(2,1)S(1)}, u32[]{:S(2)}, u32[]{:S(2)}) collective-permute-start(bf16[128,2816]{1,0:T(8,128)(2,1)S(1)} %collective-permute-done.16.refs_3_), channel_id=1, source_target_pairs={{0,2},{2,0},{4,6},{6,4},{8,10},{10,8},{12,14},{14,12},{16,18},{18,... | collective-permute-start | bytes 2162696 | tf_op jit(solution)/shard_map/ppermute | solution.py:692
  124.3 8.8 %collective-permute-start.11 = (bf16[128,1024]{1,0:T(8,128)(2,1)S(1)}, bf16[128,1024]{1,0:T(8,128)(2,1)S(1)}, u32[]{:S(2)}, u32[]{:S(2)}) collective-permute-start(bf16[128,1024]{1,0:T(8,128)(2,1)S(1)} %multiply_convert_fusion.1), channel_id=1, source_target_pairs={{0,1},{1,0},{2,3},{3,2},{4,5},{5,4},{6,7},{7,6},{8,9},{9,8},{10,11... | collective-permute-start | bytes 786440 | tf_op jit(solution)/shard_map/ppermute | solution.py:791
  130.1 8.1 %collective-permute-start.21 = (bf16[64,2816]{1,0:T(8,128)(2,1)S(1)}, bf16[64,2816]{1,0:T(8,128)(2,1)S(1)}, u32[]{:S(2)}, u32[]{:S(2)}) collective-permute-start(bf16[64,2816]{1,0:T(8,128)(2,1)S(1)} %collective-permute-done.20.refs_7_), channel_id=1, source_target_pairs={{0,2},{2,0},{4,6},{6,4},{8,10},{10,8},{12,14},{14,12},{16,18},{18,... | collective-permute-start | bytes 1081352 | tf_op jit(solution)/shard_map/ppermute | solution.py:692
  133.1 2.9 collective-permute-start.30
  149.6 8.8 %collective-permute-start.31 = (bf16[128,1024]{1,0:T(8,128)(2,1)S(1)}, bf16[128,1024]{1,0:T(8,128)(2,1)S(1)}, u32[]{:S(2)}, u32[]{:S(2)}) collective-permute-start(bf16[128,1024]{1,0:T(8,128)(2,1)S(1)} %dynamic-slice_convert_fusion.4), channel_id=1, source_target_pairs={{0,1},{1,0},{2,3},{3,2},{4,5},{5,4},{6,7},{7,6},{8,9},{9,8},{10,11... | collective-permute-start | bytes 786440 | tf_op jit(solution)/shard_map/ppermute | solution.py:818
  160.0 9.9 %collective-permute-start.32 = (bf16[128,1024]{1,0:T(8,128)(2,1)S(1)}, bf16[128,1024]{1,0:T(8,128)(2,1)S(1)}, u32[]{:S(2)}, u32[]{:S(2)}) collective-permute-start(bf16[128,1024]{1,0:T(8,128)(2,1)S(1)} %get-tuple-element.165), channel_id=1, source_target_pairs={{0,1},{1,0},{2,3},{3,2},{4,5},{5,4},{6,7},{7,6},{8,9},{9,8},{10,11... | collective-permute-start | bytes 786440 | tf_op jit(solution)/shard_map/ppermute | solution.py:791
  169.2 42.6 %collective-permute-start.61 = (bf16[64,4224]{1,0:T(8,128)(2,1)}, bf16[64,4224]{1,0:T(8,128)(2,1)S(1)}, u32[]{:S(2)}, u32[]{:S(2)}) collective-permute-start(bf16[64,4224]{1,0:T(8,128)(2,1)} %get-tuple-element.139), channel_id=1, source_target_pairs={{0,2},{2,0},{4,6},{6,4},{8,10},{10,8},{12,14},{14,12},{16,18},{18,... | collective-permute-start | bytes 1622024 | tf_op jit(solution)/shard_map/ppermute | solution.py:692
  169.3 83.3 %collective-permute-start.60 = (bf16[128,4224]{1,0:T(8,128)(2,1)}, bf16[128,4224]{1,0:T(8,128)(2,1)}, u32[]{:S(2)}, u32[]{:S(2)}) collective-permute-start(bf16[128,4224]{1,0:T(8,128)(2,1)} %get-tuple-element.137), channel_id=1, source_target_pairs={{0,2},{2,0},{4,6},{6,4},{8,10},{10,8},{12,14},{14,12},{16,18},{18,... | collective-permute-start | bytes 3244040 | tf_op jit(solution)/shard_map/ppermute | solution.py:692
  169.8 113.1 %collective-permute-start.59 = (bf16[128,4224]{1,0:T(8,128)(2,1)}, bf16[128,4224]{1,0:T(8,128)(2,1)}, u32[]{:S(2)}, u32[]{:S(2)}) collective-permute-start(bf16[128,4224]{1,0:T(8,128)(2,1)} %get-tuple-element.135), channel_id=1, source_target_pairs={{0,2},{2,0},{4,6},{6,4},{8,10},{10,8},{12,14},{14,12},{16,18},{18,... | collective-permute-start | bytes 3244040 | tf_op jit(solution)/shard_map/ppermute | solution.py:692
  209.6 19.5 %collective-permute-start.33 = (bf16[128,1024]{1,0:T(8,128)(2,1)}, bf16[128,1024]{1,0:T(8,128)(2,1)}, u32[]{:S(2)}, u32[]{:S(2)}) collective-permute-start(bf16[128,1024]{1,0:T(8,128)(2,1)} %dynamic-slice_convert_fusion.3), channel_id=1, source_target_pairs={{0,1},{1,0},{2,3},{3,2},{4,5},{5,4},{6,7},{7,6},{8,9},{9,8},{10,11... | collective-permute-start | bytes 786440 | tf_op jit(solution)/shard_map/ppermute | solution.py:818
  210.3 13.8 %collective-permute-start.34 = (bf16[128,1024]{1,0:T(8,128)(2,1)S(1)}, bf16[128,1024]{1,0:T(8,128)(2,1)S(1)}, u32[]{:S(2)}, u32[]{:S(2)}) collective-permute-start(bf16[128,1024]{1,0:T(8,128)(2,1)S(1)} %dynamic-slice_convert_fusion.2), channel_id=1, source_target_pairs={{0,1},{1,0},{2,3},{3,2},{4,5},{5,4},{6,7},{7,6},{8,9},{9,8},{10,11... | collective-permute-start | bytes 786440 | tf_op jit(solution)/shard_map/ppermute | solution.py:818
  213.6 21.5 %collective-permute-start.43 = (bf16[64,2560]{1,0:T(8,128)(2,1)}, bf16[64,2560]{1,0:T(8,128)(2,1)}, u32[]{:S(2)}, u32[]{:S(2)}) collective-permute-start(bf16[64,2560]{1,0:T(8,128)(2,1)} %get-tuple-element.120), channel_id=1, source_target_pairs={{0,2},{2,0},{4,6},{6,4},{8,10},{10,8},{12,14},{14,12},{16,18},{18,... | collective-permute-start | bytes 983048 | tf_op jit(solution)/shard_map/ppermute | solution.py:692
  228.6 12.5 %collective-permute-start.51 = (bf16[128,1664]{1,0:T(8,128)(2,1)S(1)}, bf16[128,1664]{1,0:T(8,128)(2,1)S(1)}, u32[]{:S(2)}, u32[]{:S(2)}) collective-permute-start(bf16[128,1664]{1,0:T(8,128)(2,1)S(1)} %copy-done.66), channel_id=1, source_target_pairs={{0,2},{2,0},{4,6},{6,4},{8,10},{10,8},{12,14},{14,12},{16,18},{18,... | collective-permute-start | bytes 1277960 | tf_op jit(solution)/shard_map/ppermute | solution.py:692
  229.1 4.3 %collective-permute-start.36 = (f32[16,1024]{1,0:T(8,128)S(1)}, f32[16,1024]{1,0:T(8,128)S(1)}, u32[]{:S(2)}, u32[]{:S(2)}) collective-permute-start(f32[16,1024]{1,0:T(8,128)S(1)} %add.335), channel_id=1, source_target_pairs={{0,4},{2,6},{4,0},{6,2},{8,12},{10,14},{12,8},{14,10},{16,20},{18,... | collective-permute-start | bytes 196616 | tf_op jit(solution)/shard_map/ppermute | solution.py:698
  233.5 5.8 %collective-permute-start.53 = (bf16[64,1664]{1,0:T(8,128)(2,1)S(1)}, bf16[64,1664]{1,0:T(8,128)(2,1)S(1)}, u32[]{:S(2)}, u32[]{:S(2)}) collective-permute-start(bf16[64,1664]{1,0:T(8,128)(2,1)S(1)} %copy-done.38), channel_id=1, source_target_pairs={{0,8},{8,16},{16,24},{24,28},{28,20},{20,12},{12,4},{4,0},{10,2},{... | collective-permute-start | bytes 638984 | tf_op jit(solution)/shard_map/ppermute | solution.py:689
  235.1 4.9 %collective-permute-start.37 = (f32[16,1024]{1,0:T(8,128)S(1)}, f32[16,1024]{1,0:T(8,128)S(1)}, u32[]{:S(2)}, u32[]{:S(2)}) collective-permute-start(f32[16,1024]{1,0:T(8,128)S(1)} %add.336), channel_id=1, source_target_pairs={{0,8},{2,10},{4,12},{6,14},{8,0},{10,2},{12,4},{14,6},{16,24},{18,... | collective-permute-start | bytes 196616 | tf_op jit(solution)/shard_map/ppermute | solution.py:698
  239.3 21.3 %collective-permute-start.50 = (bf16[128,1664]{1,0:T(8,128)(2,1)S(1)}, bf16[128,1664]{1,0:T(8,128)(2,1)S(1)}, u32[]{:S(2)}, u32[]{:S(2)}) collective-permute-start(bf16[128,1664]{1,0:T(8,128)(2,1)S(1)} %copy-done.65), channel_id=1, source_target_pairs={{0,2},{2,0},{4,6},{6,4},{8,10},{10,8},{12,14},{14,12},{16,18},{18,... | collective-permute-start | bytes 1277960 | tf_op jit(solution)/shard_map/ppermute | solution.py:692
  240.0 10.8 %collective-permute-start.62 = (bf16[64,4224]{1,0:T(8,128)(2,1)S(1)}, bf16[64,4224]{1,0:T(8,128)(2,1)S(1)}, u32[]{:S(2)}, u32[]{:S(2)}) collective-permute-start(bf16[64,4224]{1,0:T(8,128)(2,1)S(1)} %add_convert_fusion.6), channel_id=1, source_target_pairs={{0,8},{8,16},{16,24},{24,28},{28,20},{20,12},{12,4},{4,0},{10,2},{... | collective-permute-start | bytes 1622024 | tf_op jit(solution)/shard_map/ppermute | solution.py:689
  241.0 9.7 %collective-permute-start.38 = (f32[16,1024]{1,0:T(8,128)S(1)}, f32[16,1024]{1,0:T(8,128)S(1)}, u32[]{:S(2)}, u32[]{:S(2)}) collective-permute-start(f32[16,1024]{1,0:T(8,128)S(1)} %add.337), channel_id=1, source_target_pairs={{0,16},{2,18},{4,20},{6,22},{8,24},{10,26},{12,28},{14,30},{16,0},... | collective-permute-start | bytes 196616 | tf_op jit(solution)/shard_map/ppermute | solution.py:698
  250.7 16.9 %collective-permute-start.42 = (bf16[128,2560]{1,0:T(8,128)(2,1)S(1)}, bf16[128,2560]{1,0:T(8,128)(2,1)S(1)}, u32[]{:S(2)}, u32[]{:S(2)}) collective-permute-start(bf16[128,2560]{1,0:T(8,128)(2,1)S(1)} %copy-done.63), channel_id=1, source_target_pairs={{0,2},{2,0},{4,6},{6,4},{8,10},{10,8},{12,14},{14,12},{16,18},{18,... | collective-permute-start | bytes 1966088 | tf_op jit(solution)/shard_map/ppermute | solution.py:692
  250.8 9.7 %collective-permute-start.44 = (bf16[64,2560]{1,0:T(8,128)(2,1)S(1)}, bf16[64,2560]{1,0:T(8,128)(2,1)S(1)}, u32[]{:S(2)}, u32[]{:S(2)}) collective-permute-start(bf16[64,2560]{1,0:T(8,128)(2,1)S(1)} %add_convert_fusion.10), channel_id=1, source_target_pairs={{0,8},{8,16},{16,24},{24,28},{28,20},{20,12},{12,4},{4,0},{10,2},{... | collective-permute-start | bytes 983048 | tf_op jit(solution)/shard_map/ppermute | solution.py:689
  252.6 4.3 %collective-permute-start.39 = (f32[16,1024]{1,0:T(8,128)S(1)}, f32[16,1024]{1,0:T(8,128)S(1)}, u32[]{:S(2)}, u32[]{:S(2)}) collective-permute-start(f32[16,1024]{1,0:T(8,128)S(1)} %add.338), channel_id=1, source_target_pairs={{0,1},{1,0},{2,3},{3,2},{4,5},{5,4},{6,7},{7,6},{8,9},{9,8},{10,11... | collective-permute-start | bytes 196616 | tf_op jit(solution)/shard_map/ppermute | solution.py:791
  256.9 8.1 %collective-permute-start.54 = (bf16[128,1664]{1,0:T(8,128)(2,1)S(1)}, bf16[128,1664]{1,0:T(8,128)(2,1)S(1)}, u32[]{:S(2)}, u32[]{:S(2)}) collective-permute-start(bf16[128,1664]{1,0:T(8,128)(2,1)S(1)} %add_convert_fusion.9), channel_id=1, source_target_pairs={{0,8},{8,16},{16,24},{24,28},{28,20},{20,12},{12,4},{4,0},{10,2},{... | collective-permute-start | bytes 1277960 | tf_op jit(solution)/shard_map/ppermute | solution.py:689
  260.5 9.4 %collective-permute-start.49 = (bf16[128,1664]{1,0:T(8,128)(2,1)S(1)}, bf16[128,1664]{1,0:T(8,128)(2,1)S(1)}, u32[]{:S(2)}, u32[]{:S(2)}) collective-permute-start(bf16[128,1664]{1,0:T(8,128)(2,1)S(1)} %copy-done.64), channel_id=1, source_target_pairs={{0,2},{2,0},{4,6},{6,4},{8,10},{10,8},{12,14},{14,12},{16,18},{18,... | collective-permute-start | bytes 1277960 | tf_op jit(solution)/shard_map/ppermute | solution.py:692
  260.7 15.2 %collective-permute-start.41 = (bf16[128,2560]{1,0:T(8,128)(2,1)S(1)}, bf16[128,2560]{1,0:T(8,128)(2,1)S(1)}, u32[]{:S(2)}, u32[]{:S(2)}) collective-permute-start(bf16[128,2560]{1,0:T(8,128)(2,1)S(1)} %copy-done.62), channel_id=1, source_target_pairs={{0,2},{2,0},{4,6},{6,4},{8,10},{10,8},{12,14},{14,12},{16,18},{18,... | collective-permute-start | bytes 1966088 | tf_op jit(solution)/shard_map/ppermute | solution.py:692
  265.2 8.2 %collective-permute-start.55 = (bf16[128,1664]{1,0:T(8,128)(2,1)S(1)}, bf16[128,1664]{1,0:T(8,128)(2,1)S(1)}, u32[]{:S(2)}, u32[]{:S(2)}) collective-permute-start(bf16[128,1664]{1,0:T(8,128)(2,1)S(1)} %add_convert_fusion.8), channel_id=1, source_target_pairs={{0,8},{8,16},{16,24},{24,28},{28,20},{20,12},{12,4},{4,0},{10,2},{... | collective-permute-start | bytes 1277960 | tf_op jit(solution)/shard_map/ppermute | solution.py:689
  267.9 12.6 %collective-permute-start.45 = (bf16[128,2560]{1,0:T(8,128)(2,1)S(1)}, bf16[128,2560]{1,0:T(8,128)(2,1)S(1)}, u32[]{:S(2)}, u32[]{:S(2)}) collective-permute-start(bf16[128,2560]{1,0:T(8,128)(2,1)S(1)} %add_convert_fusion.5), channel_id=1, source_target_pairs={{0,8},{8,16},{16,24},{24,28},{28,20},{20,12},{12,4},{4,0},{10,2},{... | collective-permute-start | bytes 1966088 | tf_op jit(solution)/shard_map/ppermute | solution.py:689
  269.9 52.6 %collective-permute-start.58 = (bf16[128,4224]{1,0:T(8,128)(2,1)S(1)}, bf16[128,4224]{1,0:T(8,128)(2,1)S(1)}, u32[]{:S(2)}, u32[]{:S(2)}) collective-permute-start(bf16[128,4224]{1,0:T(8,128)(2,1)S(1)} %copy-done.60), channel_id=1, source_target_pairs={{0,2},{2,0},{4,6},{6,4},{8,10},{10,8},{12,14},{14,12},{16,18},{18,... | collective-permute-start | bytes 3244040 | tf_op jit(solution)/shard_map/ppermute | solution.py:692
  273.4 18.6 %collective-permute-start.63 = (bf16[128,4224]{1,0:T(8,128)(2,1)S(1)}, bf16[128,4224]{1,0:T(8,128)(2,1)S(1)}, u32[]{:S(2)}, u32[]{:S(2)}) collective-permute-start(bf16[128,4224]{1,0:T(8,128)(2,1)S(1)} %add_convert_fusion.2), channel_id=1, source_target_pairs={{0,8},{8,16},{16,24},{24,28},{28,20},{20,12},{12,4},{4,0},{10,2},{... | collective-permute-start | bytes 3244040 | tf_op jit(solution)/shard_map/ppermute | solution.py:689
  275.9 20.9 %collective-permute-start.40 = (bf16[128,2560]{1,0:T(8,128)(2,1)S(1)}, bf16[128,2560]{1,0:T(8,128)(2,1)S(1)}, u32[]{:S(2)}, u32[]{:S(2)}) collective-permute-start(bf16[128,2560]{1,0:T(8,128)(2,1)S(1)} %copy-done.61), channel_id=1, source_target_pairs={{0,2},{2,0},{4,6},{6,4},{8,10},{10,8},{12,14},{14,12},{16,18},{18,... | collective-permute-start | bytes 1966088 | tf_op jit(solution)/shard_map/ppermute | solution.py:692
  280.4 16.1 %collective-permute-start.56 = (bf16[128,1664]{1,0:T(8,128)(2,1)S(1)}, bf16[128,1664]{1,0:T(8,128)(2,1)S(1)}, u32[]{:S(2)}, u32[]{:S(2)}) collective-permute-start(bf16[128,1664]{1,0:T(8,128)(2,1)S(1)} %add_convert_fusion.7), channel_id=1, source_target_pairs={{0,8},{8,16},{16,24},{24,28},{28,20},{20,12},{12,4},{4,0},{10,2},{... | collective-permute-start | bytes 1277960 | tf_op jit(solution)/shard_map/ppermute | solution.py:689
  283.0 20.6 %collective-permute-start.46 = (bf16[128,2560]{1,0:T(8,128)(2,1)S(1)}, bf16[128,2560]{1,0:T(8,128)(2,1)S(1)}, u32[]{:S(2)}, u32[]{:S(2)}) collective-permute-start(bf16[128,2560]{1,0:T(8,128)(2,1)S(1)} %add_convert_fusion.4), channel_id=1, source_target_pairs={{0,8},{8,16},{16,24},{24,28},{28,20},{20,12},{12,4},{4,0},{10,2},{... | collective-permute-start | bytes 1966088 | tf_op jit(solution)/shard_map/ppermute | solution.py:689
  293.7 28.8 %collective-permute-start.64 = (bf16[128,4224]{1,0:T(8,128)(2,1)S(1)}, bf16[128,4224]{1,0:T(8,128)(2,1)S(1)}, u32[]{:S(2)}, u32[]{:S(2)}) collective-permute-start(bf16[128,4224]{1,0:T(8,128)(2,1)S(1)} %add_convert_fusion.1), channel_id=1, source_target_pairs={{0,8},{8,16},{16,24},{24,28},{28,20},{20,12},{12,4},{4,0},{10,2},{... | collective-permute-start | bytes 3244040 | tf_op jit(solution)/shard_map/ppermute | solution.py:689
  296.7 9.5 %collective-permute-start.57 = (bf16[64,1664]{1,0:T(8,128)(2,1)S(1)}, bf16[64,1664]{1,0:T(8,128)(2,1)S(1)}, u32[]{:S(2)}, u32[]{:S(2)}) collective-permute-start(bf16[64,1664]{1,0:T(8,128)(2,1)S(1)} %dynamic-slice_convert_fusion.6), channel_id=1, source_target_pairs={{0,2},{2,0},{4,6},{6,4},{8,10},{10,8},{12,14},{14,12},{16,18},{18,... | collective-permute-start | bytes 638984 | tf_op jit(solution)/shard_map/ppermute | solution.py:692
  303.9 18.4 %collective-permute-start.47 = (bf16[128,2560]{1,0:T(8,128)(2,1)S(1)}, bf16[128,2560]{1,0:T(8,128)(2,1)S(1)}, u32[]{:S(2)}, u32[]{:S(2)}) collective-permute-start(bf16[128,2560]{1,0:T(8,128)(2,1)S(1)} %add_convert_fusion.3), channel_id=1, source_target_pairs={{0,8},{8,16},{16,24},{24,28},{28,20},{20,12},{12,4},{4,0},{10,2},{... | collective-permute-start | bytes 1966088 | tf_op jit(solution)/shard_map/ppermute | solution.py:689
  322.4 6.1 %collective-permute-start.48 = (bf16[64,2560]{1,0:T(8,128)(2,1)S(1)}, bf16[64,2560]{1,0:T(8,128)(2,1)}, u32[]{:S(2)}, u32[]{:S(2)}) collective-permute-start(bf16[64,2560]{1,0:T(8,128)(2,1)S(1)} %dynamic-slice_convert_fusion.1), channel_id=1, source_target_pairs={{0,2},{2,0},{4,6},{6,4},{8,10},{10,8},{12,14},{14,12},{16,18},{18,... | collective-permute-start | bytes 983048 | tf_op jit(solution)/shard_map/ppermute | solution.py:692
  324.8 15.5 %collective-permute-start.65 = (bf16[128,4224]{1,0:T(8,128)(2,1)}, bf16[128,4224]{1,0:T(8,128)(2,1)}, u32[]{:S(2)}, u32[]{:S(2)}) collective-permute-start(bf16[128,4224]{1,0:T(8,128)(2,1)} %add_convert_fusion), channel_id=1, source_target_pairs={{0,8},{8,16},{16,24},{24,28},{28,20},{20,12},{12,4},{4,0},{10,2},{... | collective-permute-start | bytes 3244040 | tf_op jit(solution)/shard_map/ppermute | solution.py:689
  341.8 2.4 collective-permute-start.66
  (70 other events, 848.8 us)
